TPU v7x, 1024 devices: a whole 4x8x16 slice. The times are simulated.
1024 devices in a mesh: dcn: 4 (over x), blk: 32 (over z, y_hi), head: 8 (over y_lo, core).
Axes of the slice: x: 4, y: 8 (y_hi: 2, y_lo: 4; y = y_hi * 4 + y_lo), z: 16, core: 2. Of those that a mesh axis runs over, the one named last changes fastest.
Arguments:
- queries: bfloat16 [65536, 16, 128], P(('dcn', 'blk'), 'head'), may hold values from -128 to 128
- keys: bfloat16 [65536, 128], P(('dcn', 'blk')), may hold values from -5 to 5
- values: bfloat16 [65536, 128], P(('dcn', 'blk')), may hold values from -6 to 6
- out_grad: bfloat16 [65536, 16, 128], P(('dcn', 'blk'), 'head'), may hold values from -6 to 6
- doc_start: int32 [65536], P(('dcn', 'blk')), may hold values from 0 to 65535, as said below
Outputs:
- q_grad: bfloat16 [65536, 16, 128], P(('dcn', 'blk'), 'head')
- k_grad: bfloat16 [65536, 128], P(('dcn', 'blk', 'head'))
- v_grad: bfloat16 [65536, 128], P(('dcn', 'blk', 'head'))
Inputs may be any that keep to these rules, and one draw needn't show every extreme that they name: doc_start is non-decreasing, doc_start[i] <= i, and doc_start[i] is i or doc_start[i - 1]; every document has at most 1024 tokens and some document has exactly 1024.
All inputs are finite; a program needn't handle non-finite values.
Results may differ from a plain program's by a relative error of at most 0.04.
Values may be sent and summed in bfloat16 or wider, within the bound.
A program may use at most 32 MiB of HBM per device.

v0:
```python
import jax
import jax.numpy as jnp
from jax import lax
from jax.sharding import PartitionSpec as P

WIN = 2


def from_behind(block, axis, distance):
    devices = range(lax.axis_size(axis))
    route = [(i - distance, i) for i in devices if i - distance in devices]
    return lax.ppermute(block, axis, route)


def local_grads(q, dout, starts, kwin, value_window, qpos, kpos):
    scale = q.shape[-1] ** (-0.5)
    visible = (kpos[None, :] >= starts[:, None]) & (kpos[None, :] <= qpos[:, None])
    scores = jnp.einsum("ihe,je->hij", q, kwin, preferred_element_type=jnp.float32) * scale
    top = jnp.max(jnp.where(visible[None], scores, -1e30), axis=-1, keepdims=True)
    expo = jnp.where(visible[None], jnp.exp(scores - top), 0.0)
    lse = top + jnp.log(jnp.sum(expo, axis=-1, keepdims=True))
    prob = jnp.where(visible[None], jnp.exp(scores - lse), 0.0)
    prob_low = prob.astype(jnp.bfloat16)
    attended_keys = jnp.einsum(
        "hij,je->ihe", prob_low, value_window, preferred_element_type=jnp.float32
    )
    delta = jnp.sum(dout.astype(jnp.float32) * attended_keys, axis=-1)
    dprob = jnp.einsum("ihe,je->hij", dout, value_window, preferred_element_type=jnp.float32)
    dscore = (prob * (dprob - jnp.transpose(delta)[:, :, None])).astype(jnp.bfloat16)
    dq = (
        jnp.einsum("hij,je->ihe", dscore, kwin, preferred_element_type=jnp.float32) * scale
    ).astype(jnp.bfloat16)
    dk = jnp.einsum("hij,ihe->je", dscore, q, preferred_element_type=jnp.float32) * scale
    dv = jnp.einsum("hij,ihe->je", prob_low, dout, preferred_element_type=jnp.float32)
    return (dq, jnp.concatenate([dk, dv], axis=1))


def body(queries, keys, values, out_grad, doc_start):
    rows = keys.shape[0]
    window_width = keys.shape[1]
    local_heads = queries.shape[1]
    position = lax.axis_index(("dcn", "blk"))
    packed = jnp.stack([keys, values])
    pieces = []
    for step in range(WIN, 0, -1):
        pieces.append(from_behind(packed, ("dcn", "blk"), step))
    pieces.append(packed)
    window = jnp.concatenate(pieces, axis=1)
    window_span = (WIN + 1) * rows
    first_position = position * rows
    qpos = first_position + jnp.arange(rows, dtype=jnp.int32)
    kpos = first_position - WIN * rows + jnp.arange(window_span, dtype=jnp.int32)
    grad_list = []
    terms = jnp.zeros((window_span, 2 * window_width), jnp.float32)
    for single in range(local_heads):
        head_dq, head_terms = local_grads(
            queries[:, single : single + 1],
            out_grad[:, single : single + 1],
            doc_start,
            window[0],
            window[1],
            qpos,
            kpos,
        )
        grad_list.append(head_dq)
        terms = terms + head_terms
    q_grad = jnp.concatenate(grad_list, axis=1)
    terms = terms.reshape(WIN + 1, rows, 2 * window_width)
    total = terms[WIN]
    for step in range(1, WIN + 1):
        total = total + from_behind(terms[WIN - step], ("dcn", "blk"), -step)
    reduced = lax.psum_scatter(total, "head", scatter_dimension=0, tiled=True)
    k_grad = reduced[:, :window_width].astype(jnp.bfloat16)
    v_grad = reduced[:, window_width:].astype(jnp.bfloat16)
    return (q_grad, k_grad, v_grad)


def solution(mesh):
    in_specs = (
        P(("dcn", "blk"), "head", None),
        P(("dcn", "blk"), None),
        P(("dcn", "blk"), None),
        P(("dcn", "blk"), "head", None),
        P(("dcn", "blk")),
    )
    out_specs = (
        P(("dcn", "blk"), "head", None),
        P(("dcn", "blk", "head"), None),
        P(("dcn", "blk", "head"), None),
    )
    return jax.shard_map(body, mesh=mesh, in_specs=in_specs, out_specs=out_specs, check_vma=False)
```

profile of v0, /device:TPU:1, one launch (start us, length us, event | category | flops | bytes accessed | tf_op | source)
XLA Modules:
  0.0 142.7 jit_solution(14521087305263076598)
XLA Ops:
  7.2 0.0 copy-start.1
  7.2 0.0 copy-start.2
  7.2 0.0 copy-start.3
  7.2 0.0 reduce-scatter.4.cloned.1.call-start
  7.2 1.1 pad_maximum_fusion
  8.3 8.3 %collective-permute-start.1 = (bf16[2,512,128]{2,1,0:T(8,128)(2,1)S(1)}, bf16[2,512,128]{2,1,0:T(8,128)(2,1)S(1)}, u32[]{:S(2)}, u32[]{:S(2)}) collective-permute-start(bf16[2,512,128]{2,1,0:T(8,128)(2,1)S(1)} %pad_maximum_fusion), channel_id=1, source_target_pairs={{0,8},{8,16},{16,24},{24,32},{32,40},{40,48},{48,56},{56,64},{64,7... | collective-permute-start | bytes 786440 | tf_op jit(solution)/shard_map/ppermute | solution.py:12
  16.6 4.0 %collective-permute-start = (bf16[2,512,128]{2,1,0:T(8,128)(2,1)S(1)}, bf16[2,512,128]{2,1,0:T(8,128)(2,1)S(1)}, u32[]{:S(2)}, u32[]{:S(2)}) collective-permute-start(bf16[2,512,128]{2,1,0:T(8,128)(2,1)S(1)} %pad_maximum_fusion), channel_id=1, source_target_pairs={{0,16},{8,24},{16,32},{24,40},{32,48},{40,56},{48,64},{56,72},{64,... | collective-permute-start | bytes 786440 | tf_op jit(solution)/shard_map/ppermute | solution.py:12
  20.6 1.5 %fusion.36 = (bf16[512,1,128]{2,1,0:T(2,128)(2,1)S(1)}, bf16[512,1,128]{2,1,0:T(2,128)(2,1)S(1)}) fusion(bf16[512,2,128]{2,1,0:T(2,128)(2,1)} %param.8), kind=kLoop, calls=%fused_computation.62 | loop fusion | bytes 524288 | tf_op jit(solution)/shard_map/slice | solution.py:58
  22.1 0.1 copy.30
  22.3 0.1 copy.32
  22.4 1.5 %fusion.37 = (bf16[512,1,128]{2,1,0:T(2,128)(2,1)S(1)}, bf16[512,1,128]{2,1,0:T(2,128)(2,1)S(1)}) fusion(bf16[512,2,128]{2,1,0:T(2,128)(2,1)} %param.5), kind=kLoop, calls=%fused_computation.63 | loop fusion | bytes 524288 | tf_op jit(solution)/shard_map/slice | solution.py:57
  23.9 0.0 collective-permute-done.1
  23.9 0.0 collective-permute-done
  23.9 0.0 copy-done.1
  23.9 0.0 copy-done.2
  24.0 0.1 maximum_maximum_fusion
  24.0 0.0 copy-start
  24.0 0.0 copy-done.3
  24.0 0.8 select_reduce_fusion.3
  24.9 1.3 select_reduce_fusion.2
  26.1 1.3 select_reduce_fusion
  27.4 1.0 fusion.21
  28.4 0.9 fusion.25
  29.4 1.0 fusion.20
  30.4 1.0 fusion.28
  31.3 1.3 fusion.10
  32.7 0.7 convolution_multiply_fusion.2
  33.4 0.0 copy-done
  33.4 1.3 fusion.11
  34.7 0.6 convolution_multiply_fusion.3
  35.4 0.2 maximum_add_fusion
  35.6 0.1 fusion.35
  35.7 1.3 collective-permute-start.2
  37.0 1.3 collective-permute-start.3
  38.3 13.7 %collective-permute-done.2 = f32[512,256]{0,1:T(8,128)S(1)} collective-permute-done((f32[512,256]{0,1:T(8,128)S(1)}, f32[512,256]{0,1:T(8,128)S(1)}, u32[]{:S(2)}, u32[]{:S(2)}) %collective-permute-start.2) | collective-permute-done | bytes 524320 | tf_op jit(solution)/shard_map/ppermute | solution.py:12
  51.9 15.6 %collective-permute-done.3 = f32[512,256]{0,1:T(8,128)S(1)} collective-permute-done((f32[512,256]{0,1:T(8,128)S(1)}, f32[512,256]{0,1:T(8,128)S(1)}, u32[]{:S(2)}, u32[]{:S(2)}) %collective-permute-start.3) | collective-permute-done | bytes 524320 | tf_op jit(solution)/shard_map/ppermute | solution.py:12
  67.6 1.0 fusion.24
  68.5 2.0 %copy.27 = f32[512,256]{1,0:T(8,128)} copy(f32[512,256]{0,1:T(8,128)} %fusion.24) | data formatting | bytes 1048576
  70.6 0.0 reduce-scatter.4.cloned.1.call-update
  70.6 1.4 fusion.22
  72.0 1.4 fusion.23
  73.4 0.9 copy.24
  74.3 59.2 %reduce-scatter.4.cloned.1.call-done = f32[64,256]{1,0:T(8,128)} async-done(((f32[512,256]{1,0:T(8,128)}), f32[64,256]{1,0:T(8,128)}) %reduce-scatter.4.cloned.1.call-update) | async-done | bytes 65552
  133.5 0.9 copy.28
  134.5 0.7 copy.26
  135.2 0.7 copy.25
  (5 shorter events, 0.1 us)
Async XLA Ops:
  7.2 16.8 %copy-start.1 = (bf16[512,128]{1,0:T(8,128)(2,1)S(1)}, bf16[512,128]{1,0:T(8,128)(2,1)}, u32[]{:S(2)}) copy-start(bf16[512,128]{1,0:T(8,128)(2,1)} %param.7) | copy-start | bytes 393220
  7.2 16.8 %copy-start.2 = (bf16[512,128]{1,0:T(8,128)(2,1)S(1)}, bf16[512,128]{1,0:T(8,128)(2,1)}, u32[]{:S(2)}) copy-start(bf16[512,128]{1,0:T(8,128)(2,1)} %param.6) | copy-start | bytes 393220
  7.2 16.8 %copy-start.3 = (s32[512]{0:T(512)S(1)}, s32[512]{0:T(512)}, u32[]{:S(2)}) copy-start(s32[512]{0:T(512)} %param.9) | copy-start | bytes 6148
  7.2 126.3 %reduce-scatter.4.cloned.1.call-start = ((), (), s32[]{:S(2)}) async-start(), calls=%async_computation.1 | async-start | bytes 589824
  8.3 15.6 %collective-permute-start.1 = (bf16[2,512,128]{2,1,0:T(8,128)(2,1)S(1)}, bf16[2,512,128]{2,1,0:T(8,128)(2,1)S(1)}, u32[]{:S(2)}, u32[]{:S(2)}) collective-permute-start(bf16[2,512,128]{2,1,0:T(8,128)(2,1)S(1)} %pad_maximum_fusion), channel_id=1, source_target_pairs={{0,8},{8,16},{16,24},{24,32},{32,40},{40,48},{48,56},{56,64},{64,7... | collective-permute-start | bytes 786440 | tf_op jit(solution)/shard_map/ppermute | solution.py:12
  16.6 7.3 %collective-permute-start = (bf16[2,512,128]{2,1,0:T(8,128)(2,1)S(1)}, bf16[2,512,128]{2,1,0:T(8,128)(2,1)S(1)}, u32[]{:S(2)}, u32[]{:S(2)}) collective-permute-start(bf16[2,512,128]{2,1,0:T(8,128)(2,1)S(1)} %pad_maximum_fusion), channel_id=1, source_target_pairs={{0,16},{8,24},{16,32},{24,40},{32,48},{40,56},{48,64},{56,72},{64,... | collective-permute-start | bytes 786440 | tf_op jit(solution)/shard_map/ppermute | solution.py:12
  24.0 9.3 %copy-start = (bf16[2,1536,128]{2,1,0:T(8,128)(2,1)}, bf16[2,1536,128]{2,1,0:T(8,128)(2,1)S(1)}, u32[]{:S(2)}) copy-start(bf16[2,1536,128]{2,1,0:T(8,128)(2,1)S(1)} %maximum_maximum_fusion) | copy-start | bytes 2359300
  35.7 16.3 %collective-permute-start.2 = (f32[512,256]{0,1:T(8,128)S(1)}, f32[512,256]{0,1:T(8,128)S(1)}, u32[]{:S(2)}, u32[]{:S(2)}) collective-permute-start(f32[512,256]{0,1:T(8,128)S(1)} %get-tuple-element.14), channel_id=1, source_target_pairs={{8,0},{16,8},{24,16},{32,24},{40,32},{48,40},{56,48},{64,56},{72,6... | collective-permute-start | bytes 1572872 | tf_op jit(solution)/shard_map/ppermute | solution.py:12
  37.0 30.6 %collective-permute-start.3 = (f32[512,256]{0,1:T(8,128)S(1)}, f32[512,256]{0,1:T(8,128)S(1)}, u32[]{:S(2)}, u32[]{:S(2)}) collective-permute-start(f32[512,256]{0,1:T(8,128)S(1)} %get-tuple-element.15), channel_id=1, source_target_pairs={{16,0},{24,8},{32,16},{40,24},{48,32},{56,40},{64,48},{72,56},{80,... | collective-permute-start | bytes 1572872 | tf_op jit(solution)/shard_map/ppermute | solution.py:12
Sparse Core Ops, SparseCore 0:
  70.7 62.7 reduce-scatter.3
where the time goes:
time: 143 us
  waiting for transfers between devices  88.5 us (62%)
  starting transfers between devices  14.9 us (10%)
  between operations  14.3 us (10%)
  matrix products  12.8 us (9%)
  local copies, waits for them, and re-layouts  8.6 us (6%)
  other arithmetic  3.61 us (3%)
    unnamed x2, waiting for transfers between devices  59.2 us
    ppermute x4, waiting for transfers between devices, from_behind(): return lax.ppermute(block, axis, route)  29.3 us
    ppermute x4, starting transfers between devices, from_behind(): return lax.ppermute(block, axis, route)  14.9 us
    unnamed x15, local copies, waits for them, and re-layouts  5.53 us
  transfers between devices with their start and end apart: 5, of which 3 were waited for; matrix products, arithmetic and copies ran while one was open for 5% of the time, Pallas kernels for 0%

commit v1 on v0

--- a/solution.py
+++ b/solution.py
@@ -65,13 +65,25 @@
         grad_list.append(head_dq)
         terms = terms + head_terms
     q_grad = jnp.concatenate(grad_list, axis=1)
-    terms = terms.reshape(WIN + 1, rows, 2 * window_width)
-    total = terms[WIN]
+    parts = lax.axis_size("head")
+    piece = rows // parts
+    head = lax.axis_index("head")
+    chunks = terms.reshape(WIN + 1, parts, piece, 2 * window_width)
+    stride = 1
+    while stride < parts:
+        bit = (head // stride) % 2
+        chunks = chunks.reshape(WIN + 1, -1, 2, piece, 2 * window_width)
+        keep = lax.dynamic_index_in_dim(chunks, bit, axis=2, keepdims=False)
+        send = lax.dynamic_index_in_dim(chunks, 1 - bit, axis=2, keepdims=False)
+        route = [(i, i ^ stride) for i in range(parts)]
+        chunks = keep + lax.ppermute(send, "head", route)
+        stride *= 2
+    reduced = chunks.reshape(WIN + 1, piece, 2 * window_width)
+    total = reduced[WIN]
     for step in range(1, WIN + 1):
-        total = total + from_behind(terms[WIN - step], ("dcn", "blk"), -step)
-    reduced = lax.psum_scatter(total, "head", scatter_dimension=0, tiled=True)
-    k_grad = reduced[:, :window_width].astype(jnp.bfloat16)
-    v_grad = reduced[:, window_width:].astype(jnp.bfloat16)
+        total = total + from_behind(reduced[WIN - step], ("dcn", "blk"), -step)
+    k_grad = total[:, :window_width].astype(jnp.bfloat16)
+    v_grad = total[:, window_width:].astype(jnp.bfloat16)
     return (q_grad, k_grad, v_grad)
 
 

time: 143 us -> 97.7 us (0.68)
  the two profiles are of different devices: /device:TPU:1 before, /device:TPU:6 now
where the time goes in v1:
time: 97.7 us; the launch traced here: 97.3 us
  waiting for transfers between devices  46.2 us (47%)
  starting transfers between devices  27.3 us (28%)
  matrix products  10.1 us (10%)
  local copies, waits for them, and re-layouts  6.8 us (7%)
  other arithmetic  5.83 us (6%)
  between operations  1.05 us (1%)
    ppermute x4, waiting for transfers between devices, from_behind(): return lax.ppermute(block, axis, route)  24.2 us
    ppermute x3, waiting for transfers between devices, body(): chunks = keep + lax.ppermute(send, 'head', route)  22 us
    ppermute x4, starting transfers between devices, from_behind(): return lax.ppermute(block, axis, route)  21.1 us
    ppermute x3, starting transfers between devices, body(): chunks = keep + lax.ppermute(send, 'head', route)  6.21 us
    convert_element_type x2, other arithmetic, local_grads(): prob_low = prob.astype(jnp.bfloat16)  2.87 us
    dot_general x2, matrix products, local_grads(): jnp.einsum('ihe,je->hij', dout, value_window, preferred_element_type=jnp....  2.72 us
    unnamed x13, local copies, waits for them, and re-layouts  2.29 us
    dot_general x2, matrix products, local_grads(): jnp.einsum('hij,je->ihe', dscore, kwin, preferred_element_type=jnp.float32)  2.21 us
  transfers between devices with their start and end apart: 7, of which 6 were waited for; matrix products, arithmetic and copies ran while one was open for 7% of the time, Pallas kernels for 0%

profile of v1, /device:TPU:6, one launch (start us, length us, event | category | flops | bytes accessed | tf_op | source)
XLA Modules:
  0.0 97.3 jit_solution(7875327060809753612)
XLA Ops:
  0.6 0.0 copy-start.2
  0.6 0.0 copy-start.3
  0.7 0.0 copy-start.4
  0.7 1.0 %pad_maximum_fusion = bf16[2,512,128]{2,1,0:T(8,128)(2,1)S(1)} fusion(bf16[1,512,128]{2,1,0:T(8,128)(2,1)} %bitcast.181, bf16[1,512,128]{2,1,0:T(8,128)(2,1)} %bitcast.183), kind=kLoop, calls=%fused_computation.51 | loop fusion | flops 131072 | bytes 524288 | tf_op jit(solution)/shard_map/stack | solution.py:43
  1.7 7.7 %collective-permute-start.1 = (bf16[2,512,128]{2,1,0:T(8,128)(2,1)S(1)}, bf16[2,512,128]{2,1,0:T(8,128)(2,1)S(1)}, u32[]{:S(2)}, u32[]{:S(2)}) collective-permute-start(bf16[2,512,128]{2,1,0:T(8,128)(2,1)S(1)} %pad_maximum_fusion), channel_id=1, source_target_pairs={{0,8},{8,16},{16,24},{24,32},{32,40},{40,48},{48,56},{56,64},{64,7... | collective-permute-start | bytes 786440 | tf_op jit(solution)/shard_map/ppermute | solution.py:12
  9.4 4.3 %collective-permute-start = (bf16[2,512,128]{2,1,0:T(8,128)(2,1)S(1)}, bf16[2,512,128]{2,1,0:T(8,128)(2,1)S(1)}, u32[]{:S(2)}, u32[]{:S(2)}) collective-permute-start(bf16[2,512,128]{2,1,0:T(8,128)(2,1)S(1)} %pad_maximum_fusion), channel_id=1, source_target_pairs={{0,16},{8,24},{16,32},{24,40},{32,48},{40,56},{48,64},{56,72},{64,... | collective-permute-start | bytes 786440 | tf_op jit(solution)/shard_map/ppermute | solution.py:12
  13.8 1.5 %fusion.49 = (bf16[512,1,128]{2,1,0:T(2,128)(2,1)S(1)}, bf16[512,1,128]{2,1,0:T(2,128)(2,1)S(1)}) fusion(bf16[512,2,128]{2,1,0:T(2,128)(2,1)} %param.8), kind=kLoop, calls=%fused_computation.73 | loop fusion | bytes 524288 | tf_op jit(solution)/shard_map/slice | solution.py:58
  15.3 0.1 copy.25
  15.4 0.1 copy.27
  15.6 1.5 %fusion.50 = (bf16[512,1,128]{2,1,0:T(2,128)(2,1)S(1)}, bf16[512,1,128]{2,1,0:T(2,128)(2,1)S(1)}) fusion(bf16[512,2,128]{2,1,0:T(2,128)(2,1)} %param.5), kind=kLoop, calls=%fused_computation.74 | loop fusion | bytes 524288 | tf_op jit(solution)/shard_map/slice | solution.py:57
  17.1 20.2 %collective-permute-done.1 = bf16[2,512,128]{2,1,0:T(8,128)(2,1)S(1)} collective-permute-done((bf16[2,512,128]{2,1,0:T(8,128)(2,1)S(1)}, bf16[2,512,128]{2,1,0:T(8,128)(2,1)S(1)}, u32[]{:S(2)}, u32[]{:S(2)}) %collective-permute-start.1) | collective-permute-done | bytes 262176 | tf_op jit(solution)/shard_map/ppermute | solution.py:12
  37.3 1.2 %collective-permute-done = bf16[2,512,128]{2,1,0:T(8,128)(2,1)S(1)} collective-permute-done((bf16[2,512,128]{2,1,0:T(8,128)(2,1)S(1)}, bf16[2,512,128]{2,1,0:T(8,128)(2,1)S(1)}, u32[]{:S(2)}, u32[]{:S(2)}) %collective-permute-start) | collective-permute-done | bytes 262176 | tf_op jit(solution)/shard_map/ppermute | solution.py:12
  38.5 0.0 copy-done.2
  38.5 0.0 copy-done.3
  38.5 0.1 maximum_maximum_fusion
  38.5 0.0 copy-done.4
  38.6 0.8 select_reduce_fusion.3
  39.4 1.2 %select_reduce_fusion.2 = (f32[512]{0:T(512)S(1)}, f32[512]{0:T(512)S(1)}, f32[1,512,1536]{1,2,0:T(8,128)S(1)}) fusion(f32[1,512,1536]{1,2,0:T(8,128)S(1)} %get-tuple-element.22, f32[512]{0:T(512)S(1)} %get-tuple-element.21, s32[512]{0:T(512)S(1)} %iota_add_fusion.1, s32[512]{0:T(512)S(1)} %copy-done.4, s32[1536]{0:T(1024)S(1)} %iota_add_fusion, ...), kind=kOutput, calls=%fused_computation.16 | convolution fusion | flops 208403456 | bytes 6965248 | tf_op jit(solution)/shard_map/ihe,je->hij/dot_general | solution.py:18
  40.6 1.6 %fusion.12 = (bf16[1,512,1536]{1,2,0:T(8,128)(2,1)S(1)}, f32[512]{0:T(512)S(1)}) fusion(f32[1,512,1536]{1,2,0:T(8,128)S(1)} %get-tuple-element.22, f32[512]{0:T(512)S(1)} %log_add_fusion.1, s32[512]{0:T(512)S(1)} %iota_add_fusion.1, s32[512]{0:T(512)S(1)} %copy-done.4, s32[1536]{0:T(1024)S(1)} %iota_add_fusion, f32[1,512,1536]{1,2,0:T(8,128)S(1)} %get-tuple-element.23, ...), kind=kLoop, calls=%fused_computation.25 | loop fusion | flops 7077376 | bytes 7880704 | tf_op jit(solution)/shard_map/convert_element_type | solution.py:23
  42.3 0.4 fusion.32
  42.7 1.4 %fusion.11 = bf16[512,1536]{0,1:T(8,128)(2,1)S(1)} fusion(f32[1,512,1536]{1,2,0:T(8,128)S(1)} %get-tuple-element.22, f32[512]{0:T(512)S(1)} %fusion.32, f32[512]{0:T(512)S(1)} %log_add_fusion.1, bf16[2,1536,128]{2,1,0:T(8,128)(2,1)S(1)} %maximum_maximum_fusion, bf16[512,1,128]{0,2,1:T(8,128)(2,1)S(1)} %copy.25, s32[512]{0:T(512)S(1)} %iota_add_fusion.1, ...), kind=kOutput, calls=%fused_computation.22 | convolution fusion | flops 207618048 | bytes 5259264 | tf_op jit(solution)/shard_map/ihe,je->hij/dot_general | solution.py:28
  44.1 0.0 copy-start
  44.1 0.6 fusion.42
  44.7 0.6 convolution_multiply_fusion.3
  45.2 1.2 %fusion.13 = bf16[1,512,1536]{1,2,0:T(8,128)(2,1)S(1)} fusion(f32[1,512,1536]{1,2,0:T(8,128)S(1)} %get-tuple-element.23, f32[512]{0:T(512)S(1)} %log_add_fusion, s32[512]{0:T(512)S(1)} %iota_add_fusion.1, s32[512]{0:T(512)S(1)} %copy-done.4, s32[1536]{0:T(1024)S(1)} %iota_add_fusion), kind=kLoop, calls=%fused_computation.26 | loop fusion | flops 4718592 | bytes 4730880 | tf_op jit(solution)/shard_map/convert_element_type | solution.py:23
  46.5 0.0 copy-done
  46.5 0.4 fusion.35
  46.9 1.4 %fusion.10 = bf16[512,1536]{0,1:T(8,128)(2,1)S(1)} fusion(f32[1,512,1536]{1,2,0:T(8,128)S(1)} %get-tuple-element.23, f32[512]{0:T(512)S(1)} %fusion.35, f32[512]{0:T(512)S(1)} %log_add_fusion, bf16[2,1536,128]{2,1,0:T(8,128)(2,1)S(1)} %maximum_maximum_fusion, bf16[512,1,128]{0,2,1:T(8,128)(2,1)S(1)} %copy.27, s32[512]{0:T(512)S(1)} %iota_add_fusion.1, ...), kind=kOutput, calls=%fused_computation.21 | convolution fusion | flops 207618048 | bytes 5259264 | tf_op jit(solution)/shard_map/ihe,je->hij/dot_general | solution.py:28
  48.3 0.6 fusion.40
  48.8 0.6 convolution_multiply_fusion.2
  49.4 0.2 maximum_add_fusion
  49.7 0.0 copy-start.1
  49.7 1.1 %copy-done.1 = f32[3,4,2,64,256]{4,3,2,1,0:T(8,128)} copy-done((f32[3,4,2,64,256]{4,3,2,1,0:T(8,128)}, f32[3,4,2,64,256]{4,3,2,1,0:T(8,128)S(1)}, u32[]{:S(2)}) %copy-start.1) | copy-done | bytes 1572888
  50.8 0.1 dynamic-slice_bitcast_fusion
  50.9 1.9 %collective-permute-start.2 = (f32[3,4,64,256]{3,2,1,0:T(8,128)S(1)}, f32[3,4,64,256]{3,2,1,0:T(8,128)}, u32[]{:S(2)}, u32[]{:S(2)}) collective-permute-start(f32[3,4,64,256]{3,2,1,0:T(8,128)S(1)} %dynamic-slice_bitcast_fusion), channel_id=1, source_target_pairs={{0,1},{1,0},{2,3},{3,2},{4,5},{5,4},{6,7},{7,6},{8,9},{9,8},{10,11... | collective-permute-start | bytes 2359304 | tf_op jit(solution)/shard_map/ppermute | solution.py:79
  52.8 2.3 %collective-permute-done.2 = f32[3,4,64,256]{3,2,1,0:T(8,128)} collective-permute-done((f32[3,4,64,256]{3,2,1,0:T(8,128)S(1)}, f32[3,4,64,256]{3,2,1,0:T(8,128)}, u32[]{:S(2)}, u32[]{:S(2)}) %collective-permute-start.2) | collective-permute-done | bytes 786464 | tf_op jit(solution)/shard_map/ppermute | solution.py:79
  55.2 1.5 %bitcast_add_fusion = f32[3,4,64,256]{3,2,1,0:T(8,128)S(1)} fusion(f32[3,4,64,256]{3,2,1,0:T(8,128)} %collective-permute-done.2, f32[3,4,2,64,256]{4,3,2,1,0:T(8,128)} %copy-done.1, s32[]{:T(128)S(6)} %select_n.70), kind=kLoop, calls=%fused_computation.45 | loop fusion | flops 196608 | bytes 2359300 | tf_op jit(solution)/shard_map/add | solution.py:79
  56.7 0.8 dynamic-slice_bitcast_fusion.1
  57.5 2.4 %collective-permute-start.3 = (f32[3,2,64,256]{3,2,1,0:T(8,128)}, f32[3,2,64,256]{3,2,1,0:T(8,128)S(1)}, u32[]{:S(2)}, u32[]{:S(2)}) collective-permute-start(f32[3,2,64,256]{3,2,1,0:T(8,128)} %dynamic-slice_bitcast_fusion.1), channel_id=1, source_target_pairs={{0,2},{1,3},{2,0},{3,1},{4,6},{5,7},{6,4},{7,5},{8,10},{9,11},{10,... | collective-permute-start | bytes 1179656 | tf_op jit(solution)/shard_map/ppermute | solution.py:79
  59.9 1.8 %fusion.39 = bf16[512,1,128]{0,2,1:T(8,128)(2,1)S(1)} fusion(bf16[512,1536]{0,1:T(8,128)(2,1)} %copy-done, bf16[2,1536,128]{2,1,0:T(8,128)(2,1)S(1)} %maximum_maximum_fusion), kind=kOutput, calls=%fused_computation.43 | convolution fusion | flops 201457664 | bytes 2097152 | tf_op jit(solution)/shard_map/hij,je->ihe/dot_general | solution.py:31
  61.7 9.0 %collective-permute-done.3 = f32[3,2,64,256]{3,2,1,0:T(8,128)S(1)} collective-permute-done((f32[3,2,64,256]{3,2,1,0:T(8,128)}, f32[3,2,64,256]{3,2,1,0:T(8,128)S(1)}, u32[]{:S(2)}, u32[]{:S(2)}) %collective-permute-start.3) | collective-permute-done | bytes 393248 | tf_op jit(solution)/shard_map/ppermute | solution.py:79
  70.7 0.1 bitcast_add_fusion.1
  70.8 1.9 %collective-permute-start.4 = (f32[3,1,64,256]{3,2,1,0:T(8,128)S(1)}, f32[3,1,64,256]{3,2,1,0:T(8,128)S(1)}, u32[]{:S(2)}, u32[]{:S(2)}) collective-permute-start(f32[3,1,64,256]{3,2,1,0:T(8,128)S(1)} %constant_dynamic-slice_fusion), channel_id=1, source_target_pairs={{0,4},{1,5},{2,6},{3,7},{4,0},{5,1},{6,2},{7,3},{8,12},{9,13},{10,... | collective-permute-start | bytes 589832 | tf_op jit(solution)/shard_map/ppermute | solution.py:79
  72.7 0.4 fusion.38
  73.1 10.7 %collective-permute-done.4 = f32[3,1,64,256]{3,2,1,0:T(8,128)S(1)} collective-permute-done((f32[3,1,64,256]{3,2,1,0:T(8,128)S(1)}, f32[3,1,64,256]{3,2,1,0:T(8,128)S(1)}, u32[]{:S(2)}, u32[]{:S(2)}) %collective-permute-start.4) | collective-permute-done | bytes 196640 | tf_op jit(solution)/shard_map/ppermute | solution.py:79
  83.9 6.6 %collective-permute-start.5 = (f32[64,256]{1,0:T(8,128)S(1)}, f32[64,256]{1,0:T(8,128)S(1)}, u32[]{:S(2)}, u32[]{:S(2)}) collective-permute-start(f32[64,256]{1,0:T(8,128)S(1)} %get-tuple-element.15), channel_id=1, source_target_pairs={{8,0},{16,8},{24,16},{32,24},{40,32},{48,40},{56,48},{64,56},{72,6... | collective-permute-start | bytes 196616 | tf_op jit(solution)/shard_map/ppermute | solution.py:12
  90.5 2.5 %collective-permute-start.6 = (f32[64,256]{1,0:T(8,128)S(1)}, f32[64,256]{1,0:T(8,128)S(1)}, u32[]{:S(2)}, u32[]{:S(2)}) collective-permute-start(f32[64,256]{1,0:T(8,128)S(1)} %get-tuple-element.16), channel_id=1, source_target_pairs={{16,0},{24,8},{32,16},{40,24},{48,32},{56,40},{64,48},{72,56},{80,... | collective-permute-start | bytes 196616 | tf_op jit(solution)/shard_map/ppermute | solution.py:12
  93.0 0.9 copy.19
  93.9 0.0 collective-permute-done.5
  94.0 2.7 %collective-permute-done.6 = f32[64,256]{1,0:T(8,128)S(1)} collective-permute-done((f32[64,256]{1,0:T(8,128)S(1)}, f32[64,256]{1,0:T(8,128)S(1)}, u32[]{:S(2)}, u32[]{:S(2)}) %collective-permute-start.6) | collective-permute-done | bytes 65568 | tf_op jit(solution)/shard_map/ppermute | solution.py:12
  96.7 0.6 fusion.51
  (9 shorter events, 0.1 us)
Async XLA Ops:
  0.6 37.9 %copy-start.2 = (bf16[512,128]{1,0:T(8,128)(2,1)S(1)}, bf16[512,128]{1,0:T(8,128)(2,1)}, u32[]{:S(2)}) copy-start(bf16[512,128]{1,0:T(8,128)(2,1)} %param.7) | copy-start | bytes 393220
  0.6 37.8 %copy-start.3 = (bf16[512,128]{1,0:T(8,128)(2,1)S(1)}, bf16[512,128]{1,0:T(8,128)(2,1)}, u32[]{:S(2)}) copy-start(bf16[512,128]{1,0:T(8,128)(2,1)} %param.6) | copy-start | bytes 393220
  0.7 37.9 %copy-start.4 = (s32[512]{0:T(512)S(1)}, s32[512]{0:T(512)}, u32[]{:S(2)}) copy-start(s32[512]{0:T(512)} %param.9) | copy-start | bytes 6148
  1.7 35.6 %collective-permute-start.1 = (bf16[2,512,128]{2,1,0:T(8,128)(2,1)S(1)}, bf16[2,512,128]{2,1,0:T(8,128)(2,1)S(1)}, u32[]{:S(2)}, u32[]{:S(2)}) collective-permute-start(bf16[2,512,128]{2,1,0:T(8,128)(2,1)S(1)} %pad_maximum_fusion), channel_id=1, source_target_pairs={{0,8},{8,16},{16,24},{24,32},{32,40},{40,48},{48,56},{56,64},{64,7... | collective-permute-start | bytes 786440 | tf_op jit(solution)/shard_map/ppermute | solution.py:12
  9.4 29.0 %collective-permute-start = (bf16[2,512,128]{2,1,0:T(8,128)(2,1)S(1)}, bf16[2,512,128]{2,1,0:T(8,128)(2,1)S(1)}, u32[]{:S(2)}, u32[]{:S(2)}) collective-permute-start(bf16[2,512,128]{2,1,0:T(8,128)(2,1)S(1)} %pad_maximum_fusion), channel_id=1, source_target_pairs={{0,16},{8,24},{16,32},{24,40},{32,48},{40,56},{48,64},{56,72},{64,... | collective-permute-start | bytes 786440 | tf_op jit(solution)/shard_map/ppermute | solution.py:12
  44.1 2.4 %copy-start = (bf16[512,1536]{0,1:T(8,128)(2,1)}, bf16[512,1536]{0,1:T(8,128)(2,1)S(1)}, u32[]{:S(2)}) copy-start(bf16[512,1536]{0,1:T(8,128)(2,1)S(1)} %fusion.11) | copy-start | bytes 4718596
  49.7 1.1 %copy-start.1 = (f32[3,4,2,64,256]{4,3,2,1,0:T(8,128)}, f32[3,4,2,64,256]{4,3,2,1,0:T(8,128)S(1)}, u32[]{:S(2)}) copy-start(f32[3,4,2,64,256]{4,3,2,1,0:T(8,128)S(1)} %maximum_add_fusion) | copy-start | bytes 4718596
  50.9 4.3 %collective-permute-start.2 = (f32[3,4,64,256]{3,2,1,0:T(8,128)S(1)}, f32[3,4,64,256]{3,2,1,0:T(8,128)}, u32[]{:S(2)}, u32[]{:S(2)}) collective-permute-start(f32[3,4,64,256]{3,2,1,0:T(8,128)S(1)} %dynamic-slice_bitcast_fusion), channel_id=1, source_target_pairs={{0,1},{1,0},{2,3},{3,2},{4,5},{5,4},{6,7},{7,6},{8,9},{9,8},{10,11... | collective-permute-start | bytes 2359304 | tf_op jit(solution)/shard_map/ppermute | solution.py:79
  57.5 13.2 %collective-permute-start.3 = (f32[3,2,64,256]{3,2,1,0:T(8,128)}, f32[3,2,64,256]{3,2,1,0:T(8,128)S(1)}, u32[]{:S(2)}, u32[]{:S(2)}) collective-permute-start(f32[3,2,64,256]{3,2,1,0:T(8,128)} %dynamic-slice_bitcast_fusion.1), channel_id=1, source_target_pairs={{0,2},{1,3},{2,0},{3,1},{4,6},{5,7},{6,4},{7,5},{8,10},{9,11},{10,... | collective-permute-start | bytes 1179656 | tf_op jit(solution)/shard_map/ppermute | solution.py:79
  70.8 13.0 %collective-permute-start.4 = (f32[3,1,64,256]{3,2,1,0:T(8,128)S(1)}, f32[3,1,64,256]{3,2,1,0:T(8,128)S(1)}, u32[]{:S(2)}, u32[]{:S(2)}) collective-permute-start(f32[3,1,64,256]{3,2,1,0:T(8,128)S(1)} %constant_dynamic-slice_fusion), channel_id=1, source_target_pairs={{0,4},{1,5},{2,6},{3,7},{4,0},{5,1},{6,2},{7,3},{8,12},{9,13},{10,... | collective-permute-start | bytes 589832 | tf_op jit(solution)/shard_map/ppermute | solution.py:79
  83.9 10.1 %collective-permute-start.5 = (f32[64,256]{1,0:T(8,128)S(1)}, f32[64,256]{1,0:T(8,128)S(1)}, u32[]{:S(2)}, u32[]{:S(2)}) collective-permute-start(f32[64,256]{1,0:T(8,128)S(1)} %get-tuple-element.15), channel_id=1, source_target_pairs={{8,0},{16,8},{24,16},{32,24},{40,32},{48,40},{56,48},{64,56},{72,6... | collective-permute-start | bytes 196616 | tf_op jit(solution)/shard_map/ppermute | solution.py:12
  90.5 6.2 %collective-permute-start.6 = (f32[64,256]{1,0:T(8,128)S(1)}, f32[64,256]{1,0:T(8,128)S(1)}, u32[]{:S(2)}, u32[]{:S(2)}) collective-permute-start(f32[64,256]{1,0:T(8,128)S(1)} %get-tuple-element.16), channel_id=1, source_target_pairs={{16,0},{24,8},{32,16},{40,24},{48,32},{56,40},{64,48},{72,56},{80,... | collective-permute-start | bytes 196616 | tf_op jit(solution)/shard_map/ppermute | solution.py:12

commit v2 on v1

--- a/solution.py
+++ b/solution.py
@@ -10,6 +10,22 @@
     devices = range(lax.axis_size(axis))
     route = [(i - distance, i) for i in devices if i - distance in devices]
     return lax.ppermute(block, axis, route)
+
+
+def mirror(head, parts):
+    lanes = parts // 2
+    return (lanes - 1 - head // 2) * 2 + head % 2
+
+
+def nearest_next(block, back=False):
+    parts = lax.axis_size("head")
+    blocks = lax.axis_size(("dcn", "blk"))
+    route = []
+    for b in range(blocks - 1):
+        for h in range(parts):
+            pair = (b * parts + h, (b + 1) * parts + mirror(h, parts))
+            route.append(pair[::-1] if back else pair)
+    return lax.ppermute(block, ("dcn", "blk", "head"), route)
 
 
 def local_grads(q, dout, starts, kwin, value_window, qpos, kpos):
@@ -43,7 +59,10 @@
     packed = jnp.stack([keys, values])
     pieces = []
     for step in range(WIN, 0, -1):
-        pieces.append(from_behind(packed, ("dcn", "blk"), step))
+        if step == 1:
+            pieces.append(nearest_next(packed))
+        else:
+            pieces.append(from_behind(packed, ("dcn", "blk"), step))
     pieces.append(packed)
     window = jnp.concatenate(pieces, axis=1)
     window_span = (WIN + 1) * rows
@@ -69,6 +88,8 @@
     piece = rows // parts
     head = lax.axis_index("head")
     chunks = terms.reshape(WIN + 1, parts, piece, 2 * window_width)
+    order = jnp.array([mirror(c, parts) for c in range(parts)], jnp.int32)
+    chunks = chunks.at[WIN - 1].set(chunks[WIN - 1][order])
     stride = 1
     while stride < parts:
         bit = (head // stride) % 2
@@ -81,7 +102,10 @@
     reduced = chunks.reshape(WIN + 1, piece, 2 * window_width)
     total = reduced[WIN]
     for step in range(1, WIN + 1):
-        total = total + from_behind(reduced[WIN - step], ("dcn", "blk"), -step)
+        if step == 1:
+            total = total + nearest_next(reduced[WIN - step], back=True)
+        else:
+            total = total + from_behind(reduced[WIN - step], ("dcn", "blk"), -step)
     k_grad = total[:, :window_width].astype(jnp.bfloat16)
     v_grad = total[:, window_width:].astype(jnp.bfloat16)
     return (q_grad, k_grad, v_grad)

time: 97.7 us -> 102 us (1.044)
  the two profiles are of different devices: /device:TPU:6 before, /device:TPU:15 now
where the time goes in v2:
time: 102 us; the launch traced here: 100 us
  waiting for transfers between devices  39.8 us (39%)
  starting transfers between devices  28.7 us (28%)
  matrix products  11.5 us (11%)
  local copies, waits for them, and re-layouts  11 us (11%)
  other arithmetic  8.15 us (8%)
  between operations  1.13 us (1%)
    ppermute x2, waiting for transfers between devices, nearest_next(): return lax.ppermute(block, ('dcn', 'blk', 'head'), route)  19.2 us
    ppermute x3, waiting for transfers between devices, body(): chunks = keep + lax.ppermute(send, 'head', route)  18.4 us
    ppermute x2, starting transfers between devices, nearest_next(): return lax.ppermute(block, ('dcn', 'blk', 'head'), route)  13.4 us
    ppermute x3, starting transfers between devices, body(): chunks = keep + lax.ppermute(send, 'head', route)  9.06 us
    ppermute x2, starting transfers between devices, from_behind(): return lax.ppermute(block, axis, route)  6.21 us
    unnamed x27, local copies, waits for them, and re-layouts  3.19 us
    dot_general x2, matrix products, local_grads(): jnp.einsum('ihe,je->hij', dout, value_window, preferred_element_type=jnp....  2.71 us
    add x3, other arithmetic, body(): chunks = keep + lax.ppermute(send, 'head', route)  2.55 us
  transfers between devices with their start and end apart: 7, of which 6 were waited for; matrix products, arithmetic and copies ran while one was open for 7% of the time, Pallas kernels for 0%

profile of v2, /device:TPU:15, one launch (start us, length us, event | category | flops | bytes accessed | tf_op | source)
XLA Modules:
  0.0 100.3 jit_solution(17778670937759338186)
XLA Ops:
  0.6 0.0 copy-start.9
  0.6 0.0 copy-start.10
  0.7 0.0 copy-start.11
  0.7 1.0 %pad_maximum_fusion.2 = bf16[2,512,128]{2,1,0:T(8,128)(2,1)S(1)} fusion(bf16[1,512,128]{2,1,0:T(8,128)(2,1)} %bitcast.170, bf16[1,512,128]{2,1,0:T(8,128)(2,1)} %bitcast.172), kind=kLoop, calls=%fused_computation.54 | loop fusion | flops 131072 | bytes 524288 | tf_op jit(solution)/shard_map/stack | solution.py:59
  1.7 5.8 %collective-permute-start.1 = (bf16[2,512,128]{2,1,0:T(8,128)(2,1)S(1)}, bf16[2,512,128]{2,1,0:T(8,128)(2,1)S(1)}, u32[]{:S(2)}, u32[]{:S(2)}) collective-permute-start(bf16[2,512,128]{2,1,0:T(8,128)(2,1)S(1)} %pad_maximum_fusion.2), channel_id=1, source_target_pairs={{0,14},{1,15},{2,12},{3,13},{4,10},{5,11},{6,8},{7,9},{8,22},{9,23... | collective-permute-start | bytes 786440 | tf_op jit(solution)/shard_map/ppermute | solution.py:28
  7.5 4.0 %collective-permute-start = (bf16[2,512,128]{2,1,0:T(8,128)(2,1)S(1)}, bf16[2,512,128]{2,1,0:T(8,128)(2,1)S(1)}, u32[]{:S(2)}, u32[]{:S(2)}) collective-permute-start(bf16[2,512,128]{2,1,0:T(8,128)(2,1)S(1)} %pad_maximum_fusion.2), channel_id=1, source_target_pairs={{0,16},{8,24},{16,32},{24,40},{32,48},{40,56},{48,64},{56,72},{64,... | collective-permute-start | bytes 786440 | tf_op jit(solution)/shard_map/ppermute | solution.py:12
  11.5 0.7 pad_clamp_fusion
  12.2 1.5 %fusion.38 = (bf16[512,1,128]{2,1,0:T(2,128)(2,1)S(1)}, bf16[512,1,128]{2,1,0:T(2,128)(2,1)S(1)}) fusion(bf16[512,2,128]{2,1,0:T(2,128)(2,1)} %param.11), kind=kLoop, calls=%fused_computation.77 | loop fusion | bytes 524288 | tf_op jit(solution)/shard_map/slice | solution.py:77
  13.7 0.1 copy.20
  13.8 0.1 copy.22
  14.0 1.5 %fusion.39 = (bf16[512,1,128]{2,1,0:T(2,128)(2,1)S(1)}, bf16[512,1,128]{2,1,0:T(2,128)(2,1)S(1)}) fusion(bf16[512,2,128]{2,1,0:T(2,128)(2,1)} %param.8), kind=kLoop, calls=%fused_computation.78 | loop fusion | bytes 524288 | tf_op jit(solution)/shard_map/slice | solution.py:76
  15.5 19.2 %collective-permute-done.1 = bf16[2,512,128]{2,1,0:T(8,128)(2,1)S(1)} collective-permute-done((bf16[2,512,128]{2,1,0:T(8,128)(2,1)S(1)}, bf16[2,512,128]{2,1,0:T(8,128)(2,1)S(1)}, u32[]{:S(2)}, u32[]{:S(2)}) %collective-permute-start.1) | collective-permute-done | bytes 262176 | tf_op jit(solution)/shard_map/ppermute | solution.py:28
  34.6 0.4 collective-permute-done
  35.0 0.0 copy-done.9
  35.0 0.0 copy-done.10
  35.0 0.1 maximum_maximum_fusion
  35.1 0.0 copy-start.5
  35.1 0.0 copy-done.11
  35.1 0.8 select_reduce_fusion.3
  35.9 1.2 %select_reduce_fusion.2 = (f32[512]{0:T(512)S(1)}, f32[512]{0:T(512)S(1)}, f32[1,512,1536]{1,2,0:T(8,128)S(1)}) fusion(f32[1,512,1536]{1,2,0:T(8,128)S(1)} %get-tuple-element.32, f32[512]{0:T(512)S(1)} %get-tuple-element.31, s32[512]{0:T(512)S(1)} %iota_add_fusion.1, s32[512]{0:T(512)S(1)} %copy-done.11, s32[1536]{0:T(1024)S(1)} %iota_add_fusion, ...), kind=kOutput, calls=%fused_computation.17 | convolution fusion | flops 208403456 | bytes 6965248 | tf_op jit(solution)/shard_map/ihe,je->hij/dot_general | solution.py:34
  37.1 1.3 %select_reduce_fusion = f32[512]{0:T(512)S(1)} fusion(f32[1,512,1536]{1,2,0:T(8,128)S(1)} %get-tuple-element.33, f32[512]{0:T(512)S(1)} %get-tuple-element.22, s32[512]{0:T(512)S(1)} %iota_add_fusion.1, s32[512]{0:T(512)S(1)} %copy-done.11, s32[1536]{0:T(1024)S(1)} %iota_add_fusion), kind=kLoop, calls=%fused_computation.14 | loop fusion | flops 4718080 | bytes 3160064 | tf_op jit(solution)/shard_map/reduce_sum | solution.py:37
  38.4 1.0 %fusion.21 = f32[512]{0:T(512)S(1)} fusion(bf16[512,1,128]{0,2,1:T(8,128)(2,1)S(1)} %copy.22, bf16[2,1536,128]{2,1,0:T(8,128)(2,1)S(1)} %maximum_maximum_fusion, f32[1,512,1536]{1,2,0:T(8,128)S(1)} %get-tuple-element.33, f32[512]{0:T(512)S(1)} %get-tuple-element.34, s32[512]{0:T(512)S(1)} %iota_add_fusion.1, s32[512]{0:T(512)S(1)} %copy-done.11, ...), kind=kOutput, calls=%fused_computation.40 | convolution fusion | flops 206241280 | bytes 3686400 | tf_op jit(solution)/shard_map/hij,je->ihe/dot_general | solution.py:40
  39.5 0.8 fusion.25
  40.3 0.0 copy-start.3
  40.3 1.0 %fusion.20 = f32[512]{0:T(512)S(1)} fusion(bf16[512,1,128]{0,2,1:T(8,128)(2,1)S(1)} %copy.20, bf16[2,1536,128]{2,1,0:T(8,128)(2,1)S(1)} %maximum_maximum_fusion, f32[1,512,1536]{1,2,0:T(8,128)S(1)} %get-tuple-element.32, f32[512]{0:T(512)S(1)} %get-tuple-element.35, s32[512]{0:T(512)S(1)} %iota_add_fusion.1, s32[512]{0:T(512)S(1)} %copy-done.11, ...), kind=kOutput, calls=%fused_computation.39 | convolution fusion | flops 206241280 | bytes 3686400 | tf_op jit(solution)/shard_map/hij,je->ihe/dot_general | solution.py:40
  41.3 0.8 fusion.28
  42.2 0.0 copy-start.4
  42.2 1.4 %fusion.10 = bf16[512,1536]{0,1:T(8,128)(2,1)S(1)} fusion(f32[1,512,1536]{1,2,0:T(8,128)S(1)} %get-tuple-element.33, f32[512]{0:T(512)S(1)} %fusion.21, f32[512]{0:T(512)S(1)} %get-tuple-element.34, bf16[2,1536,128]{2,1,0:T(8,128)(2,1)S(1)} %maximum_maximum_fusion, bf16[512,1,128]{0,2,1:T(8,128)(2,1)S(1)} %copy.22, s32[512]{0:T(512)S(1)} %iota_add_fusion.1, ...), kind=kOutput, calls=%fused_computation.22 | convolution fusion | flops 207618048 | bytes 5259264 | tf_op jit(solution)/shard_map/ihe,je->hij/dot_general | solution.py:44
  43.6 0.0 copy-start
  43.6 0.6 convolution_multiply_fusion.2
  44.2 0.0 copy-done.5
  44.2 1.3 %fusion.11 = bf16[512,1536]{0,1:T(8,128)(2,1)S(1)} fusion(f32[1,512,1536]{1,2,0:T(8,128)S(1)} %get-tuple-element.32, f32[512]{0:T(512)S(1)} %fusion.20, f32[512]{0:T(512)S(1)} %get-tuple-element.35, bf16[2,1536,128]{2,1,0:T(8,128)(2,1)S(1)} %maximum_maximum_fusion, bf16[512,1,128]{0,2,1:T(8,128)(2,1)S(1)} %copy.20, s32[512]{0:T(512)S(1)} %iota_add_fusion.1, ...), kind=kOutput, calls=%fused_computation.23 | convolution fusion | flops 207618048 | bytes 5259264 | tf_op jit(solution)/shard_map/ihe,je->hij/dot_general | solution.py:44
  45.5 0.0 copy-done
  45.5 0.6 convolution_multiply_fusion.3
  46.1 0.0 copy-done.3
  46.1 0.0 copy-done.4
  46.1 0.9 fusion.24
  47.0 2.4 %gather_fusion = f32[8,64,256]{2,1,0:T(8,128)} fusion(f32[8,64,256]{2,1,0:T(8,128)} %bitcast.169, s32[1024]{0:T(1024)S(1)} %pad_clamp_fusion), kind=kCustom, calls=%fused_computation | custom fusion | bytes 1048608 | tf_op jit(solution)/shard_map/gather | solution.py:92
  49.4 1.6 %maximum_add_fusion = f32[3,8,64,256]{3,2,1,0:T(8,128)S(1)} fusion(f32[3,8,64,128]{3,2,1,0:T(8,128)} %bitcast.166, f32[3,8,64,128]{3,2,1,0:T(8,128)S(1)} %bitcast.162, f32[3,8,64,128]{3,2,1,0:T(8,128)} %bitcast.165, f32[3,8,64,128]{3,2,1,0:T(8,128)S(1)} %bitcast.161), kind=kLoop, calls=%fused_computation.30 | loop fusion | flops 1179648 | bytes 4718592 | tf_op jit(solution)/shard_map/add | solution.py:85
  51.1 0.0 copy-done.8
  51.1 0.0 copy-start.1
  51.1 0.0 copy-start.2
  51.1 1.1 %copy-done.2 = f32[3,8,64,256]{3,2,1,0:T(8,128)} copy-done((f32[3,8,64,256]{3,2,1,0:T(8,128)}, f32[3,8,64,256]{3,2,1,0:T(8,128)S(1)}, u32[]{:S(2)}) %copy-start.2) | copy-done | bytes 1572888
  52.3 1.0 dynamic-slice_bitcast_fusion
  53.3 4.4 %collective-permute-start.2 = (f32[3,4,64,256]{3,2,1,0:T(8,128)}, f32[3,4,64,256]{3,2,1,0:T(8,128)}, u32[]{:S(2)}, u32[]{:S(2)}) collective-permute-start(f32[3,4,64,256]{3,2,1,0:T(8,128)} %dynamic-slice_bitcast_fusion), channel_id=1, source_target_pairs={{0,1},{1,0},{2,3},{3,2},{4,5},{5,4},{6,7},{7,6},{8,9},{9,8},{10,11... | collective-permute-start | bytes 2359304 | tf_op jit(solution)/shard_map/ppermute | solution.py:100
  57.7 2.2 %collective-permute-done.2 = f32[3,4,64,256]{3,2,1,0:T(8,128)} collective-permute-done((f32[3,4,64,256]{3,2,1,0:T(8,128)}, f32[3,4,64,256]{3,2,1,0:T(8,128)}, u32[]{:S(2)}, u32[]{:S(2)}) %collective-permute-start.2) | collective-permute-done | bytes 786464 | tf_op jit(solution)/shard_map/ppermute | solution.py:100
  59.9 1.5 %bitcast_add_fusion = f32[3,4,64,256]{3,2,1,0:T(8,128)S(1)} fusion(f32[3,4,64,256]{3,2,1,0:T(8,128)} %collective-permute-done.2, f32[3,4,2,64,256]{4,3,2,1,0:T(8,128)} %bitcast.164, s32[]{:T(128)S(6)} %select_n.74), kind=kLoop, calls=%fused_computation.44 | loop fusion | flops 196608 | bytes 2359300 | tf_op jit(solution)/shard_map/add | solution.py:100
  61.4 0.9 copy-done.7
  62.2 0.8 dynamic-slice_bitcast_fusion.1
  63.0 1.9 %collective-permute-start.3 = (f32[3,2,64,256]{3,2,1,0:T(8,128)}, f32[3,2,64,256]{3,2,1,0:T(8,128)S(1)}, u32[]{:S(2)}, u32[]{:S(2)}) collective-permute-start(f32[3,2,64,256]{3,2,1,0:T(8,128)} %dynamic-slice_bitcast_fusion.1), channel_id=1, source_target_pairs={{0,2},{1,3},{2,0},{3,1},{4,6},{5,7},{6,4},{7,5},{8,10},{9,11},{10,... | collective-permute-start | bytes 1179656 | tf_op jit(solution)/shard_map/ppermute | solution.py:100
  65.0 0.0 copy-done.1
  65.0 0.0 copy-start.6
  65.0 1.5 %fusion.22 = bf16[512,1,128]{0,2,1:T(8,128)(2,1)S(1)} fusion(bf16[512,1536]{0,1:T(8,128)(2,1)S(1)} %copy-done.1, bf16[2,1536,128]{2,1,0:T(8,128)(2,1)} %copy-done.5), kind=kOutput, calls=%fused_computation.41 | convolution fusion | flops 201457664 | bytes 2097152 | tf_op jit(solution)/shard_map/hij,je->ihe/dot_general | solution.py:47
  66.5 9.0 %collective-permute-done.3 = f32[3,2,64,256]{3,2,1,0:T(8,128)S(1)} collective-permute-done((f32[3,2,64,256]{3,2,1,0:T(8,128)}, f32[3,2,64,256]{3,2,1,0:T(8,128)S(1)}, u32[]{:S(2)}, u32[]{:S(2)}) %collective-permute-start.3) | collective-permute-done | bytes 393248 | tf_op jit(solution)/shard_map/ppermute | solution.py:100
  75.5 1.0 %bitcast_add_fusion.1 = f32[3,2,64,256]{3,2,1,0:T(8,128)S(1)} fusion(f32[3,2,64,256]{3,2,1,0:T(8,128)S(1)} %collective-permute-done.3, f32[3,2,2,64,256]{4,3,2,1,0:T(8,128)} %bitcast.168, s32[]{:T(128)S(6)} %select_n.78), kind=kLoop, calls=%fused_computation.52 | loop fusion | flops 98304 | bytes 1179652 | tf_op jit(solution)/shard_map/add | solution.py:100
  76.5 2.8 %collective-permute-start.4 = (f32[3,1,64,256]{3,2,1,0:T(8,128)S(1)}, f32[3,1,64,256]{3,2,1,0:T(8,128)S(1)}, u32[]{:S(2)}, u32[]{:S(2)}) collective-permute-start(f32[3,1,64,256]{3,2,1,0:T(8,128)S(1)} %constant_dynamic-slice_fusion), channel_id=1, source_target_pairs={{0,4},{1,5},{2,6},{3,7},{4,0},{5,1},{6,2},{7,3},{8,12},{9,13},{10,... | collective-permute-start | bytes 589832 | tf_op jit(solution)/shard_map/ppermute | solution.py:100
  79.3 0.4 fusion.23
  79.7 7.2 %collective-permute-done.4 = f32[3,1,64,256]{3,2,1,0:T(8,128)S(1)} collective-permute-done((f32[3,1,64,256]{3,2,1,0:T(8,128)S(1)}, f32[3,1,64,256]{3,2,1,0:T(8,128)S(1)}, u32[]{:S(2)}, u32[]{:S(2)}) %collective-permute-start.4) | collective-permute-done | bytes 196640 | tf_op jit(solution)/shard_map/ppermute | solution.py:100
  87.0 7.6 %collective-permute-start.5 = (f32[64,256]{1,0:T(8,128)S(1)}, f32[64,256]{1,0:T(8,128)S(1)}, u32[]{:S(2)}, u32[]{:S(2)}) collective-permute-start(f32[64,256]{1,0:T(8,128)S(1)} %get-tuple-element.27), channel_id=1, source_target_pairs={{14,0},{15,1},{12,2},{13,3},{10,4},{11,5},{8,6},{9,7},{22,8},{23,9... | collective-permute-start | bytes 196616 | tf_op jit(solution)/shard_map/ppermute | solution.py:28
  94.7 2.2 %collective-permute-start.6 = (f32[64,256]{1,0:T(8,128)S(1)}, f32[64,256]{1,0:T(8,128)S(1)}, u32[]{:S(2)}, u32[]{:S(2)}) collective-permute-start(f32[64,256]{1,0:T(8,128)S(1)} %get-tuple-element.28), channel_id=1, source_target_pairs={{16,0},{24,8},{32,16},{40,24},{48,32},{56,40},{64,48},{72,56},{80,... | collective-permute-start | bytes 196616 | tf_op jit(solution)/shard_map/ppermute | solution.py:12
  96.9 0.9 copy.18
  97.8 0.0 collective-permute-done.5
  97.8 1.9 %collective-permute-done.6 = f32[64,256]{1,0:T(8,128)S(1)} collective-permute-done((f32[64,256]{1,0:T(8,128)S(1)}, f32[64,256]{1,0:T(8,128)S(1)}, u32[]{:S(2)}, u32[]{:S(2)}) %collective-permute-start.6) | collective-permute-done | bytes 65568 | tf_op jit(solution)/shard_map/ppermute | solution.py:12
  99.7 0.6 fusion.40
  (12 shorter events, 0.2 us)
Async XLA Ops:
  0.6 34.4 %copy-start.9 = (bf16[512,128]{1,0:T(8,128)(2,1)S(1)}, bf16[512,128]{1,0:T(8,128)(2,1)}, u32[]{:S(2)}) copy-start(bf16[512,128]{1,0:T(8,128)(2,1)} %param.10) | copy-start | bytes 393220
  0.6 34.4 %copy-start.10 = (bf16[512,128]{1,0:T(8,128)(2,1)S(1)}, bf16[512,128]{1,0:T(8,128)(2,1)}, u32[]{:S(2)}) copy-start(bf16[512,128]{1,0:T(8,128)(2,1)} %param.9) | copy-start | bytes 393220
  0.7 34.4 %copy-start.11 = (s32[512]{0:T(512)S(1)}, s32[512]{0:T(512)}, u32[]{:S(2)}) copy-start(s32[512]{0:T(512)} %param.12) | copy-start | bytes 6148
  1.7 32.9 %collective-permute-start.1 = (bf16[2,512,128]{2,1,0:T(8,128)(2,1)S(1)}, bf16[2,512,128]{2,1,0:T(8,128)(2,1)S(1)}, u32[]{:S(2)}, u32[]{:S(2)}) collective-permute-start(bf16[2,512,128]{2,1,0:T(8,128)(2,1)S(1)} %pad_maximum_fusion.2), channel_id=1, source_target_pairs={{0,14},{1,15},{2,12},{3,13},{4,10},{5,11},{6,8},{7,9},{8,22},{9,23... | collective-permute-start | bytes 786440 | tf_op jit(solution)/shard_map/ppermute | solution.py:28
  7.5 27.5 %collective-permute-start = (bf16[2,512,128]{2,1,0:T(8,128)(2,1)S(1)}, bf16[2,512,128]{2,1,0:T(8,128)(2,1)S(1)}, u32[]{:S(2)}, u32[]{:S(2)}) collective-permute-start(bf16[2,512,128]{2,1,0:T(8,128)(2,1)S(1)} %pad_maximum_fusion.2), channel_id=1, source_target_pairs={{0,16},{8,24},{16,32},{24,40},{32,48},{40,56},{48,64},{56,72},{64,... | collective-permute-start | bytes 786440 | tf_op jit(solution)/shard_map/ppermute | solution.py:12
  35.1 9.1 %copy-start.5 = (bf16[2,1536,128]{2,1,0:T(8,128)(2,1)}, bf16[2,1536,128]{2,1,0:T(8,128)(2,1)S(1)}, u32[]{:S(2)}) copy-start(bf16[2,1536,128]{2,1,0:T(8,128)(2,1)S(1)} %maximum_maximum_fusion) | copy-start | bytes 2359300
  40.3 5.8 %copy-start.3 = (f32[1536,128]{1,0:T(8,128)}, f32[1536,128]{1,0:T(8,128)S(1)}, u32[]{:S(2)}) copy-start(f32[1536,128]{1,0:T(8,128)S(1)} %fusion.25) | copy-start | bytes 2359300
  42.2 3.9 %copy-start.4 = (f32[1536,128]{1,0:T(8,128)}, f32[1536,128]{1,0:T(8,128)S(1)}, u32[]{:S(2)}) copy-start(f32[1536,128]{1,0:T(8,128)S(1)} %fusion.28) | copy-start | bytes 2359300
  43.6 2.0 %copy-start = (bf16[512,1536]{0,1:T(8,128)(2,1)}, bf16[512,1536]{0,1:T(8,128)(2,1)S(1)}, u32[]{:S(2)}) copy-start(bf16[512,1536]{0,1:T(8,128)(2,1)S(1)} %fusion.10) | copy-start | bytes 4718596
  49.4 1.7 %copy-start.8 = (f32[8,64,256]{2,1,0:T(8,128)S(1)}, f32[8,64,256]{2,1,0:T(8,128)}, u32[]{:S(2)}) copy-start(f32[8,64,256]{2,1,0:T(8,128)} %gather_fusion) | copy-start | bytes 1572868
  51.1 13.9 %copy-start.1 = (bf16[512,1536]{0,1:T(8,128)(2,1)S(1)}, bf16[512,1536]{0,1:T(8,128)(2,1)}, u32[]{:S(2)}) copy-start(bf16[512,1536]{0,1:T(8,128)(2,1)} %copy-done) | copy-start | bytes 4718596
  51.1 1.2 %copy-start.2 = (f32[3,8,64,256]{3,2,1,0:T(8,128)}, f32[3,8,64,256]{3,2,1,0:T(8,128)S(1)}, u32[]{:S(2)}) copy-start(f32[3,8,64,256]{3,2,1,0:T(8,128)S(1)} %bitcast_dynamic-update-slice_fusion) | copy-start | bytes 4718596
  53.3 6.6 %collective-permute-start.2 = (f32[3,4,64,256]{3,2,1,0:T(8,128)}, f32[3,4,64,256]{3,2,1,0:T(8,128)}, u32[]{:S(2)}, u32[]{:S(2)}) collective-permute-start(f32[3,4,64,256]{3,2,1,0:T(8,128)} %dynamic-slice_bitcast_fusion), channel_id=1, source_target_pairs={{0,1},{1,0},{2,3},{3,2},{4,5},{5,4},{6,7},{7,6},{8,9},{9,8},{10,11... | collective-permute-start | bytes 2359304 | tf_op jit(solution)/shard_map/ppermute | solution.py:100
  61.4 0.9 copy-start.7
  63.0 12.4 %collective-permute-start.3 = (f32[3,2,64,256]{3,2,1,0:T(8,128)}, f32[3,2,64,256]{3,2,1,0:T(8,128)S(1)}, u32[]{:S(2)}, u32[]{:S(2)}) collective-permute-start(f32[3,2,64,256]{3,2,1,0:T(8,128)} %dynamic-slice_bitcast_fusion.1), channel_id=1, source_target_pairs={{0,2},{1,3},{2,0},{3,1},{4,6},{5,7},{6,4},{7,5},{8,10},{9,11},{10,... | collective-permute-start | bytes 1179656 | tf_op jit(solution)/shard_map/ppermute | solution.py:100
  65.0 14.3 %copy-start.6 = (bf16[2,1536,128]{2,1,0:T(8,128)(2,1)S(1)}, bf16[2,1536,128]{2,1,0:T(8,128)(2,1)}, u32[]{:S(2)}) copy-start(bf16[2,1536,128]{2,1,0:T(8,128)(2,1)} %copy-done.5) | copy-start | bytes 2359300
  76.5 10.4 %collective-permute-start.4 = (f32[3,1,64,256]{3,2,1,0:T(8,128)S(1)}, f32[3,1,64,256]{3,2,1,0:T(8,128)S(1)}, u32[]{:S(2)}, u32[]{:S(2)}) collective-permute-start(f32[3,1,64,256]{3,2,1,0:T(8,128)S(1)} %constant_dynamic-slice_fusion), channel_id=1, source_target_pairs={{0,4},{1,5},{2,6},{3,7},{4,0},{5,1},{6,2},{7,3},{8,12},{9,13},{10,... | collective-permute-start | bytes 589832 | tf_op jit(solution)/shard_map/ppermute | solution.py:100
  87.0 10.8 %collective-permute-start.5 = (f32[64,256]{1,0:T(8,128)S(1)}, f32[64,256]{1,0:T(8,128)S(1)}, u32[]{:S(2)}, u32[]{:S(2)}) collective-permute-start(f32[64,256]{1,0:T(8,128)S(1)} %get-tuple-element.27), channel_id=1, source_target_pairs={{14,0},{15,1},{12,2},{13,3},{10,4},{11,5},{8,6},{9,7},{22,8},{23,9... | collective-permute-start | bytes 196616 | tf_op jit(solution)/shard_map/ppermute | solution.py:28
  94.7 5.0 %collective-permute-start.6 = (f32[64,256]{1,0:T(8,128)S(1)}, f32[64,256]{1,0:T(8,128)S(1)}, u32[]{:S(2)}, u32[]{:S(2)}) collective-permute-start(f32[64,256]{1,0:T(8,128)S(1)} %get-tuple-element.28), channel_id=1, source_target_pairs={{16,0},{24,8},{32,16},{40,24},{48,32},{56,40},{64,48},{72,56},{80,... | collective-permute-start | bytes 196616 | tf_op jit(solution)/shard_map/ppermute | solution.py:12

commit v3 on v2

--- a/solution.py
+++ b/solution.py
@@ -2,6 +2,8 @@
 import jax.numpy as jnp
 from jax import lax
 from jax.sharding import PartitionSpec as P
+from jax.experimental import pallas as pl
+from jax.experimental.pallas import tpu as pltpu
 
 WIN = 2
 
@@ -26,6 +28,77 @@
             pair = (b * parts + h, (b + 1) * parts + mirror(h, parts))
             route.append(pair[::-1] if back else pair)
     return lax.ppermute(block, ("dcn", "blk", "head"), route)
+
+
+def head_reduce_kernel(x_ref, o_ref, r1, r2, r3, a1, a2, send_sems, recv_sems):
+    mesh_id = pl.DeviceIdType.MESH
+    dcn = lax.axis_index("dcn")
+    blk = lax.axis_index("blk")
+    head = lax.axis_index("head")
+    bits = [head % 2, (head // 2) % 2, (head // 4) % 2]
+    partners = [head + 1 - 2 * bits[0], head + 2 - 4 * bits[1], head + 4 - 8 * bits[2]]
+    barrier = pltpu.get_barrier_semaphore()
+    for partner in partners:
+        pl.semaphore_signal(barrier, 1, device_id=(dcn, blk, partner), device_id_type=mesh_id)
+    pl.semaphore_wait(barrier, 3)
+    windows = x_ref.shape[0]
+    sources = [x_ref, a1, a2]
+    targets = [r1, r2, r3]
+    copies = [[None] * windows for _ in range(3)]
+
+    def keep_bit(stage, w):
+        if stage > 0 and w == windows - 2:
+            return 1 - bits[stage]
+        return bits[stage]
+
+    def send(stage, w):
+        keep = keep_bit(stage, w)
+        copy = pltpu.make_async_remote_copy(
+            src_ref=sources[stage].at[w, 1 - keep],
+            dst_ref=targets[stage].at[w],
+            send_sem=send_sems.at[stage, w],
+            recv_sem=recv_sems.at[stage, w],
+            device_id=(dcn, blk, partners[stage]),
+            device_id_type=mesh_id,
+        )
+        copy.start()
+        copies[stage][w] = copy
+
+    for w in range(windows):
+        send(0, w)
+    for stage in range(3):
+        for w in range(windows):
+            copies[stage][w].wait_recv()
+            summed = sources[stage][w, keep_bit(stage, w)] + targets[stage][w]
+            if stage < 2:
+                sources[stage + 1][w] = summed
+                send(stage + 1, w)
+            else:
+                o_ref[w] = summed
+    for stage in range(3):
+        for w in range(windows):
+            copies[stage][w].wait_send()
+
+
+def head_reduce(chunks):
+    windows, rest = chunks.shape[0], chunks.shape[4:]
+    f32 = jnp.float32
+    return pl.pallas_call(
+        head_reduce_kernel,
+        out_shape=jax.ShapeDtypeStruct((windows,) + rest, f32),
+        in_specs=[pl.BlockSpec(memory_space=pltpu.VMEM)],
+        out_specs=pl.BlockSpec(memory_space=pltpu.VMEM),
+        scratch_shapes=[
+            pltpu.VMEM((windows, 2, 2) + rest, f32),
+            pltpu.VMEM((windows, 2) + rest, f32),
+            pltpu.VMEM((windows,) + rest, f32),
+            pltpu.VMEM((windows, 2, 2) + rest, f32),
+            pltpu.VMEM((windows, 2) + rest, f32),
+            pltpu.SemaphoreType.DMA((3, windows)),
+            pltpu.SemaphoreType.DMA((3, windows)),
+        ],
+        compiler_params=pltpu.CompilerParams(collective_id=0, has_side_effects=True),
+    )(chunks)
 
 
 def local_grads(q, dout, starts, kwin, value_window, qpos, kpos):
@@ -87,19 +160,9 @@
     parts = lax.axis_size("head")
     piece = rows // parts
     head = lax.axis_index("head")
-    chunks = terms.reshape(WIN + 1, parts, piece, 2 * window_width)
-    order = jnp.array([mirror(c, parts) for c in range(parts)], jnp.int32)
-    chunks = chunks.at[WIN - 1].set(chunks[WIN - 1][order])
-    stride = 1
-    while stride < parts:
-        bit = (head // stride) % 2
-        chunks = chunks.reshape(WIN + 1, -1, 2, piece, 2 * window_width)
-        keep = lax.dynamic_index_in_dim(chunks, bit, axis=2, keepdims=False)
-        send = lax.dynamic_index_in_dim(chunks, 1 - bit, axis=2, keepdims=False)
-        route = [(i, i ^ stride) for i in range(parts)]
-        chunks = keep + lax.ppermute(send, "head", route)
-        stride *= 2
-    reduced = chunks.reshape(WIN + 1, piece, 2 * window_width)
+    chunks = terms.reshape(WIN + 1, 2, 2, 2, piece, 2 * window_width)
+    chunks = jnp.transpose(chunks, (0, 3, 2, 1, 4, 5))
+    reduced = head_reduce(chunks)
     total = reduced[WIN]
     for step in range(1, WIN + 1):
         if step == 1:

time: 102 us -> 86.6 us (0.85); the launches traced: 100 us -> 86.2 us
  Pallas kernels: 0 us -> 23 us
  waiting for transfers between devices: 39.8 us -> 22.8 us
  starting transfers between devices: 28.7 us -> 18.9 us
  local copies, waits for them, and re-layouts: 11 us -> 5.63 us
  matrix products: 11.5 us -> 8.69 us
  other arithmetic: 8.15 us -> 6.27 us
    pallas_call x0 -> x1, Pallas kernels: none -> 23 us  [head_reduce(): pl.pallas_call(head_reduce_kernel, out_shape=jax.ShapeDtypeStruct((window...]
    ppermute x3 -> x0, waiting for transfers between devices: 18.4 us -> none  [body(): chunks = keep + lax.ppermute(send, 'head', route)]
    ppermute x3 -> x0, starting transfers between devices: 9.06 us -> none  [body(): chunks = keep + lax.ppermute(send, 'head', route)]
    add x5 -> x0, other arithmetic: 5.06 us -> none  [the longest x3 2.55 us: body(): chunks = keep + lax.ppermute(send, 'head', route)]
    convert_element_type x0 -> x2, other arithmetic: none -> 2.88 us  [local_grads(): prob_low = prob.astype(jnp.bfloat16)]
    gather x1 -> x0, local copies, waits for them, and re-layouts: 2.41 us -> none  [body(): chunks = chunks.at[WIN - 1].set(chunks[WIN - 1][order])]
    unnamed x27 -> x9, local copies, waits for them, and re-layouts: 3.19 us -> 1.14 us
    squeeze x3 -> x0, local copies, waits for them, and re-layouts: 1.79 us -> none  [body(): send = lax.dynamic_index_in_dim(chunks, 1 - bit, axis=2, keepdims=False)]
  transfers between devices with their start and end apart: 7 -> 4, of which waited for: 6 -> 3; matrix products, arithmetic and copies ran while one was open for 7% -> 5% of each run, Pallas kernels for 0% -> 0%
where the time goes in v3:
time: 86.6 us; the launch traced here: 86.2 us
  Pallas kernels  23 us (27%)
  waiting for transfers between devices  22.8 us (26%)
  starting transfers between devices  18.9 us (22%)
  matrix products  8.69 us (10%)
  other arithmetic  6.27 us (7%)
  local copies, waits for them, and re-layouts  5.63 us (7%)
    pallas_call x1, Pallas kernels, head_reduce(): pl.pallas_call(head_reduce_kernel, out_shape=jax.ShapeDtypeStruct((window...  23 us
    ppermute x2, waiting for transfers between devices, nearest_next(): return lax.ppermute(block, ('dcn', 'blk', 'head'), route)  19.8 us
    ppermute x2, starting transfers between devices, nearest_next(): return lax.ppermute(block, ('dcn', 'blk', 'head'), route)  12.7 us
    ppermute x2, starting transfers between devices, from_behind(): return lax.ppermute(block, axis, route)  6.21 us
    ppermute x2, waiting for transfers between devices, from_behind(): return lax.ppermute(block, axis, route)  3.01 us
    convert_element_type x2, other arithmetic, local_grads(): prob_low = prob.astype(jnp.bfloat16)  2.88 us
    dot_general x2, matrix products, local_grads(): jnp.einsum('ihe,je->hij', dout, value_window, preferred_element_type=jnp....  2.69 us
    dot_general x2, matrix products, local_grads(): jnp.einsum('ihe,je->hij', q, kwin, preferred_element_type=jnp.float32)  2.07 us
  transfers between devices with their start and end apart: 4, of which 3 were waited for; matrix products, arithmetic and copies ran while one was open for 5% of the time, Pallas kernels for 0%

profile of v3, /device:TPU:15, one launch (start us, length us, event | category | flops | bytes accessed | tf_op | source)
XLA Modules:
  0.0 86.2 jit_solution(16228516498787455774)
XLA Ops:
  0.6 0.0 copy-start
  0.6 0.0 copy-start.1
  0.7 0.0 copy-start.2
  0.7 1.0 %pad_maximum_fusion = bf16[2,512,128]{2,1,0:T(8,128)(2,1)S(1)} fusion(bf16[1,512,128]{2,1,0:T(8,128)(2,1)} %bitcast.172, bf16[1,512,128]{2,1,0:T(8,128)(2,1)} %bitcast.174), kind=kLoop, calls=%fused_computation.52 | loop fusion | flops 131072 | bytes 524288 | tf_op jit(solution)/shard_map/stack | solution.py:132
  1.7 5.8 %collective-permute-start.1 = (bf16[2,512,128]{2,1,0:T(8,128)(2,1)S(1)}, bf16[2,512,128]{2,1,0:T(8,128)(2,1)S(1)}, u32[]{:S(2)}, u32[]{:S(2)}) collective-permute-start(bf16[2,512,128]{2,1,0:T(8,128)(2,1)S(1)} %pad_maximum_fusion), channel_id=1, source_target_pairs={{0,14},{1,15},{2,12},{3,13},{4,10},{5,11},{6,8},{7,9},{8,22},{9,23... | collective-permute-start | bytes 786440 | tf_op jit(solution)/shard_map/ppermute | solution.py:30
  7.5 4.0 %collective-permute-start = (bf16[2,512,128]{2,1,0:T(8,128)(2,1)S(1)}, bf16[2,512,128]{2,1,0:T(8,128)(2,1)S(1)}, u32[]{:S(2)}, u32[]{:S(2)}) collective-permute-start(bf16[2,512,128]{2,1,0:T(8,128)(2,1)S(1)} %pad_maximum_fusion), channel_id=1, source_target_pairs={{0,16},{8,24},{16,32},{24,40},{32,48},{40,56},{48,64},{56,72},{64,... | collective-permute-start | bytes 786440 | tf_op jit(solution)/shard_map/ppermute | solution.py:14
  11.5 1.5 %fusion.51 = (bf16[512,1,128]{2,1,0:T(2,128)(2,1)S(1)}, bf16[512,1,128]{2,1,0:T(2,128)(2,1)S(1)}) fusion(bf16[512,2,128]{2,1,0:T(2,128)(2,1)} %param.8), kind=kLoop, calls=%fused_computation.69 | loop fusion | bytes 524288 | tf_op jit(solution)/shard_map/slice | solution.py:150
  13.0 0.1 copy.37
  13.2 0.1 copy.39
  13.3 1.5 %fusion.52 = (bf16[512,1,128]{2,1,0:T(2,128)(2,1)S(1)}, bf16[512,1,128]{2,1,0:T(2,128)(2,1)S(1)}) fusion(bf16[512,2,128]{2,1,0:T(2,128)(2,1)} %param.5), kind=kLoop, calls=%fused_computation.70 | loop fusion | bytes 524288 | tf_op jit(solution)/shard_map/slice | solution.py:149
  14.8 19.8 %collective-permute-done.1 = bf16[2,512,128]{2,1,0:T(8,128)(2,1)S(1)} collective-permute-done((bf16[2,512,128]{2,1,0:T(8,128)(2,1)S(1)}, bf16[2,512,128]{2,1,0:T(8,128)(2,1)S(1)}, u32[]{:S(2)}, u32[]{:S(2)}) %collective-permute-start.1) | collective-permute-done | bytes 262176 | tf_op jit(solution)/shard_map/ppermute | solution.py:30
  34.6 0.4 collective-permute-done
  35.0 0.0 copy-done
  35.0 0.0 copy-done.1
  35.0 0.1 maximum_maximum_fusion
  35.1 0.0 copy-done.2
  35.1 0.8 select_reduce_fusion.3
  35.9 1.2 %select_reduce_fusion.2 = (f32[512]{0:T(512)S(1)}, f32[512]{0:T(512)S(1)}, f32[1,512,1536]{1,2,0:T(8,128)S(1)}) fusion(f32[1,512,1536]{1,2,0:T(8,128)S(1)} %get-tuple-element.22, f32[512]{0:T(512)S(1)} %get-tuple-element.21, s32[512]{0:T(512)S(1)} %iota_add_fusion.1, s32[512]{0:T(512)S(1)} %copy-done.2, s32[1536]{0:T(1024)S(1)} %iota_add_fusion, ...), kind=kOutput, calls=%fused_computation.16 | convolution fusion | flops 208403456 | bytes 6965248 | tf_op jit(solution)/shard_map/ihe,je->hij/dot_general | solution.py:107
  37.2 1.7 %fusion.12 = (bf16[1,512,1536]{1,2,0:T(8,128)(2,1)S(1)}, f32[512]{0:T(512)S(1)}) fusion(f32[1,512,1536]{1,2,0:T(8,128)S(1)} %get-tuple-element.22, f32[512]{0:T(512)S(1)} %log_add_fusion.1, s32[512]{0:T(512)S(1)} %iota_add_fusion.1, s32[512]{0:T(512)S(1)} %copy-done.2, s32[1536]{0:T(1024)S(1)} %iota_add_fusion, f32[1,512,1536]{1,2,0:T(8,128)S(1)} %get-tuple-element.23, ...), kind=kLoop, calls=%fused_computation.25 | loop fusion | flops 7077376 | bytes 7880704 | tf_op jit(solution)/shard_map/convert_element_type | solution.py:112
  38.8 0.4 fusion.37
  39.2 1.3 %fusion.11 = bf16[512,1536]{0,1:T(8,128)(2,1)S(1)} fusion(f32[1,512,1536]{1,2,0:T(8,128)S(1)} %get-tuple-element.22, f32[512]{0:T(512)S(1)} %fusion.37, f32[512]{0:T(512)S(1)} %log_add_fusion.1, bf16[2,1536,128]{2,1,0:T(8,128)(2,1)S(1)} %maximum_maximum_fusion, bf16[512,1,128]{0,2,1:T(8,128)(2,1)S(1)} %copy.37, s32[512]{0:T(512)S(1)} %iota_add_fusion.1, ...), kind=kOutput, calls=%fused_computation.22 | convolution fusion | flops 207618048 | bytes 5259264 | tf_op jit(solution)/shard_map/ihe,je->hij/dot_general | solution.py:117
  40.6 0.4 fusion.44
  41.0 0.6 convolution_multiply_fusion.3
  41.6 1.2 %fusion.13 = bf16[1,512,1536]{1,2,0:T(8,128)(2,1)S(1)} fusion(f32[1,512,1536]{1,2,0:T(8,128)S(1)} %get-tuple-element.23, f32[512]{0:T(512)S(1)} %log_add_fusion, s32[512]{0:T(512)S(1)} %iota_add_fusion.1, s32[512]{0:T(512)S(1)} %copy-done.2, s32[1536]{0:T(1024)S(1)} %iota_add_fusion), kind=kLoop, calls=%fused_computation.26 | loop fusion | flops 4718592 | bytes 4730880 | tf_op jit(solution)/shard_map/convert_element_type | solution.py:112
  42.8 0.4 fusion.40
  43.2 1.3 %fusion.10 = bf16[512,1536]{0,1:T(8,128)(2,1)S(1)} fusion(f32[1,512,1536]{1,2,0:T(8,128)S(1)} %get-tuple-element.23, f32[512]{0:T(512)S(1)} %fusion.40, f32[512]{0:T(512)S(1)} %log_add_fusion, bf16[2,1536,128]{2,1,0:T(8,128)(2,1)S(1)} %maximum_maximum_fusion, bf16[512,1,128]{0,2,1:T(8,128)(2,1)S(1)} %copy.39, s32[512]{0:T(512)S(1)} %iota_add_fusion.1, ...), kind=kOutput, calls=%fused_computation.21 | convolution fusion | flops 207618048 | bytes 5259264 | tf_op jit(solution)/shard_map/ihe,je->hij/dot_general | solution.py:117
  44.6 0.4 fusion.43
  45.0 0.6 convolution_multiply_fusion.2
  45.6 0.6 fusion.21
  46.2 0.6 fusion.19
  46.7 1.4 %fusion.14.x_ref = f32[3,2,2,2,64,256]{5,4,3,2,1,0:T(8,128)} fusion(f32[3,2,2,2,64,128]{5,4,1,2,3,0:T(8,128)S(1)} %fusion.21, f32[3,2,2,2,64,128]{5,4,1,2,3,0:T(8,128)S(1)} %fusion.19, f32[3,2,2,2,64,128]{5,4,3,2,1,0:T(8,128)S(1)} %bitcast.171, f32[3,2,2,2,64,128]{5,4,3,2,1,0:T(8,128)S(1)} %bitcast.170), kind=kLoop, calls=%fused_computation.28 | loop fusion | flops 1179648 | bytes 4718592 | tf_op jit(solution)/shard_map/transpose | solution.py:164
  48.1 23.0 %shard_map.76 = f32[3,64,256]{2,1,0:T(8,128)} custom-call(f32[3,2,2,2,64,256]{5,4,3,2,1,0:T(8,128)} %fusion.14.x_ref), custom_call_target="tpu_custom_call" | custom-call | tf_op jit(solution)/shard_map/pallas_call | solution.py:86
  71.1 0.9 %slice_bitcast_fusion.11 = (f32[64,256]{1,0:T(8,128)S(1)}, f32[64,256]{1,0:T(8,128)S(1)}) fusion(f32[3,64,256]{2,1,0:T(8,128)} %shard_map.76), kind=kLoop, calls=%fused_computation.64 | loop fusion | bytes 262144 | tf_op jit(solution)/shard_map/squeeze | solution.py:169
  72.0 6.9 %collective-permute-start.2 = (f32[64,256]{1,0:T(8,128)S(1)}, f32[64,256]{1,0:T(8,128)S(1)}, u32[]{:S(2)}, u32[]{:S(2)}) collective-permute-start(f32[64,256]{1,0:T(8,128)S(1)} %get-tuple-element.15), channel_id=1, source_target_pairs={{14,0},{15,1},{12,2},{13,3},{10,4},{11,5},{8,6},{9,7},{22,8},{23,9... | collective-permute-start | bytes 196616 | tf_op jit(solution)/shard_map/ppermute | solution.py:30
  78.9 2.2 %collective-permute-start.3 = (f32[64,256]{1,0:T(8,128)S(1)}, f32[64,256]{1,0:T(8,128)S(1)}, u32[]{:S(2)}, u32[]{:S(2)}) collective-permute-start(f32[64,256]{1,0:T(8,128)S(1)} %get-tuple-element.16), channel_id=1, source_target_pairs={{16,0},{24,8},{32,16},{40,24},{48,32},{56,40},{64,48},{72,56},{80,... | collective-permute-start | bytes 196616 | tf_op jit(solution)/shard_map/ppermute | solution.py:14
  81.2 0.9 %copy.25 = bf16[512,2,128]{2,1,0:T(2,128)(2,1)} copy(bf16[512,2,128]{0,2,1:T(8,128)(2,1)S(1)} %pad_maximum_fusion.1) | data formatting | bytes 524288
  82.0 0.0 collective-permute-done.2
  82.0 2.6 %collective-permute-done.3 = f32[64,256]{1,0:T(8,128)S(1)} collective-permute-done((f32[64,256]{1,0:T(8,128)S(1)}, f32[64,256]{1,0:T(8,128)S(1)}, u32[]{:S(2)}, u32[]{:S(2)}) %collective-permute-start.3) | collective-permute-done | bytes 65568 | tf_op jit(solution)/shard_map/ppermute | solution.py:14
  84.7 0.9 fusion.50
  85.5 0.6 fusion.53
  (5 shorter events, 0.1 us)
Async XLA Ops:
  0.6 34.4 %copy-start = (bf16[512,128]{1,0:T(8,128)(2,1)S(1)}, bf16[512,128]{1,0:T(8,128)(2,1)}, u32[]{:S(2)}) copy-start(bf16[512,128]{1,0:T(8,128)(2,1)} %param.7) | copy-start | bytes 393220
  0.6 34.4 %copy-start.1 = (bf16[512,128]{1,0:T(8,128)(2,1)S(1)}, bf16[512,128]{1,0:T(8,128)(2,1)}, u32[]{:S(2)}) copy-start(bf16[512,128]{1,0:T(8,128)(2,1)} %param.6) | copy-start | bytes 393220
  0.7 34.4 %copy-start.2 = (s32[512]{0:T(512)S(1)}, s32[512]{0:T(512)}, u32[]{:S(2)}) copy-start(s32[512]{0:T(512)} %param.9) | copy-start | bytes 6148
  1.7 32.9 %collective-permute-start.1 = (bf16[2,512,128]{2,1,0:T(8,128)(2,1)S(1)}, bf16[2,512,128]{2,1,0:T(8,128)(2,1)S(1)}, u32[]{:S(2)}, u32[]{:S(2)}) collective-permute-start(bf16[2,512,128]{2,1,0:T(8,128)(2,1)S(1)} %pad_maximum_fusion), channel_id=1, source_target_pairs={{0,14},{1,15},{2,12},{3,13},{4,10},{5,11},{6,8},{7,9},{8,22},{9,23... | collective-permute-start | bytes 786440 | tf_op jit(solution)/shard_map/ppermute | solution.py:30
  7.5 27.5 %collective-permute-start = (bf16[2,512,128]{2,1,0:T(8,128)(2,1)S(1)}, bf16[2,512,128]{2,1,0:T(8,128)(2,1)S(1)}, u32[]{:S(2)}, u32[]{:S(2)}) collective-permute-start(bf16[2,512,128]{2,1,0:T(8,128)(2,1)S(1)} %pad_maximum_fusion), channel_id=1, source_target_pairs={{0,16},{8,24},{16,32},{24,40},{32,48},{40,56},{48,64},{56,72},{64,... | collective-permute-start | bytes 786440 | tf_op jit(solution)/shard_map/ppermute | solution.py:14
  72.0 10.1 %collective-permute-start.2 = (f32[64,256]{1,0:T(8,128)S(1)}, f32[64,256]{1,0:T(8,128)S(1)}, u32[]{:S(2)}, u32[]{:S(2)}) collective-permute-start(f32[64,256]{1,0:T(8,128)S(1)} %get-tuple-element.15), channel_id=1, source_target_pairs={{14,0},{15,1},{12,2},{13,3},{10,4},{11,5},{8,6},{9,7},{22,8},{23,9... | collective-permute-start | bytes 196616 | tf_op jit(solution)/shard_map/ppermute | solution.py:30
  78.9 5.8 %collective-permute-start.3 = (f32[64,256]{1,0:T(8,128)S(1)}, f32[64,256]{1,0:T(8,128)S(1)}, u32[]{:S(2)}, u32[]{:S(2)}) collective-permute-start(f32[64,256]{1,0:T(8,128)S(1)} %get-tuple-element.16), channel_id=1, source_target_pairs={{16,0},{24,8},{32,16},{40,24},{48,32},{56,40},{64,48},{72,56},{80,... | collective-permute-start | bytes 196616 | tf_op jit(solution)/shard_map/ppermute | solution.py:14

commit v4 on v3

--- a/solution.py
+++ b/solution.py
@@ -30,24 +30,51 @@
     return lax.ppermute(block, ("dcn", "blk", "head"), route)
 
 
-def head_reduce_kernel(x_ref, o_ref, r1, r2, r3, a1, a2, send_sems, recv_sems):
+def grad_reduce_kernel(x_ref, k_out, v_out, r1, r2, r3, a1, a2, a3, total, back, sends, recvs):
     mesh_id = pl.DeviceIdType.MESH
     dcn = lax.axis_index("dcn")
     blk = lax.axis_index("blk")
     head = lax.axis_index("head")
+    per_dcn = lax.axis_size("blk")
+    blocks = lax.axis_size("dcn") * per_dcn
+    parts = lax.axis_size("head")
+    block = dcn * per_dcn + blk
     bits = [head % 2, (head // 2) % 2, (head // 4) % 2]
     partners = [head + 1 - 2 * bits[0], head + 2 - 4 * bits[1], head + 4 - 8 * bits[2]]
+    flipped = mirror(head, parts)
+
+    def device(b, h):
+        return (b // per_dcn, b % per_dcn, h)
+
+    back_heads = [flipped if w == WIN - 1 else head for w in range(WIN)]
+    sends_back = [block >= WIN - w for w in range(WIN)]
+    gets_back = [block + WIN - w < blocks for w in range(WIN)]
     barrier = pltpu.get_barrier_semaphore()
     for partner in partners:
         pl.semaphore_signal(barrier, 1, device_id=(dcn, blk, partner), device_id_type=mesh_id)
-    pl.semaphore_wait(barrier, 3)
+    for w in range(WIN):
+        distance = WIN - w
+
+        @pl.when(sends_back[w])
+        def _():
+            pl.semaphore_signal(barrier, 1, device_id=device(block - distance, back_heads[w]), device_id_type=mesh_id)
+
+        @pl.when(gets_back[w])
+        def _():
+            pl.semaphore_signal(barrier, 1, device_id=device(block + distance, back_heads[w]), device_id_type=mesh_id)
+
+    peers = len(partners)
+    for w in range(WIN):
+        peers = peers + sends_back[w].astype(jnp.int32) + gets_back[w].astype(jnp.int32)
+    pl.semaphore_wait(barrier, peers)
+
     windows = x_ref.shape[0]
     sources = [x_ref, a1, a2]
     targets = [r1, r2, r3]
     copies = [[None] * windows for _ in range(3)]
 
     def keep_bit(stage, w):
-        if stage > 0 and w == windows - 2:
+        if stage > 0 and w == WIN - 1:
             return 1 - bits[stage]
         return bits[stage]
 
@@ -56,13 +83,23 @@
         copy = pltpu.make_async_remote_copy(
             src_ref=sources[stage].at[w, 1 - keep],
             dst_ref=targets[stage].at[w],
-            send_sem=send_sems.at[stage, w],
-            recv_sem=recv_sems.at[stage, w],
+            send_sem=sends.at[stage, w],
+            recv_sem=recvs.at[stage, w],
             device_id=(dcn, blk, partners[stage]),
             device_id_type=mesh_id,
         )
         copy.start()
         copies[stage][w] = copy
+
+    def back_copy(w, b):
+        return pltpu.make_async_remote_copy(
+            src_ref=a3.at[w],
+            dst_ref=back.at[w],
+            send_sem=sends.at[3, w],
+            recv_sem=recvs.at[3, w],
+            device_id=device(b, back_heads[w]),
+            device_id_type=mesh_id,
+        )
 
     for w in range(windows):
         send(0, w)
@@ -73,29 +110,55 @@
             if stage < 2:
                 sources[stage + 1][w] = summed
                 send(stage + 1, w)
+            elif w < WIN:
+                a3[w] = summed
+
+                @pl.when(sends_back[w])
+                def _():
+                    back_copy(w, block - (WIN - w)).start()
+
             else:
-                o_ref[w] = summed
+                total[...] = summed
+    for w in range(WIN - 1, -1, -1):
+
+        @pl.when(gets_back[w])
+        def _():
+            back_copy(w, block + WIN - w).wait_recv()
+            total[...] = total[...] + back[w]
+
+    width = k_out.shape[1]
+    k_out[...] = total[:, :width].astype(k_out.dtype)
+    v_out[...] = total[:, width:].astype(v_out.dtype)
     for stage in range(3):
         for w in range(windows):
             copies[stage][w].wait_send()
-
-
-def head_reduce(chunks):
+    for w in range(WIN):
+
+        @pl.when(sends_back[w])
+        def _():
+            back_copy(w, block - (WIN - w)).wait_send()
+
+
+def grad_reduce(chunks, width, dtype):
     windows, rest = chunks.shape[0], chunks.shape[4:]
     f32 = jnp.float32
+    out = jax.ShapeDtypeStruct((rest[0], width), dtype)
     return pl.pallas_call(
-        head_reduce_kernel,
-        out_shape=jax.ShapeDtypeStruct((windows,) + rest, f32),
+        grad_reduce_kernel,
+        out_shape=(out, out),
         in_specs=[pl.BlockSpec(memory_space=pltpu.VMEM)],
-        out_specs=pl.BlockSpec(memory_space=pltpu.VMEM),
+        out_specs=(pl.BlockSpec(memory_space=pltpu.VMEM), pl.BlockSpec(memory_space=pltpu.VMEM)),
         scratch_shapes=[
             pltpu.VMEM((windows, 2, 2) + rest, f32),
             pltpu.VMEM((windows, 2) + rest, f32),
             pltpu.VMEM((windows,) + rest, f32),
             pltpu.VMEM((windows, 2, 2) + rest, f32),
             pltpu.VMEM((windows, 2) + rest, f32),
-            pltpu.SemaphoreType.DMA((3, windows)),
-            pltpu.SemaphoreType.DMA((3, windows)),
+            pltpu.VMEM((WIN,) + rest, f32),
+            pltpu.VMEM(rest, f32),
+            pltpu.VMEM((WIN,) + rest, f32),
+            pltpu.SemaphoreType.DMA((4, windows)),
+            pltpu.SemaphoreType.DMA((4, windows)),
         ],
         compiler_params=pltpu.CompilerParams(collective_id=0, has_side_effects=True),
     )(chunks)
@@ -162,15 +225,7 @@
     head = lax.axis_index("head")
     chunks = terms.reshape(WIN + 1, 2, 2, 2, piece, 2 * window_width)
     chunks = jnp.transpose(chunks, (0, 3, 2, 1, 4, 5))
-    reduced = head_reduce(chunks)
-    total = reduced[WIN]
-    for step in range(1, WIN + 1):
-        if step == 1:
-            total = total + nearest_next(reduced[WIN - step], back=True)
-        else:
-            total = total + from_behind(reduced[WIN - step], ("dcn", "blk"), -step)
-    k_grad = total[:, :window_width].astype(jnp.bfloat16)
-    v_grad = total[:, window_width:].astype(jnp.bfloat16)
+    k_grad, v_grad = grad_reduce(chunks, window_width, jnp.bfloat16)
     return (q_grad, k_grad, v_grad)
 
 

time: 86.6 us -> 82 us (0.947)
  the two profiles are of different devices: /device:TPU:15 before, /device:TPU:54 now
where the time goes in v4:
time: 82 us; the launch traced here: 81.6 us
  Pallas kernels  30.8 us (38%)
  waiting for transfers between devices  20.1 us (25%)
  starting transfers between devices  8.89 us (11%)
  matrix products  8.69 us (11%)
  local copies, waits for them, and re-layouts  6.82 us (8%)
  other arithmetic  5.43 us (7%)
  between operations  0.83 us (1%)
    pallas_call x1, Pallas kernels, grad_reduce(): pl.pallas_call(grad_reduce_kernel, out_shape=(out, out), in_specs=[pl.Blo...  30.8 us
    ppermute x1, waiting for transfers between devices, from_behind(): return lax.ppermute(block, axis, route)  18.9 us
    ppermute x1, starting transfers between devices, nearest_next(): return lax.ppermute(block, ('dcn', 'blk', 'head'), route)  4.61 us
    ppermute x1, starting transfers between devices, from_behind(): return lax.ppermute(block, axis, route)  4.28 us
    unnamed x11, local copies, waits for them, and re-layouts  3.79 us
    convert_element_type x2, other arithmetic, local_grads(): prob_low = prob.astype(jnp.bfloat16)  2.88 us
    dot_general x2, matrix products, local_grads(): jnp.einsum('ihe,je->hij', dout, value_window, preferred_element_type=jnp....  2.69 us
    dot_general x2, matrix products, local_grads(): jnp.einsum('ihe,je->hij', q, kwin, preferred_element_type=jnp.float32)  2.07 us
  transfers between devices with their start and end apart: 2, of which 2 were waited for; matrix products, arithmetic and copies ran while one was open for 4% of the time, Pallas kernels for 0%

profile of v4, /device:TPU:54, one launch (start us, length us, event | category | flops | bytes accessed | tf_op | source)
XLA Modules:
  0.0 81.6 jit_solution(7431069875977005683)
XLA Ops:
  0.6 0.0 copy-start
  0.6 0.0 copy-start.1
  0.7 0.0 copy-start.2
  0.7 1.0 %pad_maximum_fusion = bf16[2,512,128]{2,1,0:T(8,128)(2,1)S(1)} fusion(bf16[1,512,128]{2,1,0:T(8,128)(2,1)} %bitcast.162, bf16[1,512,128]{2,1,0:T(8,128)(2,1)} %bitcast.164), kind=kLoop, calls=%fused_computation.52 | loop fusion | flops 131072 | bytes 524288 | tf_op jit(solution)/shard_map/stack | solution.py:195
  1.7 4.6 %collective-permute-start.1 = (bf16[2,512,128]{2,1,0:T(8,128)(2,1)S(1)}, bf16[2,512,128]{2,1,0:T(8,128)(2,1)S(1)}, u32[]{:S(2)}, u32[]{:S(2)}) collective-permute-start(bf16[2,512,128]{2,1,0:T(8,128)(2,1)S(1)} %pad_maximum_fusion), channel_id=1, source_target_pairs={{0,14},{1,15},{2,12},{3,13},{4,10},{5,11},{6,8},{7,9},{8,22},{9,23... | collective-permute-start | bytes 786440 | tf_op jit(solution)/shard_map/ppermute | solution.py:30
  6.3 4.3 %collective-permute-start = (bf16[2,512,128]{2,1,0:T(8,128)(2,1)S(1)}, bf16[2,512,128]{2,1,0:T(8,128)(2,1)S(1)}, u32[]{:S(2)}, u32[]{:S(2)}) collective-permute-start(bf16[2,512,128]{2,1,0:T(8,128)(2,1)S(1)} %pad_maximum_fusion), channel_id=1, source_target_pairs={{0,16},{8,24},{16,32},{24,40},{32,48},{40,56},{48,64},{56,72},{64,... | collective-permute-start | bytes 786440 | tf_op jit(solution)/shard_map/ppermute | solution.py:14
  10.6 1.5 %fusion.49 = (bf16[512,1,128]{2,1,0:T(2,128)(2,1)S(1)}, bf16[512,1,128]{2,1,0:T(2,128)(2,1)S(1)}) fusion(bf16[512,2,128]{2,1,0:T(2,128)(2,1)} %param.8), kind=kLoop, calls=%fused_computation.64 | loop fusion | bytes 524288 | tf_op jit(solution)/shard_map/slice | solution.py:213
  12.2 0.1 copy.37
  12.3 0.1 copy.39
  12.5 1.5 %fusion.50 = (bf16[512,1,128]{2,1,0:T(2,128)(2,1)S(1)}, bf16[512,1,128]{2,1,0:T(2,128)(2,1)S(1)}) fusion(bf16[512,2,128]{2,1,0:T(2,128)(2,1)} %param.5), kind=kLoop, calls=%fused_computation.65 | loop fusion | bytes 524288 | tf_op jit(solution)/shard_map/slice | solution.py:212
  14.0 1.2 %collective-permute-done.1 = bf16[2,512,128]{2,1,0:T(8,128)(2,1)S(1)} collective-permute-done((bf16[2,512,128]{2,1,0:T(8,128)(2,1)S(1)}, bf16[2,512,128]{2,1,0:T(8,128)(2,1)S(1)}, u32[]{:S(2)}, u32[]{:S(2)}) %collective-permute-start.1) | collective-permute-done | bytes 262176 | tf_op jit(solution)/shard_map/ppermute | solution.py:30
  15.1 18.9 %collective-permute-done = bf16[2,512,128]{2,1,0:T(8,128)(2,1)S(1)} collective-permute-done((bf16[2,512,128]{2,1,0:T(8,128)(2,1)S(1)}, bf16[2,512,128]{2,1,0:T(8,128)(2,1)S(1)}, u32[]{:S(2)}, u32[]{:S(2)}) %collective-permute-start) | collective-permute-done | bytes 262176 | tf_op jit(solution)/shard_map/ppermute | solution.py:14
  34.1 0.0 copy-done
  34.1 0.0 copy-done.1
  34.1 0.1 maximum_maximum_fusion
  34.1 0.0 copy-done.2
  34.1 0.8 %select_reduce_fusion.3 = (f32[512]{0:T(512)S(1)}, f32[1,512,1536]{1,2,0:T(8,128)S(1)}) fusion(s32[512]{0:T(512)S(1)} %iota_add_fusion.1, s32[512]{0:T(512)S(1)} %copy-done.2, s32[1536]{0:T(1024)S(1)} %iota_add_fusion, bf16[512,1,128]{2,1,0:T(2,128)(2,1)S(1)} %get-tuple-element.17, bf16[2,1536,128]{2,1,0:T(8,128)(2,1)S(1)} %maximum_maximum_fusion), kind=kOutput, calls=%fused_computation.17 | convolution fusion | flops 206044672 | bytes 3815424 | tf_op jit(solution)/shard_map/ihe,je->hij/dot_general | solution.py:170
  35.0 1.3 %select_reduce_fusion.2 = (f32[512]{0:T(512)S(1)}, f32[512]{0:T(512)S(1)}, f32[1,512,1536]{1,2,0:T(8,128)S(1)}) fusion(f32[1,512,1536]{1,2,0:T(8,128)S(1)} %get-tuple-element.22, f32[512]{0:T(512)S(1)} %get-tuple-element.21, s32[512]{0:T(512)S(1)} %iota_add_fusion.1, s32[512]{0:T(512)S(1)} %copy-done.2, s32[1536]{0:T(1024)S(1)} %iota_add_fusion, ...), kind=kOutput, calls=%fused_computation.16 | convolution fusion | flops 208403456 | bytes 6965248 | tf_op jit(solution)/shard_map/ihe,je->hij/dot_general | solution.py:170
  36.2 1.7 %fusion.12 = (bf16[1,512,1536]{1,2,0:T(8,128)(2,1)S(1)}, f32[512]{0:T(512)S(1)}) fusion(f32[1,512,1536]{1,2,0:T(8,128)S(1)} %get-tuple-element.22, f32[512]{0:T(512)S(1)} %log_add_fusion.1, s32[512]{0:T(512)S(1)} %iota_add_fusion.1, s32[512]{0:T(512)S(1)} %copy-done.2, s32[1536]{0:T(1024)S(1)} %iota_add_fusion, f32[1,512,1536]{1,2,0:T(8,128)S(1)} %get-tuple-element.23, ...), kind=kLoop, calls=%fused_computation.25 | loop fusion | flops 7077376 | bytes 7880704 | tf_op jit(solution)/shard_map/convert_element_type | solution.py:175
  37.9 0.4 fusion.37
  38.3 1.3 %fusion.11 = bf16[512,1536]{0,1:T(8,128)(2,1)S(1)} fusion(f32[1,512,1536]{1,2,0:T(8,128)S(1)} %get-tuple-element.22, f32[512]{0:T(512)S(1)} %fusion.37, f32[512]{0:T(512)S(1)} %log_add_fusion.1, bf16[2,1536,128]{2,1,0:T(8,128)(2,1)S(1)} %maximum_maximum_fusion, bf16[512,1,128]{0,2,1:T(8,128)(2,1)S(1)} %copy.37, s32[512]{0:T(512)S(1)} %iota_add_fusion.1, ...), kind=kOutput, calls=%fused_computation.22 | convolution fusion | flops 207618048 | bytes 5259264 | tf_op jit(solution)/shard_map/ihe,je->hij/dot_general | solution.py:180
  39.7 0.4 fusion.44
  40.1 0.6 convolution_multiply_fusion.3
  40.7 1.2 %fusion.13 = bf16[1,512,1536]{1,2,0:T(8,128)(2,1)S(1)} fusion(f32[1,512,1536]{1,2,0:T(8,128)S(1)} %get-tuple-element.23, f32[512]{0:T(512)S(1)} %log_add_fusion, s32[512]{0:T(512)S(1)} %iota_add_fusion.1, s32[512]{0:T(512)S(1)} %copy-done.2, s32[1536]{0:T(1024)S(1)} %iota_add_fusion), kind=kLoop, calls=%fused_computation.26 | loop fusion | flops 4718592 | bytes 4730880 | tf_op jit(solution)/shard_map/convert_element_type | solution.py:175
  41.9 0.4 fusion.40
  42.3 1.3 %fusion.10 = bf16[512,1536]{0,1:T(8,128)(2,1)S(1)} fusion(f32[1,512,1536]{1,2,0:T(8,128)S(1)} %get-tuple-element.23, f32[512]{0:T(512)S(1)} %fusion.40, f32[512]{0:T(512)S(1)} %log_add_fusion, bf16[2,1536,128]{2,1,0:T(8,128)(2,1)S(1)} %maximum_maximum_fusion, bf16[512,1,128]{0,2,1:T(8,128)(2,1)S(1)} %copy.39, s32[512]{0:T(512)S(1)} %iota_add_fusion.1, ...), kind=kOutput, calls=%fused_computation.21 | convolution fusion | flops 207618048 | bytes 5259264 | tf_op jit(solution)/shard_map/ihe,je->hij/dot_general | solution.py:180
  43.7 0.4 fusion.43
  44.1 0.6 convolution_multiply_fusion.2
  44.7 0.6 fusion.21
  45.2 0.6 fusion.19
  45.8 1.4 %fusion.14.x_ref = f32[3,2,2,2,64,256]{5,4,3,2,1,0:T(8,128)} fusion(f32[3,2,2,2,64,128]{5,4,1,2,3,0:T(8,128)S(1)} %fusion.21, f32[3,2,2,2,64,128]{5,4,1,2,3,0:T(8,128)S(1)} %fusion.19, f32[3,2,2,2,64,128]{5,4,3,2,1,0:T(8,128)S(1)} %bitcast.161, f32[3,2,2,2,64,128]{5,4,3,2,1,0:T(8,128)S(1)} %bitcast.160), kind=kLoop, calls=%fused_computation.28 | loop fusion | flops 1179648 | bytes 4718592 | tf_op jit(solution)/shard_map/transpose | solution.py:227
  47.2 30.8 %shard_map.76 = (bf16[64,128]{1,0:T(8,128)(2,1)}, bf16[64,128]{1,0:T(8,128)(2,1)}) custom-call(f32[3,2,2,2,64,256]{5,4,3,2,1,0:T(8,128)} %fusion.14.x_ref), custom_call_target="tpu_custom_call" | custom-call | tf_op jit(solution)/shard_map/pallas_call | solution.py:146
  78.1 0.9 %copy.25 = bf16[512,2,128]{2,1,0:T(2,128)(2,1)} copy(bf16[512,2,128]{0,2,1:T(8,128)(2,1)S(1)} %pad_maximum_fusion.1) | data formatting | bytes 524288
  78.9 1.3 %copy.60 = bf16[64,128]{1,0:T(8,128)(2,1)} copy(bf16[64,128]{1,0:T(8,128)(2,1)} %get-tuple-element.28) | data formatting | bytes 32768
  80.3 1.3 %copy.61 = bf16[64,128]{1,0:T(8,128)(2,1)} copy(bf16[64,128]{1,0:T(8,128)(2,1)} %get-tuple-element.29) | data formatting | bytes 32768
  (5 shorter events, 0.1 us)
Async XLA Ops:
  0.6 33.4 %copy-start = (bf16[512,128]{1,0:T(8,128)(2,1)S(1)}, bf16[512,128]{1,0:T(8,128)(2,1)}, u32[]{:S(2)}) copy-start(bf16[512,128]{1,0:T(8,128)(2,1)} %param.7) | copy-start | bytes 393220
  0.6 33.4 %copy-start.1 = (bf16[512,128]{1,0:T(8,128)(2,1)S(1)}, bf16[512,128]{1,0:T(8,128)(2,1)}, u32[]{:S(2)}) copy-start(bf16[512,128]{1,0:T(8,128)(2,1)} %param.6) | copy-start | bytes 393220
  0.7 33.5 %copy-start.2 = (s32[512]{0:T(512)S(1)}, s32[512]{0:T(512)}, u32[]{:S(2)}) copy-start(s32[512]{0:T(512)} %param.9) | copy-start | bytes 6148
  1.7 13.4 %collective-permute-start.1 = (bf16[2,512,128]{2,1,0:T(8,128)(2,1)S(1)}, bf16[2,512,128]{2,1,0:T(8,128)(2,1)S(1)}, u32[]{:S(2)}, u32[]{:S(2)}) collective-permute-start(bf16[2,512,128]{2,1,0:T(8,128)(2,1)S(1)} %pad_maximum_fusion), channel_id=1, source_target_pairs={{0,14},{1,15},{2,12},{3,13},{4,10},{5,11},{6,8},{7,9},{8,22},{9,23... | collective-permute-start | bytes 786440 | tf_op jit(solution)/shard_map/ppermute | solution.py:30
  6.3 27.7 %collective-permute-start = (bf16[2,512,128]{2,1,0:T(8,128)(2,1)S(1)}, bf16[2,512,128]{2,1,0:T(8,128)(2,1)S(1)}, u32[]{:S(2)}, u32[]{:S(2)}) collective-permute-start(bf16[2,512,128]{2,1,0:T(8,128)(2,1)S(1)} %pad_maximum_fusion), channel_id=1, source_target_pairs={{0,16},{8,24},{16,32},{24,40},{32,48},{40,56},{48,64},{56,72},{64,... | collective-permute-start | bytes 786440 | tf_op jit(solution)/shard_map/ppermute | solution.py:14

commit v5 on v4

--- a/solution.py
+++ b/solution.py
@@ -205,21 +205,7 @@
     first_position = position * rows
     qpos = first_position + jnp.arange(rows, dtype=jnp.int32)
     kpos = first_position - WIN * rows + jnp.arange(window_span, dtype=jnp.int32)
-    grad_list = []
-    terms = jnp.zeros((window_span, 2 * window_width), jnp.float32)
-    for single in range(local_heads):
-        head_dq, head_terms = local_grads(
-            queries[:, single : single + 1],
-            out_grad[:, single : single + 1],
-            doc_start,
-            window[0],
-            window[1],
-            qpos,
-            kpos,
-        )
-        grad_list.append(head_dq)
-        terms = terms + head_terms
-    q_grad = jnp.concatenate(grad_list, axis=1)
+    q_grad, terms = local_grads(queries, out_grad, doc_start, window[0], window[1], qpos, kpos)
     parts = lax.axis_size("head")
     piece = rows // parts
     head = lax.axis_index("head")

time: 82 us -> 82.3 us (level)
    slice x2 -> x0, local copies, waits for them, and re-layouts: 3.03 us -> none  [the longest x1 1.54 us: body(): out_grad[:, single:single + 1]]
    convert_element_type x2 -> x0, other arithmetic: 2.88 us -> none  [local_grads(): prob_low = prob.astype(jnp.bfloat16)]
    unnamed x11 -> x5, local copies, waits for them, and re-layouts: 3.79 us -> 5.75 us
    reduce_sum x0 -> x1, other arithmetic: none -> 1.44 us  [local_grads(): lse = top + jnp.log(jnp.sum(expo, axis=-1, keepdims=True))]
    transpose x1 -> x0, other arithmetic: 1.41 us -> none  [body(): chunks = jnp.transpose(chunks, (0, 3, 2, 1, 4, 5))]
    and x0 -> x1, other arithmetic: none -> 1.36 us  [local_grads(): (kpos[None, :] >= starts[:, None]) & (kpos[None, :] <= qpos[:, None])]
    reshape x0 -> x1, local copies, waits for them, and re-layouts: none -> 1.29 us  [body(): chunks = terms.reshape(WIN + 1, 2, 2, 2, piece, 2 * window_width)]
    dot_general x2 -> x1, matrix products: 0.84 us -> 1.82 us  [local_grads(): jnp.einsum('hij,je->ihe', prob_low, value_window, preferred_element_type=...]
where the time goes in v5:
time: 82.3 us; the launch traced here: 81.9 us
  Pallas kernels  30.8 us (37%)
  waiting for transfers between devices  19.8 us (24%)
  matrix products  9.14 us (11%)
  starting transfers between devices  8.89 us (11%)
  local copies, waits for them, and re-layouts  7.5 us (9%)
  other arithmetic  4.94 us (6%)
    pallas_call x1, Pallas kernels, grad_reduce(): pl.pallas_call(grad_reduce_kernel, out_shape=(out, out), in_specs=[pl.Blo...  30.8 us
    ppermute x1, waiting for transfers between devices, from_behind(): return lax.ppermute(block, axis, route)  18.9 us
    unnamed x5, local copies, waits for them, and re-layouts  5.75 us
    ppermute x1, starting transfers between devices, nearest_next(): return lax.ppermute(block, ('dcn', 'blk', 'head'), route)  4.61 us
    ppermute x1, starting transfers between devices, from_behind(): return lax.ppermute(block, axis, route)  4.28 us
    dot_general x1, matrix products, local_grads(): jnp.einsum('ihe,je->hij', dout, value_window, preferred_element_type=jnp....  2.35 us
    dot_general x1, matrix products, local_grads(): jnp.einsum('hij,ihe->je', prob_low, dout, preferred_element_type=jnp.floa...  1.85 us
    dot_general x1, matrix products, local_grads(): jnp.einsum('hij,je->ihe', prob_low, value_window, preferred_element_type=...  1.82 us
  transfers between devices with their start and end apart: 2, of which 2 were waited for; matrix products, arithmetic and copies ran while one was open for 4% of the time, Pallas kernels for 0%

profile of v5, /device:TPU:54, one launch (start us, length us, event | category | flops | bytes accessed | tf_op | source)
XLA Modules:
  0.0 81.9 jit_solution(3605782663210288484)
XLA Ops:
  0.6 1.0 %pad_maximum_fusion.1 = bf16[2,512,128]{2,1,0:T(8,128)(2,1)S(1)} fusion(bf16[1,512,128]{2,1,0:T(8,128)(2,1)} %bitcast.73, bf16[1,512,128]{2,1,0:T(8,128)(2,1)} %bitcast.75), kind=kLoop, calls=%fused_computation.29 | loop fusion | flops 131072 | bytes 524288 | tf_op jit(solution)/shard_map/stack | solution.py:195
  1.6 4.6 %collective-permute-start.1 = (bf16[2,512,128]{2,1,0:T(8,128)(2,1)S(1)}, bf16[2,512,128]{2,1,0:T(8,128)(2,1)S(1)}, u32[]{:S(2)}, u32[]{:S(2)}) collective-permute-start(bf16[2,512,128]{2,1,0:T(8,128)(2,1)S(1)} %pad_maximum_fusion.1), channel_id=1, source_target_pairs={{0,14},{1,15},{2,12},{3,13},{4,10},{5,11},{6,8},{7,9},{8,22},{9,23... | collective-permute-start | bytes 786440 | tf_op jit(solution)/shard_map/ppermute | solution.py:30
  6.2 4.3 %collective-permute-start = (bf16[2,512,128]{2,1,0:T(8,128)(2,1)S(1)}, bf16[2,512,128]{2,1,0:T(8,128)(2,1)S(1)}, u32[]{:S(2)}, u32[]{:S(2)}) collective-permute-start(bf16[2,512,128]{2,1,0:T(8,128)(2,1)S(1)} %pad_maximum_fusion.1), channel_id=1, source_target_pairs={{0,16},{8,24},{16,32},{24,40},{32,48},{40,56},{48,64},{56,72},{64,... | collective-permute-start | bytes 786440 | tf_op jit(solution)/shard_map/ppermute | solution.py:14
  10.6 1.1 %copy.28 = bf16[512,2,128]{0,2,1:T(8,128)(2,1)S(1)} copy(bf16[512,2,128]{2,1,0:T(2,128)(2,1)} %param.5) | data formatting | bytes 524288 | tf_op args[0]
  11.7 1.1 %copy.22 = bf16[512,2,128]{0,2,1:T(8,128)(2,1)S(1)} copy(bf16[512,2,128]{2,1,0:T(2,128)(2,1)} %param.8) | data formatting | bytes 524288 | tf_op args[3]
  12.8 1.4 %compare_and_fusion = pred[512,1536]{0,1:T(8,128)(4,1)S(1)} fusion(s32[512]{0:T(512)S(1)} %iota_add_fusion.1, s32[512]{0:T(512)} %param.9, s32[1536]{0:T(1024)S(1)} %iota_add_fusion), kind=kLoop, calls=%fused_computation.13 | loop fusion | flops 2359296 | bytes 796672 | tf_op jit(solution)/shard_map/and | solution.py:169
  14.2 0.9 %collective-permute-done.1 = bf16[2,512,128]{2,1,0:T(8,128)(2,1)S(1)} collective-permute-done((bf16[2,512,128]{2,1,0:T(8,128)(2,1)S(1)}, bf16[2,512,128]{2,1,0:T(8,128)(2,1)S(1)}, u32[]{:S(2)}, u32[]{:S(2)}) %collective-permute-start.1) | collective-permute-done | bytes 262176 | tf_op jit(solution)/shard_map/ppermute | solution.py:30
  15.1 18.9 %collective-permute-done = bf16[2,512,128]{2,1,0:T(8,128)(2,1)S(1)} collective-permute-done((bf16[2,512,128]{2,1,0:T(8,128)(2,1)S(1)}, bf16[2,512,128]{2,1,0:T(8,128)(2,1)S(1)}, u32[]{:S(2)}, u32[]{:S(2)}) %collective-permute-start) | collective-permute-done | bytes 262176 | tf_op jit(solution)/shard_map/ppermute | solution.py:14
  34.0 1.0 %maximum_maximum_fusion = bf16[2,1536,128]{2,1,0:T(8,128)(2,1)S(1)} fusion(bf16[1,512,128]{2,1,0:T(8,128)(2,1)} %bitcast.74, bf16[1,512,128]{2,1,0:T(8,128)(2,1)} %bitcast.76, bf16[2,512,128]{2,1,0:T(8,128)(2,1)S(1)} %collective-permute-done.1, bf16[2,512,128]{2,1,0:T(8,128)(2,1)S(1)} %collective-permute-done), kind=kLoop, calls=%fused_computation.25 | loop fusion | flops 3145728 | bytes 1572864 | tf_op jit(solution)/shard_map/concatenate | solution.py:203
  35.0 1.4 %fusion.2 = (f32[2,512]{1,0:T(2,128)S(1)}, f32[1536,512,2]{1,0,2:T(8,128)S(1)}) fusion(pred[512,1536]{0,1:T(8,128)(4,1)S(1)} %compare_and_fusion, bf16[512,2,128]{0,2,1:T(8,128)(2,1)S(1)} %copy.28, bf16[2,1536,128]{2,1,0:T(8,128)(2,1)S(1)} %maximum_maximum_fusion), kind=kOutput, calls=%fused_computation.6 | convolution fusion | flops 407370752 | bytes 7737344 | tf_op jit(solution)/shard_map/ihe,je->hij/dot_general | solution.py:170
  36.4 1.4 %fusion.5 = f32[2,512]{1,0:T(2,128)S(1)} fusion(f32[1536,512,2]{1,0,2:T(8,128)S(1)} %get-tuple-element.14, f32[2,512]{1,0:T(2,128)S(1)} %get-tuple-element.13, pred[512,1536]{0,1:T(8,128)(4,1)S(1)} %compare_and_fusion), kind=kLoop, calls=%fused_computation.9 | loop fusion | flops 6290432 | bytes 7086080 | tf_op jit(solution)/shard_map/reduce_sum | solution.py:173
  37.8 1.8 %fusion.12 = f32[512,2]{0,1:T(2,128)S(1)} fusion(bf16[512,2,128]{0,2,1:T(8,128)(2,1)S(1)} %copy.22, bf16[2,1536,128]{2,1,0:T(8,128)(2,1)S(1)} %maximum_maximum_fusion, f32[1536,512,2]{1,0,2:T(8,128)S(1)} %get-tuple-element.14, f32[2,512]{1,0:T(2,128)S(1)} %log_add_fusion, pred[512,1536]{0,1:T(8,128)(4,1)S(1)} %compare_and_fusion), kind=kOutput, calls=%fused_computation.23 | convolution fusion | flops 409336832 | bytes 7741440 | tf_op jit(solution)/shard_map/hij,je->ihe/dot_general | solution.py:176
  39.7 1.8 %convolution_bitcast_fusion = f32[1536,128]{0,1:T(8,128)S(1)} fusion(bf16[512,2,128]{0,2,1:T(8,128)(2,1)S(1)} %copy.22, f32[1536,512,2]{1,0,2:T(8,128)S(1)} %get-tuple-element.14, f32[2,512]{1,0:T(2,128)S(1)} %log_add_fusion, pred[512,1536]{0,1:T(8,128)(4,1)S(1)} %compare_and_fusion), kind=kOutput, calls=%fused_computation.14 | convolution fusion | flops 408944640 | bytes 8130560 | tf_op jit(solution)/shard_map/hij,ihe->je/dot_general | solution.py:186
  41.5 2.3 %fusion.1 = bf16[2,512,1536]{1,2,0:T(8,128)(2,1)S(1)} fusion(f32[1536,512,2]{1,0,2:T(8,128)S(1)} %get-tuple-element.14, bf16[512,2,128]{0,2,1:T(8,128)(2,1)S(1)} %copy.22, f32[2,512]{1,0:T(2,128)S(1)} %bitcast.77, f32[2,512]{1,0:T(2,128)S(1)} %log_add_fusion, pred[512,1536]{0,1:T(8,128)(4,1)S(1)} %compare_and_fusion, ...), kind=kOutput, calls=%fused_computation.2 | convolution fusion | flops 412090368 | bytes 10887168 | tf_op jit(solution)/shard_map/ihe,je->hij/dot_general | solution.py:180
  43.9 0.6 fusion.13
  44.5 1.2 %fusion.9 = f32[1536,128]{0,1:T(8,128)S(1)} fusion(bf16[2,512,1536]{1,2,0:T(8,128)(2,1)S(1)} %fusion.1, bf16[512,2,128]{0,2,1:T(8,128)(2,1)S(1)} %copy.28), kind=kOutput, calls=%fused_computation.16 | convolution fusion | flops 402849792 | bytes 4194304 | tf_op jit(solution)/shard_map/hij,ihe->je/dot_general | solution.py:185
  45.6 0.9 %copy.33 = bf16[512,2,128]{2,1,0:T(2,128)(2,1)} copy(bf16[512,2,128]{0,2,1:T(8,128)(2,1)S(1)} %fusion.13) | data formatting | bytes 524288
  46.5 0.1 pad_maximum_fusion
  46.6 0.5 copy.31
  47.1 1.3 %copy.43 = f32[3,2,2,2,64,256]{5,4,1,2,3,0:T(8,128)} copy(f32[3,2,2,2,64,256]{5,4,3,2,1,0:T(8,128)S(1)} %bitcast.72) | data formatting | bytes 3145728 | tf_op jit(solution)/shard_map/reshape | solution.py:212
  48.4 30.8 %shard_map.76 = (bf16[64,128]{1,0:T(8,128)(2,1)}, bf16[64,128]{1,0:T(8,128)(2,1)}) custom-call(f32[3,2,2,2,64,256]{5,4,3,2,1,0:T(8,128)} %bitcast.71), custom_call_target="tpu_custom_call" | custom-call | tf_op jit(solution)/shard_map/pallas_call | solution.py:146
  79.2 1.3 %copy.46 = bf16[64,128]{1,0:T(8,128)(2,1)} copy(bf16[64,128]{1,0:T(8,128)(2,1)} %get-tuple-element.19) | data formatting | bytes 32768
  80.5 1.3 %copy.47 = bf16[64,128]{1,0:T(8,128)(2,1)} copy(bf16[64,128]{1,0:T(8,128)(2,1)} %get-tuple-element.20) | data formatting | bytes 32768
  (3 shorter events, 0.0 us)
Async XLA Ops:
  1.6 13.4 %collective-permute-start.1 = (bf16[2,512,128]{2,1,0:T(8,128)(2,1)S(1)}, bf16[2,512,128]{2,1,0:T(8,128)(2,1)S(1)}, u32[]{:S(2)}, u32[]{:S(2)}) collective-permute-start(bf16[2,512,128]{2,1,0:T(8,128)(2,1)S(1)} %pad_maximum_fusion.1), channel_id=1, source_target_pairs={{0,14},{1,15},{2,12},{3,13},{4,10},{5,11},{6,8},{7,9},{8,22},{9,23... | collective-permute-start | bytes 786440 | tf_op jit(solution)/shard_map/ppermute | solution.py:30
  6.2 27.7 %collective-permute-start = (bf16[2,512,128]{2,1,0:T(8,128)(2,1)S(1)}, bf16[2,512,128]{2,1,0:T(8,128)(2,1)S(1)}, u32[]{:S(2)}, u32[]{:S(2)}) collective-permute-start(bf16[2,512,128]{2,1,0:T(8,128)(2,1)S(1)} %pad_maximum_fusion.1), channel_id=1, source_target_pairs={{0,16},{8,24},{16,32},{24,40},{32,48},{40,56},{48,64},{56,72},{64,... | collective-permute-start | bytes 786440 | tf_op jit(solution)/shard_map/ppermute | solution.py:14

commit v6 on v5

--- a/solution.py
+++ b/solution.py
@@ -164,6 +164,69 @@
     )(chunks)
 
 
+def attention_kernel(q_ref, d_ref, k_ref, v_ref, s_ref, dq_ref, t_ref, dk_acc, dv_acc):
+    heads, rows, width = q_ref.shape
+    span = k_ref.shape[0]
+    tile = 128
+    reach = min(span, WIN * rows + tile)
+    scale = width ** (-0.5)
+    f32 = jnp.float32
+    dk_acc[...] = jnp.zeros_like(dk_acc)
+    dv_acc[...] = jnp.zeros_like(dv_acc)
+    contract_last = (((1,), (1,)), ((), ()))
+    contract_first = (((0,), (0,)), ((), ()))
+    for h in range(heads):
+        for r0 in range(0, rows, tile):
+            k0 = min(r0, span - reach)
+            qt = q_ref[h, r0 : r0 + tile, :]
+            dt = d_ref[h, r0 : r0 + tile, :]
+            kt = k_ref[k0 : k0 + reach, :]
+            vt = v_ref[k0 : k0 + reach, :]
+            starts = s_ref[r0 : r0 + tile, :]
+            row = r0 + lax.broadcasted_iota(jnp.int32, (tile, reach), 0)
+            col = k0 + lax.broadcasted_iota(jnp.int32, (tile, reach), 1)
+            visible = (col >= starts) & (col <= row + WIN * rows)
+            scores = lax.dot_general(qt, kt, contract_last, preferred_element_type=f32) * scale
+            top = jnp.max(jnp.where(visible, scores, -1e30), axis=1, keepdims=True)
+            expo = jnp.where(visible, jnp.exp(scores - top), 0.0)
+            lse = top + jnp.log(jnp.sum(expo, axis=1, keepdims=True))
+            prob = jnp.where(visible, jnp.exp(scores - lse), 0.0)
+            prob_low = prob.astype(jnp.bfloat16)
+            attended = jnp.dot(prob_low, vt, preferred_element_type=f32)
+            delta = jnp.sum(dt.astype(f32) * attended, axis=1, keepdims=True)
+            dprob = lax.dot_general(dt, vt, contract_last, preferred_element_type=f32)
+            dscore = (prob * (dprob - delta)).astype(jnp.bfloat16)
+            dq = jnp.dot(dscore, kt, preferred_element_type=f32) * scale
+            dq_ref[h, r0 : r0 + tile, :] = dq.astype(dq_ref.dtype)
+            dk_acc[k0 : k0 + reach, :] += lax.dot_general(dscore, qt, contract_first, preferred_element_type=f32)
+            dv_acc[k0 : k0 + reach, :] += lax.dot_general(prob_low, dt, contract_first, preferred_element_type=f32)
+    piece = t_ref.shape[4]
+    for w in range(t_ref.shape[0]):
+        for c in range(rows // piece):
+            first = w * rows + c * piece
+            place = (w, c % 2, (c // 2) % 2, c // 4)
+            t_ref[place + (slice(None), slice(0, width))] = dk_acc[first : first + piece, :] * scale
+            t_ref[place + (slice(None), slice(width, 2 * width))] = dv_acc[first : first + piece, :]
+
+
+def attention(q, dout, kwin, vwin, starts, parts):
+    heads, rows, width = q.shape
+    span = kwin.shape[0]
+    f32 = jnp.float32
+    piece = rows // parts
+    vmem = pl.BlockSpec(memory_space=pltpu.VMEM)
+    return pl.pallas_call(
+        attention_kernel,
+        out_shape=(
+            jax.ShapeDtypeStruct(q.shape, q.dtype),
+            jax.ShapeDtypeStruct((span // rows, 2, 2, 2, piece, 2 * width), f32),
+        ),
+        in_specs=[vmem] * 5,
+        out_specs=(vmem, vmem),
+        scratch_shapes=[pltpu.VMEM((span, width), f32), pltpu.VMEM((span, width), f32)],
+    )(q, dout, kwin, vwin, starts)
+
+
 def local_grads(q, dout, starts, kwin, value_window, qpos, kpos):
     scale = q.shape[-1] ** (-0.5)
     visible = (kpos[None, :] >= starts[:, None]) & (kpos[None, :] <= qpos[:, None])
@@ -205,12 +268,18 @@
     first_position = position * rows
     qpos = first_position + jnp.arange(rows, dtype=jnp.int32)
     kpos = first_position - WIN * rows + jnp.arange(window_span, dtype=jnp.int32)
-    q_grad, terms = local_grads(queries, out_grad, doc_start, window[0], window[1], qpos, kpos)
     parts = lax.axis_size("head")
-    piece = rows // parts
-    head = lax.axis_index("head")
-    chunks = terms.reshape(WIN + 1, 2, 2, 2, piece, 2 * window_width)
-    chunks = jnp.transpose(chunks, (0, 3, 2, 1, 4, 5))
+    window_start = first_position - WIN * rows
+    starts = (doc_start - window_start).reshape(rows, 1)
+    dq, chunks = attention(
+        jnp.transpose(queries, (1, 0, 2)),
+        jnp.transpose(out_grad, (1, 0, 2)),
+        window[0],
+        window[1],
+        starts,
+        parts,
+    )
+    q_grad = jnp.transpose(dq, (1, 0, 2))
     k_grad, v_grad = grad_reduce(chunks, window_width, jnp.bfloat16)
     return (q_grad, k_grad, v_grad)
 

time: 82.3 us -> 82 us (level)
  Pallas kernels: 30.8 us -> 42 us
  matrix products: 9.14 us -> 0 us
  other arithmetic: 4.94 us -> 1.77 us
    pallas_call x0 -> x1, Pallas kernels: none -> 11.1 us  [attention(): pl.pallas_call(attention_kernel, out_shape=(jax.ShapeDtypeStruct(q.shape,...]
    dot_general x6 -> x0, matrix products: 9.14 us -> none  [the longest x1 2.35 us: local_grads(): jnp.einsum('ihe,je->hij', dout, value_window, preferred_element_type=jnp....]
    transpose x0 -> x1, local copies, waits for them, and re-layouts: none -> 1.89 us  [body(): jnp.transpose(out_grad, (1, 0, 2))]
    reduce_sum x1 -> x0, other arithmetic: 1.44 us -> none  [local_grads(): lse = top + jnp.log(jnp.sum(expo, axis=-1, keepdims=True))]
    and x1 -> x0, other arithmetic: 1.36 us -> none  [local_grads(): (kpos[None, :] >= starts[:, None]) & (kpos[None, :] <= qpos[:, None])]
    unnamed x5 -> x7, local copies, waits for them, and re-layouts: 5.75 us -> 4.58 us
    concatenate x1, other arithmetic: 1.02 us -> 0.05 us  [body(): window = jnp.concatenate(pieces, axis=1)]
    squeeze x0 -> x1, local copies, waits for them, and re-layouts: none -> 0.94 us  [body(): window[1]]
where the time goes in v6:
time: 82 us; the launch traced here: 81.6 us
  Pallas kernels  42 us (51%)
  waiting for transfers between devices  20 us (24%)
  starting transfers between devices  8.89 us (11%)
  local copies, waits for them, and re-layouts  8.27 us (10%)
  other arithmetic  1.77 us (2%)
    pallas_call x1, Pallas kernels, grad_reduce(): pl.pallas_call(grad_reduce_kernel, out_shape=(out, out), in_specs=[pl.Blo...  30.8 us
    ppermute x1, waiting for transfers between devices, from_behind(): return lax.ppermute(block, axis, route)  18.9 us
    pallas_call x1, Pallas kernels, attention(): pl.pallas_call(attention_kernel, out_shape=(jax.ShapeDtypeStruct(q.shape,...  11.1 us
    ppermute x1, starting transfers between devices, nearest_next(): return lax.ppermute(block, ('dcn', 'blk', 'head'), route)  4.61 us
    unnamed x7, local copies, waits for them, and re-layouts  4.58 us
    ppermute x1, starting transfers between devices, from_behind(): return lax.ppermute(block, axis, route)  4.28 us
    transpose x1, local copies, waits for them, and re-layouts, body(): jnp.transpose(out_grad, (1, 0, 2))  1.89 us
  transfers between devices with their start and end apart: 2, of which 2 were waited for; matrix products, arithmetic and copies ran while one was open for 4% of the time, Pallas kernels for 0%

profile of v6, /device:TPU:54, one launch (start us, length us, event | category | flops | bytes accessed | tf_op | source)
XLA Modules:
  0.0 81.6 jit_solution(313726215809456353)
XLA Ops:
  0.6 0.0 copy-start
  0.6 0.0 copy-start.1
  0.7 1.0 %pad_maximum_fusion = bf16[2,512,128]{2,1,0:T(8,128)(2,1)S(1)} fusion(bf16[1,512,128]{2,1,0:T(8,128)(2,1)} %bitcast.12, bf16[1,512,128]{2,1,0:T(8,128)(2,1)} %bitcast.14), kind=kLoop, calls=%fused_computation.3 | loop fusion | flops 131072 | bytes 524288 | tf_op jit(solution)/shard_map/stack | solution.py:258
  1.7 4.6 %collective-permute-start.1 = (bf16[2,512,128]{2,1,0:T(8,128)(2,1)S(1)}, bf16[2,512,128]{2,1,0:T(8,128)(2,1)S(1)}, u32[]{:S(2)}, u32[]{:S(2)}) collective-permute-start(bf16[2,512,128]{2,1,0:T(8,128)(2,1)S(1)} %pad_maximum_fusion), channel_id=1, source_target_pairs={{0,14},{1,15},{2,12},{3,13},{4,10},{5,11},{6,8},{7,9},{8,22},{9,23... | collective-permute-start | bytes 786440 | tf_op jit(solution)/shard_map/ppermute | solution.py:30
  6.3 4.3 %collective-permute-start = (bf16[2,512,128]{2,1,0:T(8,128)(2,1)S(1)}, bf16[2,512,128]{2,1,0:T(8,128)(2,1)S(1)}, u32[]{:S(2)}, u32[]{:S(2)}) collective-permute-start(bf16[2,512,128]{2,1,0:T(8,128)(2,1)S(1)} %pad_maximum_fusion), channel_id=1, source_target_pairs={{0,16},{8,24},{16,32},{24,40},{32,48},{40,56},{48,64},{56,72},{64,... | collective-permute-start | bytes 786440 | tf_op jit(solution)/shard_map/ppermute | solution.py:14
  10.6 0.7 broadcast_subtract_fusion
  11.3 0.9 %copy.13.s_ref = s32[512,1]{1,0:T(8,128)} copy(s32[512,1]{0,1:T(1,128)S(1)} %bitcast.17) | data formatting | bytes 4096 | tf_op jit(solution)/shard_map/reshape | solution.py:273
  12.2 1.9 %copy_bitcast_fusion = (bf16[2,512,128]{2,1,0:T(8,128)(2,1)}, bf16[2,512,128]{2,1,0:T(8,128)(2,1)}) fusion(bf16[512,2,128]{2,1,0:T(2,128)(2,1)} %param.8, bf16[512,2,128]{2,1,0:T(2,128)(2,1)} %param.5), kind=kLoop, calls=%fused_computation.4 | loop fusion | bytes 1048576 | tf_op jit(solution)/shard_map/transpose | solution.py:276
  14.0 1.1 %collective-permute-done.1 = bf16[2,512,128]{2,1,0:T(8,128)(2,1)S(1)} collective-permute-done((bf16[2,512,128]{2,1,0:T(8,128)(2,1)S(1)}, bf16[2,512,128]{2,1,0:T(8,128)(2,1)S(1)}, u32[]{:S(2)}, u32[]{:S(2)}) %collective-permute-start.1) | collective-permute-done | bytes 262176 | tf_op jit(solution)/shard_map/ppermute | solution.py:30
  15.1 18.9 %collective-permute-done = bf16[2,512,128]{2,1,0:T(8,128)(2,1)S(1)} collective-permute-done((bf16[2,512,128]{2,1,0:T(8,128)(2,1)S(1)}, bf16[2,512,128]{2,1,0:T(8,128)(2,1)S(1)}, u32[]{:S(2)}, u32[]{:S(2)}) %collective-permute-start) | collective-permute-done | bytes 262176 | tf_op jit(solution)/shard_map/ppermute | solution.py:14
  34.0 0.0 copy-done
  34.0 0.0 copy-done.1
  34.1 0.1 maximum_maximum_fusion
  34.1 0.9 %slice_bitcast_fusion = (bf16[1536,128]{1,0:T(8,128)(2,1)}, bf16[1536,128]{1,0:T(8,128)(2,1)}) fusion(bf16[2,1536,128]{2,1,0:T(8,128)(2,1)S(1)} %maximum_maximum_fusion), kind=kLoop, calls=%fused_computation.1 | loop fusion | bytes 1572864 | tf_op jit(solution)/shard_map/squeeze | solution.py:278
  35.0 11.1 %shard_map.76 = (bf16[2,512,128]{2,1,0:T(8,128)(2,1)}, f32[3,2,2,2,64,256]{5,4,3,2,1,0:T(8,128)}) custom-call(bf16[2,512,128]{2,1,0:T(8,128)(2,1)} %get-tuple-element.20.q_ref, bf16[2,512,128]{2,1,0:T(8,128)(2,1)} %get-tuple-element.19.d_ref, bf16[1536,128]{1,0:T(8,128)(2,1)} %get-tuple-element.18.k_ref, bf16[1536,128]{1,0:T(8,128)(2,1)} %get-tuple-element.17.v_ref, ...), custom_call_target="tpu_custom_call" | custom-call | tf_op jit(solution)/shard_map/pallas_call | solution.py:218
  46.2 1.9 %copy.14 = bf16[512,2,128]{2,1,0:T(2,128)(2,1)} copy(bf16[512,2,128]{2,0,1:T(8,128)(2,1)} %bitcast.16) | data formatting | bytes 524288
  48.1 30.8 %shard_map.77 = (bf16[64,128]{1,0:T(8,128)(2,1)}, bf16[64,128]{1,0:T(8,128)(2,1)}) custom-call(f32[3,2,2,2,64,256]{5,4,3,2,1,0:T(8,128)} %get-tuple-element.8.x_ref), custom_call_target="tpu_custom_call" | custom-call | tf_op jit(solution)/shard_map/pallas_call | solution.py:146
  78.9 1.3 %copy.19 = bf16[64,128]{1,0:T(8,128)(2,1)} copy(bf16[64,128]{1,0:T(8,128)(2,1)} %get-tuple-element.25) | data formatting | bytes 32768
  80.3 1.3 %copy.20 = bf16[64,128]{1,0:T(8,128)(2,1)} copy(bf16[64,128]{1,0:T(8,128)(2,1)} %get-tuple-element.26) | data formatting | bytes 32768
Async XLA Ops:
  0.6 33.4 %copy-start = (bf16[512,128]{1,0:T(8,128)(2,1)S(1)}, bf16[512,128]{1,0:T(8,128)(2,1)}, u32[]{:S(2)}) copy-start(bf16[512,128]{1,0:T(8,128)(2,1)} %param.7) | copy-start | bytes 393220
  0.6 33.4 %copy-start.1 = (bf16[512,128]{1,0:T(8,128)(2,1)S(1)}, bf16[512,128]{1,0:T(8,128)(2,1)}, u32[]{:S(2)}) copy-start(bf16[512,128]{1,0:T(8,128)(2,1)} %param.6) | copy-start | bytes 393220
  1.7 13.4 %collective-permute-start.1 = (bf16[2,512,128]{2,1,0:T(8,128)(2,1)S(1)}, bf16[2,512,128]{2,1,0:T(8,128)(2,1)S(1)}, u32[]{:S(2)}, u32[]{:S(2)}) collective-permute-start(bf16[2,512,128]{2,1,0:T(8,128)(2,1)S(1)} %pad_maximum_fusion), channel_id=1, source_target_pairs={{0,14},{1,15},{2,12},{3,13},{4,10},{5,11},{6,8},{7,9},{8,22},{9,23... | collective-permute-start | bytes 786440 | tf_op jit(solution)/shard_map/ppermute | solution.py:30
  6.3 27.7 %collective-permute-start = (bf16[2,512,128]{2,1,0:T(8,128)(2,1)S(1)}, bf16[2,512,128]{2,1,0:T(8,128)(2,1)S(1)}, u32[]{:S(2)}, u32[]{:S(2)}) collective-permute-start(bf16[2,512,128]{2,1,0:T(8,128)(2,1)S(1)} %pad_maximum_fusion), channel_id=1, source_target_pairs={{0,16},{8,24},{16,32},{24,40},{32,48},{40,56},{48,64},{56,72},{64,... | collective-permute-start | bytes 786440 | tf_op jit(solution)/shard_map/ppermute | solution.py:14

commit v7 on v6

--- a/solution.py
+++ b/solution.py
@@ -30,7 +30,7 @@
     return lax.ppermute(block, ("dcn", "blk", "head"), route)
 
 
-def grad_reduce_kernel(x_ref, k_out, v_out, r1, r2, r3, a1, a2, a3, total, back, sends, recvs):
+def grad_reduce_kernel(x_ref, k_out, v_out, r1, r2, r3, a1, a2, t1, t2, a3, total, back, sends, recvs):
     mesh_id = pl.DeviceIdType.MESH
     dcn = lax.axis_index("dcn")
     blk = lax.axis_index("blk")
@@ -69,7 +69,8 @@
     pl.semaphore_wait(barrier, peers)
 
     windows = x_ref.shape[0]
-    sources = [x_ref, a1, a2]
+    kept = [x_ref, a1, a2]
+    outgoing = [None, t1, t2]
     targets = [r1, r2, r3]
     copies = [[None] * windows for _ in range(3)]
 
@@ -80,8 +81,9 @@
 
     def send(stage, w):
         keep = keep_bit(stage, w)
+        source = x_ref.at[w, 1 - keep] if stage == 0 else outgoing[stage].at[w]
         copy = pltpu.make_async_remote_copy(
-            src_ref=sources[stage].at[w, 1 - keep],
+            src_ref=source,
             dst_ref=targets[stage].at[w],
             send_sem=sends.at[stage, w],
             recv_sem=recvs.at[stage, w],
@@ -106,12 +108,15 @@
     for stage in range(3):
         for w in range(windows):
             copies[stage][w].wait_recv()
-            summed = sources[stage][w, keep_bit(stage, w)] + targets[stage][w]
+            arrived = targets[stage][w].astype(jnp.float32)
+            summed = kept[stage][w, keep_bit(stage, w)] + arrived
             if stage < 2:
-                sources[stage + 1][w] = summed
+                kept[stage + 1][w] = summed
+                away = kept[stage + 1][w, 1 - keep_bit(stage + 1, w)]
+                outgoing[stage + 1][w] = away.astype(outgoing[stage + 1].dtype)
                 send(stage + 1, w)
             elif w < WIN:
-                a3[w] = summed
+                a3[w] = summed.astype(a3.dtype)
 
                 @pl.when(sends_back[w])
                 def _():
@@ -124,7 +129,7 @@
         @pl.when(gets_back[w])
         def _():
             back_copy(w, block + WIN - w).wait_recv()
-            total[...] = total[...] + back[w]
+            total[...] = total[...] + back[w].astype(jnp.float32)
 
     width = k_out.shape[1]
     k_out[...] = total[:, :width].astype(k_out.dtype)
@@ -142,6 +147,7 @@
 def grad_reduce(chunks, width, dtype):
     windows, rest = chunks.shape[0], chunks.shape[4:]
     f32 = jnp.float32
+    link = jnp.bfloat16
     out = jax.ShapeDtypeStruct((rest[0], width), dtype)
     return pl.pallas_call(
         grad_reduce_kernel,
@@ -150,13 +156,15 @@
         out_specs=(pl.BlockSpec(memory_space=pltpu.VMEM), pl.BlockSpec(memory_space=pltpu.VMEM)),
         scratch_shapes=[
             pltpu.VMEM((windows, 2, 2) + rest, f32),
-            pltpu.VMEM((windows, 2) + rest, f32),
-            pltpu.VMEM((windows,) + rest, f32),
+            pltpu.VMEM((windows, 2) + rest, link),
+            pltpu.VMEM((windows,) + rest, link),
             pltpu.VMEM((windows, 2, 2) + rest, f32),
             pltpu.VMEM((windows, 2) + rest, f32),
-            pltpu.VMEM((WIN,) + rest, f32),
+            pltpu.VMEM((windows, 2) + rest, link),
+            pltpu.VMEM((windows,) + rest, link),
+            pltpu.VMEM((WIN,) + rest, link),
             pltpu.VMEM(rest, f32),
-            pltpu.VMEM((WIN,) + rest, f32),
+            pltpu.VMEM((WIN,) + rest, link),
             pltpu.SemaphoreType.DMA((4, windows)),
             pltpu.SemaphoreType.DMA((4, windows)),
         ],

time: 82 us -> 74.1 us (0.904)
  the two profiles are of different devices: /device:TPU:54 before, /device:TPU:15 now
where the time goes in v7:
time: 74.1 us; the launch traced here: 73.6 us
  Pallas kernels  33.1 us (45%)
  waiting for transfers between devices  20.1 us (27%)
  starting transfers between devices  9.77 us (13%)
  local copies, waits for them, and re-layouts  8.27 us (11%)
  other arithmetic  1.77 us (2%)
    pallas_call x1, Pallas kernels, grad_reduce(): pl.pallas_call(grad_reduce_kernel, out_shape=(out, out), in_specs=[pl.Blo...  21.9 us
    ppermute x1, waiting for transfers between devices, nearest_next(): return lax.ppermute(block, ('dcn', 'blk', 'head'), route)  19.7 us
    pallas_call x1, Pallas kernels, attention(): pl.pallas_call(attention_kernel, out_shape=(jax.ShapeDtypeStruct(q.shape,...  11.1 us
    ppermute x1, starting transfers between devices, nearest_next(): return lax.ppermute(block, ('dcn', 'blk', 'head'), route)  5.77 us
    unnamed x7, local copies, waits for them, and re-layouts  4.58 us
    ppermute x1, starting transfers between devices, from_behind(): return lax.ppermute(block, axis, route)  4 us
    transpose x1, local copies, waits for them, and re-layouts, body(): jnp.transpose(out_grad, (1, 0, 2))  1.89 us
  transfers between devices with their start and end apart: 2, of which 2 were waited for; matrix products, arithmetic and copies ran while one was open for 5% of the time, Pallas kernels for 0%

profile of v7, /device:TPU:15, one launch (start us, length us, event | category | flops | bytes accessed | tf_op | source)
XLA Modules:
  0.0 73.6 jit_solution(11836928317535730707)
XLA Ops:
  0.6 0.0 copy-start
  0.6 0.0 copy-start.1
  0.7 1.0 %pad_maximum_fusion = bf16[2,512,128]{2,1,0:T(8,128)(2,1)S(1)} fusion(bf16[1,512,128]{2,1,0:T(8,128)(2,1)} %bitcast.12, bf16[1,512,128]{2,1,0:T(8,128)(2,1)} %bitcast.14), kind=kLoop, calls=%fused_computation.3 | loop fusion | flops 131072 | bytes 524288 | tf_op jit(solution)/shard_map/stack | solution.py:266
  1.7 5.8 %collective-permute-start.1 = (bf16[2,512,128]{2,1,0:T(8,128)(2,1)S(1)}, bf16[2,512,128]{2,1,0:T(8,128)(2,1)S(1)}, u32[]{:S(2)}, u32[]{:S(2)}) collective-permute-start(bf16[2,512,128]{2,1,0:T(8,128)(2,1)S(1)} %pad_maximum_fusion), channel_id=1, source_target_pairs={{0,14},{1,15},{2,12},{3,13},{4,10},{5,11},{6,8},{7,9},{8,22},{9,23... | collective-permute-start | bytes 786440 | tf_op jit(solution)/shard_map/ppermute | solution.py:30
  7.5 4.0 %collective-permute-start = (bf16[2,512,128]{2,1,0:T(8,128)(2,1)S(1)}, bf16[2,512,128]{2,1,0:T(8,128)(2,1)S(1)}, u32[]{:S(2)}, u32[]{:S(2)}) collective-permute-start(bf16[2,512,128]{2,1,0:T(8,128)(2,1)S(1)} %pad_maximum_fusion), channel_id=1, source_target_pairs={{0,16},{8,24},{16,32},{24,40},{32,48},{40,56},{48,64},{56,72},{64,... | collective-permute-start | bytes 786440 | tf_op jit(solution)/shard_map/ppermute | solution.py:14
  11.5 0.7 broadcast_subtract_fusion
  12.2 0.9 %copy.13.s_ref = s32[512,1]{1,0:T(8,128)} copy(s32[512,1]{0,1:T(1,128)S(1)} %bitcast.17) | data formatting | bytes 4096 | tf_op jit(solution)/shard_map/reshape | solution.py:281
  13.0 1.9 %copy_bitcast_fusion = (bf16[2,512,128]{2,1,0:T(8,128)(2,1)}, bf16[2,512,128]{2,1,0:T(8,128)(2,1)}) fusion(bf16[512,2,128]{2,1,0:T(2,128)(2,1)} %param.8, bf16[512,2,128]{2,1,0:T(2,128)(2,1)} %param.5), kind=kLoop, calls=%fused_computation.4 | loop fusion | bytes 1048576 | tf_op jit(solution)/shard_map/transpose | solution.py:284
  14.9 19.7 %collective-permute-done.1 = bf16[2,512,128]{2,1,0:T(8,128)(2,1)S(1)} collective-permute-done((bf16[2,512,128]{2,1,0:T(8,128)(2,1)S(1)}, bf16[2,512,128]{2,1,0:T(8,128)(2,1)S(1)}, u32[]{:S(2)}, u32[]{:S(2)}) %collective-permute-start.1) | collective-permute-done | bytes 262176 | tf_op jit(solution)/shard_map/ppermute | solution.py:30
  34.6 0.4 collective-permute-done
  35.0 0.0 copy-done
  35.0 0.0 copy-done.1
  35.0 0.1 maximum_maximum_fusion
  35.0 0.9 %slice_bitcast_fusion = (bf16[1536,128]{1,0:T(8,128)(2,1)}, bf16[1536,128]{1,0:T(8,128)(2,1)}) fusion(bf16[2,1536,128]{2,1,0:T(8,128)(2,1)S(1)} %maximum_maximum_fusion), kind=kLoop, calls=%fused_computation.1 | loop fusion | bytes 1572864 | tf_op jit(solution)/shard_map/squeeze | solution.py:286
  36.0 11.1 %shard_map.76 = (bf16[2,512,128]{2,1,0:T(8,128)(2,1)}, f32[3,2,2,2,64,256]{5,4,3,2,1,0:T(8,128)}) custom-call(bf16[2,512,128]{2,1,0:T(8,128)(2,1)} %get-tuple-element.20.q_ref, bf16[2,512,128]{2,1,0:T(8,128)(2,1)} %get-tuple-element.19.d_ref, bf16[1536,128]{1,0:T(8,128)(2,1)} %get-tuple-element.18.k_ref, bf16[1536,128]{1,0:T(8,128)(2,1)} %get-tuple-element.17.v_ref, ...), custom_call_target="tpu_custom_call" | custom-call | tf_op jit(solution)/shard_map/pallas_call | solution.py:226
  47.1 1.9 %copy.14 = bf16[512,2,128]{2,1,0:T(2,128)(2,1)} copy(bf16[512,2,128]{2,0,1:T(8,128)(2,1)} %bitcast.16) | data formatting | bytes 524288
  49.1 21.9 %shard_map.77 = (bf16[64,128]{1,0:T(8,128)(2,1)}, bf16[64,128]{1,0:T(8,128)(2,1)}) custom-call(f32[3,2,2,2,64,256]{5,4,3,2,1,0:T(8,128)} %get-tuple-element.8.x_ref), custom_call_target="tpu_custom_call" | custom-call | tf_op jit(solution)/shard_map/pallas_call | solution.py:152
  71.0 1.3 %copy.19 = bf16[64,128]{1,0:T(8,128)(2,1)} copy(bf16[64,128]{1,0:T(8,128)(2,1)} %get-tuple-element.25) | data formatting | bytes 32768
  72.3 1.3 %copy.20 = bf16[64,128]{1,0:T(8,128)(2,1)} copy(bf16[64,128]{1,0:T(8,128)(2,1)} %get-tuple-element.26) | data formatting | bytes 32768
Async XLA Ops:
  0.6 34.4 %copy-start = (bf16[512,128]{1,0:T(8,128)(2,1)S(1)}, bf16[512,128]{1,0:T(8,128)(2,1)}, u32[]{:S(2)}) copy-start(bf16[512,128]{1,0:T(8,128)(2,1)} %param.7) | copy-start | bytes 393220
  0.6 34.4 %copy-start.1 = (bf16[512,128]{1,0:T(8,128)(2,1)S(1)}, bf16[512,128]{1,0:T(8,128)(2,1)}, u32[]{:S(2)}) copy-start(bf16[512,128]{1,0:T(8,128)(2,1)} %param.6) | copy-start | bytes 393220
  1.7 32.9 %collective-permute-start.1 = (bf16[2,512,128]{2,1,0:T(8,128)(2,1)S(1)}, bf16[2,512,128]{2,1,0:T(8,128)(2,1)S(1)}, u32[]{:S(2)}, u32[]{:S(2)}) collective-permute-start(bf16[2,512,128]{2,1,0:T(8,128)(2,1)S(1)} %pad_maximum_fusion), channel_id=1, source_target_pairs={{0,14},{1,15},{2,12},{3,13},{4,10},{5,11},{6,8},{7,9},{8,22},{9,23... | collective-permute-start | bytes 786440 | tf_op jit(solution)/shard_map/ppermute | solution.py:30
  7.5 27.5 %collective-permute-start = (bf16[2,512,128]{2,1,0:T(8,128)(2,1)S(1)}, bf16[2,512,128]{2,1,0:T(8,128)(2,1)S(1)}, u32[]{:S(2)}, u32[]{:S(2)}) collective-permute-start(bf16[2,512,128]{2,1,0:T(8,128)(2,1)S(1)} %pad_maximum_fusion), channel_id=1, source_target_pairs={{0,16},{8,24},{16,32},{24,40},{32,48},{40,56},{48,64},{56,72},{64,... | collective-permute-start | bytes 786440 | tf_op jit(solution)/shard_map/ppermute | solution.py:14

commit v8 on v7

--- a/solution.py
+++ b/solution.py
@@ -30,7 +30,7 @@
     return lax.ppermute(block, ("dcn", "blk", "head"), route)
 
 
-def grad_reduce_kernel(x_ref, k_out, v_out, r1, r2, r3, a1, a2, t1, t2, a3, total, back, sends, recvs):
+def grad_reduce_kernel(x_ref, o_ref, r1, r2, r3, a1, a2, t1, t2, a3, total, back, sends, recvs):
     mesh_id = pl.DeviceIdType.MESH
     dcn = lax.axis_index("dcn")
     blk = lax.axis_index("blk")
@@ -131,9 +131,7 @@
             back_copy(w, block + WIN - w).wait_recv()
             total[...] = total[...] + back[w].astype(jnp.float32)
 
-    width = k_out.shape[1]
-    k_out[...] = total[:, :width].astype(k_out.dtype)
-    v_out[...] = total[:, width:].astype(v_out.dtype)
+    o_ref[...] = total[...]
     for stage in range(3):
         for w in range(windows):
             copies[stage][w].wait_send()
@@ -148,12 +146,11 @@
     windows, rest = chunks.shape[0], chunks.shape[4:]
     f32 = jnp.float32
     link = jnp.bfloat16
-    out = jax.ShapeDtypeStruct((rest[0], width), dtype)
-    return pl.pallas_call(
+    total = pl.pallas_call(
         grad_reduce_kernel,
-        out_shape=(out, out),
+        out_shape=jax.ShapeDtypeStruct(rest, f32),
         in_specs=[pl.BlockSpec(memory_space=pltpu.VMEM)],
-        out_specs=(pl.BlockSpec(memory_space=pltpu.VMEM), pl.BlockSpec(memory_space=pltpu.VMEM)),
+        out_specs=pl.BlockSpec(memory_space=pltpu.VMEM),
         scratch_shapes=[
             pltpu.VMEM((windows, 2, 2) + rest, f32),
             pltpu.VMEM((windows, 2) + rest, link),
@@ -170,11 +167,12 @@
         ],
         compiler_params=pltpu.CompilerParams(collective_id=0, has_side_effects=True),
     )(chunks)
-
-
-def attention_kernel(q_ref, d_ref, k_ref, v_ref, s_ref, dq_ref, t_ref, dk_acc, dv_acc):
+    return total[:, :width].astype(dtype), total[:, width:].astype(dtype)
+
+
+def attention_kernel(q_ref, d_ref, w_ref, s_ref, dq_ref, t_ref, dk_acc, dv_acc):
     heads, rows, width = q_ref.shape
-    span = k_ref.shape[0]
+    span = w_ref.shape[1]
     tile = 128
     reach = min(span, WIN * rows + tile)
     scale = width ** (-0.5)
@@ -188,8 +186,8 @@
             k0 = min(r0, span - reach)
             qt = q_ref[h, r0 : r0 + tile, :]
             dt = d_ref[h, r0 : r0 + tile, :]
-            kt = k_ref[k0 : k0 + reach, :]
-            vt = v_ref[k0 : k0 + reach, :]
+            kt = w_ref[0, k0 : k0 + reach, :]
+            vt = w_ref[1, k0 : k0 + reach, :]
             starts = s_ref[r0 : r0 + tile, :]
             row = r0 + lax.broadcasted_iota(jnp.int32, (tile, reach), 0)
             col = k0 + lax.broadcasted_iota(jnp.int32, (tile, reach), 1)
@@ -197,8 +195,7 @@
             scores = lax.dot_general(qt, kt, contract_last, preferred_element_type=f32) * scale
             top = jnp.max(jnp.where(visible, scores, -1e30), axis=1, keepdims=True)
             expo = jnp.where(visible, jnp.exp(scores - top), 0.0)
-            lse = top + jnp.log(jnp.sum(expo, axis=1, keepdims=True))
-            prob = jnp.where(visible, jnp.exp(scores - lse), 0.0)
+            prob = expo / jnp.sum(expo, axis=1, keepdims=True)
             prob_low = prob.astype(jnp.bfloat16)
             attended = jnp.dot(prob_low, vt, preferred_element_type=f32)
             delta = jnp.sum(dt.astype(f32) * attended, axis=1, keepdims=True)
@@ -217,9 +214,9 @@
             t_ref[place + (slice(None), slice(width, 2 * width))] = dv_acc[first : first + piece, :]
 
 
-def attention(q, dout, kwin, vwin, starts, parts):
+def attention(q, dout, window, starts, parts):
     heads, rows, width = q.shape
-    span = kwin.shape[0]
+    span = window.shape[1]
     f32 = jnp.float32
     piece = rows // parts
     vmem = pl.BlockSpec(memory_space=pltpu.VMEM)
@@ -229,10 +226,10 @@
             jax.ShapeDtypeStruct(q.shape, q.dtype),
             jax.ShapeDtypeStruct((span // rows, 2, 2, 2, piece, 2 * width), f32),
         ),
-        in_specs=[vmem] * 5,
+        in_specs=[vmem] * 4,
         out_specs=(vmem, vmem),
         scratch_shapes=[pltpu.VMEM((span, width), f32), pltpu.VMEM((span, width), f32)],
-    )(q, dout, kwin, vwin, starts)
+    )(q, dout, window, starts)
 
 
 def local_grads(q, dout, starts, kwin, value_window, qpos, kpos):
@@ -282,8 +279,7 @@
     dq, chunks = attention(
         jnp.transpose(queries, (1, 0, 2)),
         jnp.transpose(out_grad, (1, 0, 2)),
-        window[0],
-        window[1],
+        window,
         starts,
         parts,
     )

time: 74.1 us -> 72.5 us (0.978)
  local copies, waits for them, and re-layouts: 8.27 us -> 5.3 us
  other arithmetic: 1.77 us -> 3.51 us
    unnamed x7 -> x5, local copies, waits for them, and re-layouts: 4.58 us -> 1.93 us
    squeeze x1 -> x0, local copies, waits for them, and re-layouts: 0.94 us -> none  [body(): window[1]]
    concatenate x1, other arithmetic: 0.05 us -> 0.94 us  [body(): window = jnp.concatenate(pieces, axis=1)]
    another operation x0 -> x1, other arithmetic: none -> 0.85 us
where the time goes in v8:
time: 72.5 us; the launch traced here: 72.2 us
  Pallas kernels  32.8 us (45%)
  waiting for transfers between devices  20.1 us (28%)
  starting transfers between devices  9.77 us (13%)
  local copies, waits for them, and re-layouts  5.3 us (7%)
  other arithmetic  3.51 us (5%)
    pallas_call x1, Pallas kernels, grad_reduce(): pl.pallas_call(grad_reduce_kernel, out_shape=jax.ShapeDtypeStruct(rest, f...  21.9 us
    ppermute x1, waiting for transfers between devices, nearest_next(): return lax.ppermute(block, ('dcn', 'blk', 'head'), route)  19.7 us
    pallas_call x1, Pallas kernels, attention(): pl.pallas_call(attention_kernel, out_shape=(jax.ShapeDtypeStruct(q.shape,...  10.9 us
    ppermute x1, starting transfers between devices, nearest_next(): return lax.ppermute(block, ('dcn', 'blk', 'head'), route)  5.77 us
    ppermute x1, starting transfers between devices, from_behind(): return lax.ppermute(block, axis, route)  4 us
    unnamed x5, local copies, waits for them, and re-layouts  1.93 us
    transpose x1, local copies, waits for them, and re-layouts, body(): jnp.transpose(out_grad, (1, 0, 2))  1.89 us
  transfers between devices with their start and end apart: 2, of which 2 were waited for; matrix products, arithmetic and copies ran while one was open for 5% of the time, Pallas kernels for 0%

profile of v8, /device:TPU:15, one launch (start us, length us, event | category | flops | bytes accessed | tf_op | source)
XLA Modules:
  0.0 72.2 jit_solution(127581036684353892)
XLA Ops:
  0.6 0.0 copy-start
  0.6 0.0 copy-start.1
  0.7 1.0 %pad_maximum_fusion = bf16[2,512,128]{2,1,0:T(8,128)(2,1)S(1)} fusion(bf16[1,512,128]{2,1,0:T(8,128)(2,1)} %bitcast.8, bf16[1,512,128]{2,1,0:T(8,128)(2,1)} %bitcast.10), kind=kLoop, calls=%fused_computation.1 | loop fusion | flops 131072 | bytes 524288 | tf_op jit(solution)/shard_map/stack | solution.py:263
  1.7 5.8 %collective-permute-start.1 = (bf16[2,512,128]{2,1,0:T(8,128)(2,1)S(1)}, bf16[2,512,128]{2,1,0:T(8,128)(2,1)S(1)}, u32[]{:S(2)}, u32[]{:S(2)}) collective-permute-start(bf16[2,512,128]{2,1,0:T(8,128)(2,1)S(1)} %pad_maximum_fusion), channel_id=1, source_target_pairs={{0,14},{1,15},{2,12},{3,13},{4,10},{5,11},{6,8},{7,9},{8,22},{9,23... | collective-permute-start | bytes 786440 | tf_op jit(solution)/shard_map/ppermute | solution.py:30
  7.5 4.0 %collective-permute-start = (bf16[2,512,128]{2,1,0:T(8,128)(2,1)S(1)}, bf16[2,512,128]{2,1,0:T(8,128)(2,1)S(1)}, u32[]{:S(2)}, u32[]{:S(2)}) collective-permute-start(bf16[2,512,128]{2,1,0:T(8,128)(2,1)S(1)} %pad_maximum_fusion), channel_id=1, source_target_pairs={{0,16},{8,24},{16,32},{24,40},{32,48},{40,56},{48,64},{56,72},{64,... | collective-permute-start | bytes 786440 | tf_op jit(solution)/shard_map/ppermute | solution.py:14
  11.5 0.7 broadcast_subtract_fusion
  12.2 0.9 %copy.13.s_ref = s32[512,1]{1,0:T(8,128)} copy(s32[512,1]{0,1:T(1,128)S(1)} %bitcast.13) | data formatting | bytes 4096 | tf_op jit(solution)/shard_map/reshape | solution.py:278
  13.0 1.9 %copy_bitcast_fusion = (bf16[2,512,128]{2,1,0:T(8,128)(2,1)}, bf16[2,512,128]{2,1,0:T(8,128)(2,1)}) fusion(bf16[512,2,128]{2,1,0:T(2,128)(2,1)} %param.8, bf16[512,2,128]{2,1,0:T(2,128)(2,1)} %param.5), kind=kLoop, calls=%fused_computation.2 | loop fusion | bytes 1048576 | tf_op jit(solution)/shard_map/transpose | solution.py:281
  14.9 19.7 %collective-permute-done.1 = bf16[2,512,128]{2,1,0:T(8,128)(2,1)S(1)} collective-permute-done((bf16[2,512,128]{2,1,0:T(8,128)(2,1)S(1)}, bf16[2,512,128]{2,1,0:T(8,128)(2,1)S(1)}, u32[]{:S(2)}, u32[]{:S(2)}) %collective-permute-start.1) | collective-permute-done | bytes 262176 | tf_op jit(solution)/shard_map/ppermute | solution.py:30
  34.6 0.4 collective-permute-done
  35.0 0.0 copy-done
  35.0 0.0 copy-done.1
  35.0 0.9 %maximum_maximum_fusion.w_ref = bf16[2,1536,128]{2,1,0:T(8,128)(2,1)} fusion(bf16[1,512,128]{2,1,0:T(8,128)(2,1)S(1)} %bitcast.9, bf16[1,512,128]{2,1,0:T(8,128)(2,1)S(1)} %bitcast.11, bf16[2,512,128]{2,1,0:T(8,128)(2,1)S(1)} %collective-permute-done.1, bf16[2,512,128]{2,1,0:T(8,128)(2,1)S(1)} %collective-permute-done), kind=kLoop, calls=%fused_computation | loop fusion | flops 3145728 | bytes 1572864 | tf_op jit(solution)/shard_map/concatenate | solution.py:271
  35.9 10.9 %shard_map.76 = (bf16[2,512,128]{2,1,0:T(8,128)(2,1)}, f32[3,2,2,2,64,256]{5,4,3,2,1,0:T(8,128)}) custom-call(bf16[2,512,128]{2,1,0:T(8,128)(2,1)} %get-tuple-element.16.q_ref, bf16[2,512,128]{2,1,0:T(8,128)(2,1)} %get-tuple-element.15.d_ref, bf16[2,1536,128]{2,1,0:T(8,128)(2,1)} %maximum_maximum_fusion.w_ref, s32[512,1]{1,0:T(8,128)} %copy.13.s_ref), custom_call_target="tpu_custom_call" | custom-call | tf_op jit(solution)/shard_map/pallas_call | solution.py:223
  46.8 1.9 %copy.14 = bf16[512,2,128]{2,1,0:T(2,128)(2,1)} copy(bf16[512,2,128]{2,0,1:T(8,128)(2,1)} %bitcast.12) | data formatting | bytes 524288
  48.8 21.9 %shard_map.77 = f32[64,256]{1,0:T(8,128)} custom-call(f32[3,2,2,2,64,256]{5,4,3,2,1,0:T(8,128)} %get-tuple-element.6.x_ref), custom_call_target="tpu_custom_call" | custom-call | tf_op jit(solution)/shard_map/pallas_call | solution.py:149
  70.7 0.8 %convert.4 = bf16[64,256]{1,0:T(8,128)(2,1)S(1)} convert(f32[64,256]{1,0:T(8,128)} %shard_map.77) | non-fusion elementwise | flops 16384 | bytes 98304 | tf_op jit(solution)/shard_map/convert.1
  71.5 0.6 fusion
Async XLA Ops:
  0.6 34.4 %copy-start = (bf16[512,128]{1,0:T(8,128)(2,1)S(1)}, bf16[512,128]{1,0:T(8,128)(2,1)}, u32[]{:S(2)}) copy-start(bf16[512,128]{1,0:T(8,128)(2,1)} %param.7) | copy-start | bytes 393220
  0.6 34.4 %copy-start.1 = (bf16[512,128]{1,0:T(8,128)(2,1)S(1)}, bf16[512,128]{1,0:T(8,128)(2,1)}, u32[]{:S(2)}) copy-start(bf16[512,128]{1,0:T(8,128)(2,1)} %param.6) | copy-start | bytes 393220
  1.7 32.9 %collective-permute-start.1 = (bf16[2,512,128]{2,1,0:T(8,128)(2,1)S(1)}, bf16[2,512,128]{2,1,0:T(8,128)(2,1)S(1)}, u32[]{:S(2)}, u32[]{:S(2)}) collective-permute-start(bf16[2,512,128]{2,1,0:T(8,128)(2,1)S(1)} %pad_maximum_fusion), channel_id=1, source_target_pairs={{0,14},{1,15},{2,12},{3,13},{4,10},{5,11},{6,8},{7,9},{8,22},{9,23... | collective-permute-start | bytes 786440 | tf_op jit(solution)/shard_map/ppermute | solution.py:30
  7.5 27.5 %collective-permute-start = (bf16[2,512,128]{2,1,0:T(8,128)(2,1)S(1)}, bf16[2,512,128]{2,1,0:T(8,128)(2,1)S(1)}, u32[]{:S(2)}, u32[]{:S(2)}) collective-permute-start(bf16[2,512,128]{2,1,0:T(8,128)(2,1)S(1)} %pad_maximum_fusion), channel_id=1, source_target_pairs={{0,16},{8,24},{16,32},{24,40},{32,48},{40,56},{48,64},{56,72},{64,... | collective-permute-start | bytes 786440 | tf_op jit(solution)/shard_map/ppermute | solution.py:14

commit v9 on v8

--- a/solution.py
+++ b/solution.py
@@ -170,41 +170,55 @@
     return total[:, :width].astype(dtype), total[:, width:].astype(dtype)
 
 
-def attention_kernel(q_ref, d_ref, w_ref, s_ref, dq_ref, t_ref, dk_acc, dv_acc):
+def attention_kernel(f_ref, q_ref, d_ref, w_ref, s_ref, dq_ref, t_ref, dk_acc, dv_acc):
     heads, rows, width = q_ref.shape
     span = w_ref.shape[1]
     tile = 128
     reach = min(span, WIN * rows + tile)
+    skip = rows
     scale = width ** (-0.5)
     f32 = jnp.float32
     dk_acc[...] = jnp.zeros_like(dk_acc)
     dv_acc[...] = jnp.zeros_like(dv_acc)
     contract_last = (((1,), (1,)), ((), ()))
     contract_first = (((0,), (0,)), ((), ()))
+
+    def tile_grads(h, r0, k0, size):
+        qt = q_ref[h, r0 : r0 + tile, :]
+        dt = d_ref[h, r0 : r0 + tile, :]
+        kt = w_ref[0, k0 : k0 + size, :]
+        vt = w_ref[1, k0 : k0 + size, :]
+        starts = s_ref[r0 : r0 + tile, :]
+        row = r0 + lax.broadcasted_iota(jnp.int32, (tile, size), 0)
+        col = k0 + lax.broadcasted_iota(jnp.int32, (tile, size), 1)
+        visible = (col >= starts) & (col <= row + WIN * rows)
+        scores = lax.dot_general(qt, kt, contract_last, preferred_element_type=f32) * scale
+        top = jnp.max(jnp.where(visible, scores, -1e30), axis=1, keepdims=True)
+        expo = jnp.where(visible, jnp.exp(scores - top), 0.0)
+        prob = expo / jnp.sum(expo, axis=1, keepdims=True)
+        prob_low = prob.astype(jnp.bfloat16)
+        attended = jnp.dot(prob_low, vt, preferred_element_type=f32)
+        delta = jnp.sum(dt.astype(f32) * attended, axis=1, keepdims=True)
+        dprob = lax.dot_general(dt, vt, contract_last, preferred_element_type=f32)
+        dscore = (prob * (dprob - delta)).astype(jnp.bfloat16)
+        dq = jnp.dot(dscore, kt, preferred_element_type=f32) * scale
+        dq_ref[h, r0 : r0 + tile, :] = dq.astype(dq_ref.dtype)
+        dk_acc[k0 : k0 + size, :] += lax.dot_general(dscore, qt, contract_first, preferred_element_type=f32)
+        dv_acc[k0 : k0 + size, :] += lax.dot_general(prob_low, dt, contract_first, preferred_element_type=f32)
+
     for h in range(heads):
-        for r0 in range(0, rows, tile):
+        for t, r0 in enumerate(range(0, rows, tile)):
             k0 = min(r0, span - reach)
-            qt = q_ref[h, r0 : r0 + tile, :]
-            dt = d_ref[h, r0 : r0 + tile, :]
-            kt = w_ref[0, k0 : k0 + reach, :]
-            vt = w_ref[1, k0 : k0 + reach, :]
-            starts = s_ref[r0 : r0 + tile, :]
-            row = r0 + lax.broadcasted_iota(jnp.int32, (tile, reach), 0)
-            col = k0 + lax.broadcasted_iota(jnp.int32, (tile, reach), 1)
-            visible = (col >= starts) & (col <= row + WIN * rows)
-            scores = lax.dot_general(qt, kt, contract_last, preferred_element_type=f32) * scale
-            top = jnp.max(jnp.where(visible, scores, -1e30), axis=1, keepdims=True)
-            expo = jnp.where(visible, jnp.exp(scores - top), 0.0)
-            prob = expo / jnp.sum(expo, axis=1, keepdims=True)
-            prob_low = prob.astype(jnp.bfloat16)
-            attended = jnp.dot(prob_low, vt, preferred_element_type=f32)
-            delta = jnp.sum(dt.astype(f32) * attended, axis=1, keepdims=True)
-            dprob = lax.dot_general(dt, vt, contract_last, preferred_element_type=f32)
-            dscore = (prob * (dprob - delta)).astype(jnp.bfloat16)
-            dq = jnp.dot(dscore, kt, preferred_element_type=f32) * scale
-            dq_ref[h, r0 : r0 + tile, :] = dq.astype(dq_ref.dtype)
-            dk_acc[k0 : k0 + reach, :] += lax.dot_general(dscore, qt, contract_first, preferred_element_type=f32)
-            dv_acc[k0 : k0 + reach, :] += lax.dot_general(prob_low, dt, contract_first, preferred_element_type=f32)
+            short = f_ref[t] == 1
+
+            @pl.when(short)
+            def _():
+                tile_grads(h, r0, k0 + skip, reach - skip)
+
+            @pl.when(jnp.logical_not(short))
+            def _():
+                tile_grads(h, r0, k0, reach)
+
     piece = t_ref.shape[4]
     for w in range(t_ref.shape[0]):
         for c in range(rows // piece):
@@ -219,6 +233,11 @@
     span = window.shape[1]
     f32 = jnp.float32
     piece = rows // parts
+    tile = 128
+    reach = min(span, WIN * rows + tile)
+    firsts = jnp.arange(0, rows, tile, dtype=jnp.int32)
+    lowest = jnp.minimum(firsts, span - reach)
+    flags = (starts[firsts, 0] >= lowest + rows).astype(jnp.int32)
     vmem = pl.BlockSpec(memory_space=pltpu.VMEM)
     return pl.pallas_call(
         attention_kernel,
@@ -226,10 +245,10 @@
             jax.ShapeDtypeStruct(q.shape, q.dtype),
             jax.ShapeDtypeStruct((span // rows, 2, 2, 2, piece, 2 * width), f32),
         ),
-        in_specs=[vmem] * 4,
+        in_specs=[pl.BlockSpec(memory_space=pltpu.SMEM)] + [vmem] * 4,
         out_specs=(vmem, vmem),
         scratch_shapes=[pltpu.VMEM((span, width), f32), pltpu.VMEM((span, width), f32)],
-    )(q, dout, window, starts)
+    )(flags, q, dout, window, starts)
 
 
 def local_grads(q, dout, starts, kwin, value_window, qpos, kpos):

time: 72.5 us -> 73 us (level)
  the two profiles are of different devices: /device:TPU:15 before, /device:TPU:13 now
where the time goes in v9:
time: 73 us; the launch traced here: 72.6 us
  Pallas kernels  33.6 us (46%)
  waiting for transfers between devices  18.6 us (25%)
  starting transfers between devices  9.77 us (13%)
  local copies, waits for them, and re-layouts  5.93 us (8%)
  other arithmetic  4.04 us (6%)
    pallas_call x1, Pallas kernels, grad_reduce(): pl.pallas_call(grad_reduce_kernel, out_shape=jax.ShapeDtypeStruct(rest, f...  22 us
    ppermute x1, waiting for transfers between devices, nearest_next(): return lax.ppermute(block, ('dcn', 'blk', 'head'), route)  18.2 us
    pallas_call x1, Pallas kernels, attention(): pl.pallas_call(attention_kernel, out_shape=(jax.ShapeDtypeStruct(q.shape,...  11.5 us
    ppermute x1, starting transfers between devices, nearest_next(): return lax.ppermute(block, ('dcn', 'blk', 'head'), route)  5.77 us
    ppermute x1, starting transfers between devices, from_behind(): return lax.ppermute(block, axis, route)  4 us
    unnamed x5, local copies, waits for them, and re-layouts  1.93 us
    transpose x1, local copies, waits for them, and re-layouts, body(): jnp.transpose(out_grad, (1, 0, 2))  1.89 us
  transfers between devices with their start and end apart: 2, of which 2 were waited for; matrix products, arithmetic and copies ran while one was open for 6% of the time, Pallas kernels for 0%

profile of v9, /device:TPU:13, one launch (start us, length us, event | category | flops | bytes accessed | tf_op | source)
XLA Modules:
  0.0 72.6 jit_solution(16671443502449234815)
XLA Ops:
  0.6 0.0 copy-start
  0.6 0.0 copy-start.1
  0.7 1.0 %pad_maximum_fusion = bf16[2,512,128]{2,1,0:T(8,128)(2,1)S(1)} fusion(bf16[1,512,128]{2,1,0:T(8,128)(2,1)} %bitcast.12, bf16[1,512,128]{2,1,0:T(8,128)(2,1)} %bitcast.14), kind=kLoop, calls=%fused_computation.2 | loop fusion | flops 131072 | bytes 524288 | tf_op jit(solution)/shard_map/stack | solution.py:282
  1.7 5.8 %collective-permute-start.1 = (bf16[2,512,128]{2,1,0:T(8,128)(2,1)S(1)}, bf16[2,512,128]{2,1,0:T(8,128)(2,1)S(1)}, u32[]{:S(2)}, u32[]{:S(2)}) collective-permute-start(bf16[2,512,128]{2,1,0:T(8,128)(2,1)S(1)} %pad_maximum_fusion), channel_id=1, source_target_pairs={{0,14},{1,15},{2,12},{3,13},{4,10},{5,11},{6,8},{7,9},{8,22},{9,23... | collective-permute-start | bytes 786440 | tf_op jit(solution)/shard_map/ppermute | solution.py:30
  7.5 4.0 %collective-permute-start = (bf16[2,512,128]{2,1,0:T(8,128)(2,1)S(1)}, bf16[2,512,128]{2,1,0:T(8,128)(2,1)S(1)}, u32[]{:S(2)}, u32[]{:S(2)}) collective-permute-start(bf16[2,512,128]{2,1,0:T(8,128)(2,1)S(1)} %pad_maximum_fusion), channel_id=1, source_target_pairs={{0,16},{8,24},{16,32},{24,40},{32,48},{40,56},{48,64},{56,72},{64,... | collective-permute-start | bytes 786440 | tf_op jit(solution)/shard_map/ppermute | solution.py:14
  11.5 0.7 broadcast_subtract_fusion
  12.2 0.6 gather_fusion
  12.8 0.5 compare_convert_fusion.f_ref
  13.3 0.9 %copy.18.s_ref = s32[512,1]{1,0:T(8,128)} copy(s32[512,1]{0,1:T(1,128)S(1)} %bitcast.11) | data formatting | bytes 4096 | tf_op jit(solution)/shard_map/reshape | solution.py:297
  14.2 1.9 %copy_bitcast_fusion = (bf16[2,512,128]{2,1,0:T(8,128)(2,1)}, bf16[2,512,128]{2,1,0:T(8,128)(2,1)}) fusion(bf16[512,2,128]{2,1,0:T(2,128)(2,1)} %param.8, bf16[512,2,128]{2,1,0:T(2,128)(2,1)} %param.5), kind=kLoop, calls=%fused_computation.3 | loop fusion | bytes 1048576 | tf_op jit(solution)/shard_map/transpose | solution.py:300
  16.1 18.2 %collective-permute-done.1 = bf16[2,512,128]{2,1,0:T(8,128)(2,1)S(1)} collective-permute-done((bf16[2,512,128]{2,1,0:T(8,128)(2,1)S(1)}, bf16[2,512,128]{2,1,0:T(8,128)(2,1)S(1)}, u32[]{:S(2)}, u32[]{:S(2)}) %collective-permute-start.1) | collective-permute-done | bytes 262176 | tf_op jit(solution)/shard_map/ppermute | solution.py:30
  34.3 0.4 collective-permute-done
  34.7 0.0 copy-done
  34.7 0.0 copy-done.1
  34.7 0.9 %maximum_maximum_fusion.w_ref = bf16[2,1536,128]{2,1,0:T(8,128)(2,1)} fusion(bf16[1,512,128]{2,1,0:T(8,128)(2,1)S(1)} %bitcast.13, bf16[1,512,128]{2,1,0:T(8,128)(2,1)S(1)} %bitcast.15, bf16[2,512,128]{2,1,0:T(8,128)(2,1)S(1)} %collective-permute-done.1, bf16[2,512,128]{2,1,0:T(8,128)(2,1)S(1)} %collective-permute-done), kind=kLoop, calls=%fused_computation.1 | loop fusion | flops 3145728 | bytes 1572864 | tf_op jit(solution)/shard_map/concatenate | solution.py:290
  35.6 11.5 %shard_map.76 = (bf16[2,512,128]{2,1,0:T(8,128)(2,1)}, f32[3,2,2,2,64,256]{5,4,3,2,1,0:T(8,128)}) custom-call(s32[4]{0:T(128)} %compare_convert_fusion.f_ref, bf16[2,512,128]{2,1,0:T(8,128)(2,1)} %get-tuple-element.19.q_ref, bf16[2,512,128]{2,1,0:T(8,128)(2,1)} %get-tuple-element.18.d_ref, bf16[2,1536,128]{2,1,0:T(8,128)(2,1)} %maximum_maximum_fusion.w_ref, ...), custom_call_target="tpu_custom_call" | custom-call | tf_op jit(solution)/shard_map/pallas_call | solution.py:242
  47.2 1.9 %copy.19 = bf16[512,2,128]{2,1,0:T(2,128)(2,1)} copy(bf16[512,2,128]{2,0,1:T(8,128)(2,1)} %bitcast.16) | data formatting | bytes 524288
  49.1 22.0 %shard_map.77 = f32[64,256]{1,0:T(8,128)} custom-call(f32[3,2,2,2,64,256]{5,4,3,2,1,0:T(8,128)} %get-tuple-element.6.x_ref), custom_call_target="tpu_custom_call" | custom-call | tf_op jit(solution)/shard_map/pallas_call | solution.py:149
  71.1 0.8 %convert.4 = bf16[64,256]{1,0:T(8,128)(2,1)S(1)} convert(f32[64,256]{1,0:T(8,128)} %shard_map.77) | non-fusion elementwise | flops 16384 | bytes 98304 | tf_op jit(solution)/shard_map/convert.1
  72.0 0.6 fusion.3
  (1 shorter events, 0.0 us)
Async XLA Ops:
  0.6 34.1 %copy-start = (bf16[512,128]{1,0:T(8,128)(2,1)S(1)}, bf16[512,128]{1,0:T(8,128)(2,1)}, u32[]{:S(2)}) copy-start(bf16[512,128]{1,0:T(8,128)(2,1)} %param.7) | copy-start | bytes 393220
  0.6 34.1 %copy-start.1 = (bf16[512,128]{1,0:T(8,128)(2,1)S(1)}, bf16[512,128]{1,0:T(8,128)(2,1)}, u32[]{:S(2)}) copy-start(bf16[512,128]{1,0:T(8,128)(2,1)} %param.6) | copy-start | bytes 393220
  1.7 32.6 %collective-permute-start.1 = (bf16[2,512,128]{2,1,0:T(8,128)(2,1)S(1)}, bf16[2,512,128]{2,1,0:T(8,128)(2,1)S(1)}, u32[]{:S(2)}, u32[]{:S(2)}) collective-permute-start(bf16[2,512,128]{2,1,0:T(8,128)(2,1)S(1)} %pad_maximum_fusion), channel_id=1, source_target_pairs={{0,14},{1,15},{2,12},{3,13},{4,10},{5,11},{6,8},{7,9},{8,22},{9,23... | collective-permute-start | bytes 786440 | tf_op jit(solution)/shard_map/ppermute | solution.py:30
  7.5 27.2 %collective-permute-start = (bf16[2,512,128]{2,1,0:T(8,128)(2,1)S(1)}, bf16[2,512,128]{2,1,0:T(8,128)(2,1)S(1)}, u32[]{:S(2)}, u32[]{:S(2)}) collective-permute-start(bf16[2,512,128]{2,1,0:T(8,128)(2,1)S(1)} %pad_maximum_fusion), channel_id=1, source_target_pairs={{0,16},{8,24},{16,32},{24,40},{32,48},{40,56},{48,64},{56,72},{64,... | collective-permute-start | bytes 786440 | tf_op jit(solution)/shard_map/ppermute | solution.py:14

commit v10 on v8

--- a/solution.py
+++ b/solution.py
@@ -109,7 +109,7 @@
         for w in range(windows):
             copies[stage][w].wait_recv()
             arrived = targets[stage][w].astype(jnp.float32)
-            summed = kept[stage][w, keep_bit(stage, w)] + arrived
+            summed = kept[stage][w, keep_bit(stage, w)].astype(jnp.float32) + arrived
             if stage < 2:
                 kept[stage + 1][w] = summed
                 away = kept[stage + 1][w, 1 - keep_bit(stage + 1, w)]
@@ -152,7 +152,7 @@
         in_specs=[pl.BlockSpec(memory_space=pltpu.VMEM)],
         out_specs=pl.BlockSpec(memory_space=pltpu.VMEM),
         scratch_shapes=[
-            pltpu.VMEM((windows, 2, 2) + rest, f32),
+            pltpu.VMEM((windows, 2, 2) + rest, link),
             pltpu.VMEM((windows, 2) + rest, link),
             pltpu.VMEM((windows,) + rest, link),
             pltpu.VMEM((windows, 2, 2) + rest, f32),
@@ -210,8 +210,9 @@
         for c in range(rows // piece):
             first = w * rows + c * piece
             place = (w, c % 2, (c // 2) % 2, c // 4)
-            t_ref[place + (slice(None), slice(0, width))] = dk_acc[first : first + piece, :] * scale
-            t_ref[place + (slice(None), slice(width, 2 * width))] = dv_acc[first : first + piece, :]
+            dk = dk_acc[first : first + piece, :] * scale
+            t_ref[place + (slice(None), slice(0, width))] = dk.astype(t_ref.dtype)
+            t_ref[place + (slice(None), slice(width, 2 * width))] = dv_acc[first : first + piece, :].astype(t_ref.dtype)
 
 
 def attention(q, dout, window, starts, parts):
@@ -224,7 +225,7 @@
         attention_kernel,
         out_shape=(
             jax.ShapeDtypeStruct(q.shape, q.dtype),
-            jax.ShapeDtypeStruct((span // rows, 2, 2, 2, piece, 2 * width), f32),
+            jax.ShapeDtypeStruct((span // rows, 2, 2, 2, piece, 2 * width), jnp.bfloat16),
         ),
         in_specs=[vmem] * 4,
         out_specs=(vmem, vmem),

time: 72.5 us -> 72.2 us (level)
  local copies, waits for them, and re-layouts: 5.3 us -> 4.28 us
  waiting for transfers between devices: 20.1 us -> 21.1 us
    transpose x1, local copies, waits for them, and re-layouts: 1.89 us -> 0.85 us  [body(): jnp.transpose(out_grad, (1, 0, 2))]
    ppermute x1, waiting for transfers between devices: 19.7 us -> 20.7 us  [nearest_next(): return lax.ppermute(block, ('dcn', 'blk', 'head'), route)]
    unnamed x5 -> x9, local copies, waits for them, and re-layouts: 1.93 us -> 1.94 us
  transfers between devices with their start and end apart: 2 -> 2, of which waited for: 2 -> 2; matrix products, arithmetic and copies ran while one was open for 5% -> 3% of each run, Pallas kernels for 0% -> 0%
where the time goes in v10:
time: 72.2 us; the launch traced here: 71.9 us
  Pallas kernels  32.4 us (45%)
  waiting for transfers between devices  21.1 us (29%)
  starting transfers between devices  9.9 us (14%)
  local copies, waits for them, and re-layouts  4.28 us (6%)
  other arithmetic  3.54 us (5%)
    pallas_call x1, Pallas kernels, grad_reduce(): pl.pallas_call(grad_reduce_kernel, out_shape=jax.ShapeDtypeStruct(rest, f...  21.7 us
    ppermute x1, waiting for transfers between devices, nearest_next(): return lax.ppermute(block, ('dcn', 'blk', 'head'), route)  20.7 us
    pallas_call x1, Pallas kernels, attention(): pl.pallas_call(attention_kernel, out_shape=(jax.ShapeDtypeStruct(q.shape,...  10.6 us
    ppermute x1, starting transfers between devices, nearest_next(): return lax.ppermute(block, ('dcn', 'blk', 'head'), route)  5.9 us
    ppermute x1, starting transfers between devices, from_behind(): return lax.ppermute(block, axis, route)  4 us
    unnamed x9, local copies, waits for them, and re-layouts  1.94 us
  transfers between devices with their start and end apart: 2, of which 2 were waited for; matrix products, arithmetic and copies ran while one was open for 3% of the time, Pallas kernels for 0%

profile of v10, /device:TPU:15, one launch (start us, length us, event | category | flops | bytes accessed | tf_op | source)
XLA Modules:
  0.0 71.9 jit_solution(10900579633693884272)
XLA Ops:
  0.6 0.0 copy-start.2
  0.6 0.0 copy-start.3
  0.6 1.1 %pad_maximum_fusion = bf16[2,512,128]{2,1,0:T(8,128)(2,1)S(1)} fusion(bf16[1,512,128]{2,1,0:T(8,128)(2,1)} %bitcast.8, bf16[1,512,128]{2,1,0:T(8,128)(2,1)} %bitcast.10), kind=kLoop, calls=%fused_computation.1 | loop fusion | flops 131072 | bytes 524288 | tf_op jit(solution)/shard_map/stack | solution.py:264
  1.7 0.0 copy-start
  1.7 0.0 copy-start.1
  1.7 5.9 %collective-permute-start.1 = (bf16[2,512,128]{2,1,0:T(8,128)(2,1)S(1)}, bf16[2,512,128]{2,1,0:T(8,128)(2,1)S(1)}, u32[]{:S(2)}, u32[]{:S(2)}) collective-permute-start(bf16[2,512,128]{2,1,0:T(8,128)(2,1)S(1)} %pad_maximum_fusion), channel_id=1, source_target_pairs={{0,14},{1,15},{2,12},{3,13},{4,10},{5,11},{6,8},{7,9},{8,22},{9,23... | collective-permute-start | bytes 786440 | tf_op jit(solution)/shard_map/ppermute | solution.py:30
  7.6 4.0 %collective-permute-start = (bf16[2,512,128]{2,1,0:T(8,128)(2,1)S(1)}, bf16[2,512,128]{2,1,0:T(8,128)(2,1)S(1)}, u32[]{:S(2)}, u32[]{:S(2)}) collective-permute-start(bf16[2,512,128]{2,1,0:T(8,128)(2,1)S(1)} %pad_maximum_fusion), channel_id=1, source_target_pairs={{0,16},{8,24},{16,32},{24,40},{32,48},{40,56},{48,64},{56,72},{64,... | collective-permute-start | bytes 786440 | tf_op jit(solution)/shard_map/ppermute | solution.py:14
  11.7 0.7 broadcast_subtract_fusion
  12.3 0.9 %copy.13.s_ref = s32[512,1]{1,0:T(8,128)} copy(s32[512,1]{0,1:T(1,128)S(1)} %bitcast.13) | data formatting | bytes 4096 | tf_op jit(solution)/shard_map/reshape | solution.py:279
  13.2 0.0 copy-done.2
  13.2 0.0 copy-done.3
  13.2 0.8 %copy_bitcast_fusion = (bf16[2,512,128]{2,1,0:T(8,128)(2,1)}, bf16[2,512,128]{2,1,0:T(8,128)(2,1)}) fusion(bf16[512,2,128]{2,1,0:T(2,128)(2,1)S(1)} %copy-done.2, bf16[512,2,128]{2,1,0:T(2,128)(2,1)S(1)} %copy-done.3), kind=kLoop, calls=%fused_computation.2 | loop fusion | bytes 1048576 | tf_op jit(solution)/shard_map/transpose | solution.py:282
  14.1 20.7 %collective-permute-done.1 = bf16[2,512,128]{2,1,0:T(8,128)(2,1)S(1)} collective-permute-done((bf16[2,512,128]{2,1,0:T(8,128)(2,1)S(1)}, bf16[2,512,128]{2,1,0:T(8,128)(2,1)S(1)}, u32[]{:S(2)}, u32[]{:S(2)}) %collective-permute-start.1) | collective-permute-done | bytes 262176 | tf_op jit(solution)/shard_map/ppermute | solution.py:30
  34.8 0.4 collective-permute-done
  35.2 0.0 copy-done
  35.2 0.0 copy-done.1
  35.2 1.0 %maximum_maximum_fusion.w_ref = bf16[2,1536,128]{2,1,0:T(8,128)(2,1)} fusion(bf16[1,512,128]{2,1,0:T(8,128)(2,1)S(1)} %bitcast.9, bf16[1,512,128]{2,1,0:T(8,128)(2,1)S(1)} %bitcast.11, bf16[2,512,128]{2,1,0:T(8,128)(2,1)S(1)} %collective-permute-done.1, bf16[2,512,128]{2,1,0:T(8,128)(2,1)S(1)} %collective-permute-done), kind=kLoop, calls=%fused_computation | loop fusion | flops 3145728 | bytes 1572864 | tf_op jit(solution)/shard_map/concatenate | solution.py:272
  36.1 10.6 %shard_map.76 = (bf16[2,512,128]{2,1,0:T(8,128)(2,1)}, bf16[3,2,2,2,64,256]{5,4,3,2,1,0:T(8,128)(2,1)}) custom-call(bf16[2,512,128]{2,1,0:T(8,128)(2,1)} %get-tuple-element.16.q_ref, bf16[2,512,128]{2,1,0:T(8,128)(2,1)} %get-tuple-element.15.d_ref, bf16[2,1536,128]{2,1,0:T(8,128)(2,1)} %maximum_maximum_fusion.w_ref, s32[512,1]{1,0:T(8,128)} %copy.13.s_ref), custom_call_target="tpu_custom_call" | custom-call | tf_op jit(solution)/shard_map/pallas_call | solution.py:224
  46.8 1.9 %copy.14 = bf16[512,2,128]{2,1,0:T(2,128)(2,1)} copy(bf16[512,2,128]{2,0,1:T(8,128)(2,1)} %bitcast.12) | data formatting | bytes 524288
  48.7 21.7 %shard_map.77 = f32[64,256]{1,0:T(8,128)} custom-call(bf16[3,2,2,2,64,256]{5,4,3,2,1,0:T(8,128)(2,1)} %get-tuple-element.6.x_ref), custom_call_target="tpu_custom_call" | custom-call | tf_op jit(solution)/shard_map/pallas_call | solution.py:149
  70.4 0.8 %convert.4 = bf16[64,256]{1,0:T(8,128)(2,1)S(1)} convert(f32[64,256]{1,0:T(8,128)} %shard_map.77) | non-fusion elementwise | flops 16384 | bytes 98304 | tf_op jit(solution)/shard_map/convert.1
  71.3 0.6 fusion
Async XLA Ops:
  0.6 12.6 %copy-start.2 = (bf16[512,2,128]{2,1,0:T(2,128)(2,1)S(1)}, bf16[512,2,128]{2,1,0:T(2,128)(2,1)}, u32[]{:S(2)}) copy-start(bf16[512,2,128]{2,1,0:T(2,128)(2,1)} %param.8) | copy-start | bytes 786436
  0.6 12.6 %copy-start.3 = (bf16[512,2,128]{2,1,0:T(2,128)(2,1)S(1)}, bf16[512,2,128]{2,1,0:T(2,128)(2,1)}, u32[]{:S(2)}) copy-start(bf16[512,2,128]{2,1,0:T(2,128)(2,1)} %param.5) | copy-start | bytes 786436
  1.7 33.5 %copy-start = (bf16[512,128]{1,0:T(8,128)(2,1)S(1)}, bf16[512,128]{1,0:T(8,128)(2,1)}, u32[]{:S(2)}) copy-start(bf16[512,128]{1,0:T(8,128)(2,1)} %param.7) | copy-start | bytes 393220
  1.7 33.4 %copy-start.1 = (bf16[512,128]{1,0:T(8,128)(2,1)S(1)}, bf16[512,128]{1,0:T(8,128)(2,1)}, u32[]{:S(2)}) copy-start(bf16[512,128]{1,0:T(8,128)(2,1)} %param.6) | copy-start | bytes 393220
  1.7 33.0 %collective-permute-start.1 = (bf16[2,512,128]{2,1,0:T(8,128)(2,1)S(1)}, bf16[2,512,128]{2,1,0:T(8,128)(2,1)S(1)}, u32[]{:S(2)}, u32[]{:S(2)}) collective-permute-start(bf16[2,512,128]{2,1,0:T(8,128)(2,1)S(1)} %pad_maximum_fusion), channel_id=1, source_target_pairs={{0,14},{1,15},{2,12},{3,13},{4,10},{5,11},{6,8},{7,9},{8,22},{9,23... | collective-permute-start | bytes 786440 | tf_op jit(solution)/shard_map/ppermute | solution.py:30
  7.6 27.5 %collective-permute-start = (bf16[2,512,128]{2,1,0:T(8,128)(2,1)S(1)}, bf16[2,512,128]{2,1,0:T(8,128)(2,1)S(1)}, u32[]{:S(2)}, u32[]{:S(2)}) collective-permute-start(bf16[2,512,128]{2,1,0:T(8,128)(2,1)S(1)} %pad_maximum_fusion), channel_id=1, source_target_pairs={{0,16},{8,24},{16,32},{24,40},{32,48},{40,56},{48,64},{56,72},{64,... | collective-permute-start | bytes 786440 | tf_op jit(solution)/shard_map/ppermute | solution.py:14

commit v11 on v10

--- a/solution.py
+++ b/solution.py
@@ -37,35 +37,44 @@
     head = lax.axis_index("head")
     per_dcn = lax.axis_size("blk")
     blocks = lax.axis_size("dcn") * per_dcn
-    parts = lax.axis_size("head")
     block = dcn * per_dcn + blk
     bits = [head % 2, (head // 2) % 2, (head // 4) % 2]
     partners = [head + 1 - 2 * bits[0], head + 2 - 4 * bits[1], head + 4 - 8 * bits[2]]
-    flipped = mirror(head, parts)
 
     def device(b, h):
         return (b // per_dcn, b % per_dcn, h)
 
-    back_heads = [flipped if w == WIN - 1 else head for w in range(WIN)]
+    def keep_bit(stage, w):
+        if stage > 0 and w == WIN - 1:
+            return 1 - bits[stage]
+        return bits[stage]
+
+    def owner(w, half):
+        return bits[0] + 2 * keep_bit(1, w) + 4 * half
+
+    def sender(w, slot):
+        second = bits[1] if w != WIN - 1 else 1 - bits[1]
+        return bits[0] + 2 * second + 4 * slot
+
     sends_back = [block >= WIN - w for w in range(WIN)]
     gets_back = [block + WIN - w < blocks for w in range(WIN)]
     barrier = pltpu.get_barrier_semaphore()
     for partner in partners:
         pl.semaphore_signal(barrier, 1, device_id=(dcn, blk, partner), device_id_type=mesh_id)
+    peers = len(partners)
     for w in range(WIN):
         distance = WIN - w
-
-        @pl.when(sends_back[w])
-        def _():
-            pl.semaphore_signal(barrier, 1, device_id=device(block - distance, back_heads[w]), device_id_type=mesh_id)
-
-        @pl.when(gets_back[w])
-        def _():
-            pl.semaphore_signal(barrier, 1, device_id=device(block + distance, back_heads[w]), device_id_type=mesh_id)
-
-    peers = len(partners)
-    for w in range(WIN):
-        peers = peers + sends_back[w].astype(jnp.int32) + gets_back[w].astype(jnp.int32)
+        for half in range(2):
+
+            @pl.when(sends_back[w])
+            def _():
+                pl.semaphore_signal(barrier, 1, device_id=device(block - distance, owner(w, half)), device_id_type=mesh_id)
+
+            @pl.when(gets_back[w])
+            def _():
+                pl.semaphore_signal(barrier, 1, device_id=device(block + distance, sender(w, half)), device_id_type=mesh_id)
+
+        peers = peers + 2 * sends_back[w].astype(jnp.int32) + 2 * gets_back[w].astype(jnp.int32)
     pl.semaphore_wait(barrier, peers)
 
     windows = x_ref.shape[0]
@@ -73,11 +82,6 @@
     outgoing = [None, t1, t2]
     targets = [r1, r2, r3]
     copies = [[None] * windows for _ in range(3)]
-
-    def keep_bit(stage, w):
-        if stage > 0 and w == WIN - 1:
-            return 1 - bits[stage]
-        return bits[stage]
 
     def send(stage, w):
         keep = keep_bit(stage, w)
@@ -93,53 +97,60 @@
         copy.start()
         copies[stage][w] = copy
 
-    def back_copy(w, b):
+    def back_copy(w, half, slot, target):
         return pltpu.make_async_remote_copy(
-            src_ref=a3.at[w],
-            dst_ref=back.at[w],
-            send_sem=sends.at[3, w],
-            recv_sem=recvs.at[3, w],
-            device_id=device(b, back_heads[w]),
+            src_ref=a3.at[w, half],
+            dst_ref=back.at[w, slot],
+            send_sem=sends.at[3 + half, w],
+            recv_sem=recvs.at[3 + slot, w],
+            device_id=target,
             device_id_type=mesh_id,
         )
 
+    def outgoing_back(w, half):
+        return back_copy(w, half, bits[2], device(block - (WIN - w), owner(w, half)))
+
     for w in range(windows):
         send(0, w)
-    for stage in range(3):
+    for stage in range(2):
         for w in range(windows):
             copies[stage][w].wait_recv()
             arrived = targets[stage][w].astype(jnp.float32)
             summed = kept[stage][w, keep_bit(stage, w)].astype(jnp.float32) + arrived
-            if stage < 2:
-                kept[stage + 1][w] = summed
+            kept[stage + 1][w] = summed
+            if stage == 1 and w < WIN:
+                a3[w] = summed.astype(a3.dtype)
+                for half in range(2):
+
+                    @pl.when(sends_back[w])
+                    def _():
+                        outgoing_back(w, half).start()
+
+            else:
                 away = kept[stage + 1][w, 1 - keep_bit(stage + 1, w)]
                 outgoing[stage + 1][w] = away.astype(outgoing[stage + 1].dtype)
                 send(stage + 1, w)
-            elif w < WIN:
-                a3[w] = summed.astype(a3.dtype)
-
-                @pl.when(sends_back[w])
-                def _():
-                    back_copy(w, block - (WIN - w)).start()
-
-            else:
-                total[...] = summed
+    copies[2][WIN].wait_recv()
+    total[...] = a2[WIN, bits[2]] + r3[WIN].astype(jnp.float32)
     for w in range(WIN - 1, -1, -1):
-
-        @pl.when(gets_back[w])
-        def _():
-            back_copy(w, block + WIN - w).wait_recv()
-            total[...] = total[...] + back[w].astype(jnp.float32)
+        for slot in range(2):
+
+            @pl.when(gets_back[w])
+            def _():
+                back_copy(w, 0, slot, device(block + WIN - w, sender(w, slot))).wait_recv()
+                total[...] = total[...] + back[w, slot].astype(jnp.float32)
 
     o_ref[...] = total[...]
     for stage in range(3):
         for w in range(windows):
-            copies[stage][w].wait_send()
+            if copies[stage][w] is not None:
+                copies[stage][w].wait_send()
     for w in range(WIN):
-
-        @pl.when(sends_back[w])
-        def _():
-            back_copy(w, block - (WIN - w)).wait_send()
+        for half in range(2):
+
+            @pl.when(sends_back[w])
+            def _():
+                outgoing_back(w, half).wait_send()
 
 
 def grad_reduce(chunks, width, dtype):
@@ -159,11 +170,11 @@
             pltpu.VMEM((windows, 2) + rest, f32),
             pltpu.VMEM((windows, 2) + rest, link),
             pltpu.VMEM((windows,) + rest, link),
-            pltpu.VMEM((WIN,) + rest, link),
+            pltpu.VMEM((WIN, 2) + rest, link),
             pltpu.VMEM(rest, f32),
-            pltpu.VMEM((WIN,) + rest, link),
-            pltpu.SemaphoreType.DMA((4, windows)),
-            pltpu.SemaphoreType.DMA((4, windows)),
+            pltpu.VMEM((WIN, 2) + rest, link),
+            pltpu.SemaphoreType.DMA((5, windows)),
+            pltpu.SemaphoreType.DMA((5, windows)),
         ],
         compiler_params=pltpu.CompilerParams(collective_id=0, has_side_effects=True),
     )(chunks)

time: 72.2 us -> 71.5 us (level)
  the two profiles are of different devices: /device:TPU:15 before, /device:TPU:23 now
where the time goes in v11:
time: 71.5 us; the launch traced here: 71.1 us
  Pallas kernels  31.9 us (45%)
  waiting for transfers between devices  21 us (29%)
  starting transfers between devices  9.67 us (14%)
  local copies, waits for them, and re-layouts  4.28 us (6%)
  other arithmetic  3.54 us (5%)
    pallas_call x1, Pallas kernels, grad_reduce(): pl.pallas_call(grad_reduce_kernel, out_shape=jax.ShapeDtypeStruct(rest, f...  21.3 us
    ppermute x1, waiting for transfers between devices, nearest_next(): return lax.ppermute(block, ('dcn', 'blk', 'head'), route)  20.8 us
    pallas_call x1, Pallas kernels, attention(): pl.pallas_call(attention_kernel, out_shape=(jax.ShapeDtypeStruct(q.shape,...  10.6 us
    ppermute x1, starting transfers between devices, nearest_next(): return lax.ppermute(block, ('dcn', 'blk', 'head'), route)  5.67 us
    ppermute x1, starting transfers between devices, from_behind(): return lax.ppermute(block, axis, route)  4 us
    unnamed x9, local copies, waits for them, and re-layouts  1.94 us
  transfers between devices with their start and end apart: 2, of which 2 were waited for; matrix products, arithmetic and copies ran while one was open for 3% of the time, Pallas kernels for 0%

profile of v11, /device:TPU:23, one launch (start us, length us, event | category | flops | bytes accessed | tf_op | source)
XLA Modules:
  0.0 71.1 jit_solution(5319452236220506797)
XLA Ops:
  0.6 0.0 copy-start.2
  0.6 0.0 copy-start.3
  0.6 1.1 %pad_maximum_fusion = bf16[2,512,128]{2,1,0:T(8,128)(2,1)S(1)} fusion(bf16[1,512,128]{2,1,0:T(8,128)(2,1)} %bitcast.8, bf16[1,512,128]{2,1,0:T(8,128)(2,1)} %bitcast.10), kind=kLoop, calls=%fused_computation.1 | loop fusion | flops 131072 | bytes 524288 | tf_op jit(solution)/shard_map/stack | solution.py:275
  1.7 0.0 copy-start
  1.7 0.0 copy-start.1
  1.7 5.7 %collective-permute-start.1 = (bf16[2,512,128]{2,1,0:T(8,128)(2,1)S(1)}, bf16[2,512,128]{2,1,0:T(8,128)(2,1)S(1)}, u32[]{:S(2)}, u32[]{:S(2)}) collective-permute-start(bf16[2,512,128]{2,1,0:T(8,128)(2,1)S(1)} %pad_maximum_fusion), channel_id=1, source_target_pairs={{0,14},{1,15},{2,12},{3,13},{4,10},{5,11},{6,8},{7,9},{8,22},{9,23... | collective-permute-start | bytes 786440 | tf_op jit(solution)/shard_map/ppermute | solution.py:30
  7.4 4.0 %collective-permute-start = (bf16[2,512,128]{2,1,0:T(8,128)(2,1)S(1)}, bf16[2,512,128]{2,1,0:T(8,128)(2,1)S(1)}, u32[]{:S(2)}, u32[]{:S(2)}) collective-permute-start(bf16[2,512,128]{2,1,0:T(8,128)(2,1)S(1)} %pad_maximum_fusion), channel_id=1, source_target_pairs={{0,16},{8,24},{16,32},{24,40},{32,48},{40,56},{48,64},{56,72},{64,... | collective-permute-start | bytes 786440 | tf_op jit(solution)/shard_map/ppermute | solution.py:14
  11.4 0.7 broadcast_subtract_fusion
  12.1 0.9 %copy.13.s_ref = s32[512,1]{1,0:T(8,128)} copy(s32[512,1]{0,1:T(1,128)S(1)} %bitcast.13) | data formatting | bytes 4096 | tf_op jit(solution)/shard_map/reshape | solution.py:290
  13.0 0.0 copy-done.2
  13.0 0.0 copy-done.3
  13.0 0.8 %copy_bitcast_fusion = (bf16[2,512,128]{2,1,0:T(8,128)(2,1)}, bf16[2,512,128]{2,1,0:T(8,128)(2,1)}) fusion(bf16[512,2,128]{2,1,0:T(2,128)(2,1)S(1)} %copy-done.2, bf16[512,2,128]{2,1,0:T(2,128)(2,1)S(1)} %copy-done.3), kind=kLoop, calls=%fused_computation.2 | loop fusion | bytes 1048576 | tf_op jit(solution)/shard_map/transpose | solution.py:293
  13.8 20.8 %collective-permute-done.1 = bf16[2,512,128]{2,1,0:T(8,128)(2,1)S(1)} collective-permute-done((bf16[2,512,128]{2,1,0:T(8,128)(2,1)S(1)}, bf16[2,512,128]{2,1,0:T(8,128)(2,1)S(1)}, u32[]{:S(2)}, u32[]{:S(2)}) %collective-permute-start.1) | collective-permute-done | bytes 262176 | tf_op jit(solution)/shard_map/ppermute | solution.py:30
  34.6 0.2 collective-permute-done
  34.8 0.0 copy-done
  34.8 0.0 copy-done.1
  34.8 1.0 %maximum_maximum_fusion.w_ref = bf16[2,1536,128]{2,1,0:T(8,128)(2,1)} fusion(bf16[1,512,128]{2,1,0:T(8,128)(2,1)S(1)} %bitcast.9, bf16[1,512,128]{2,1,0:T(8,128)(2,1)S(1)} %bitcast.11, bf16[2,512,128]{2,1,0:T(8,128)(2,1)S(1)} %collective-permute-done.1, bf16[2,512,128]{2,1,0:T(8,128)(2,1)S(1)} %collective-permute-done), kind=kLoop, calls=%fused_computation | loop fusion | flops 3145728 | bytes 1572864 | tf_op jit(solution)/shard_map/concatenate | solution.py:283
  35.8 10.6 %shard_map.76 = (bf16[2,512,128]{2,1,0:T(8,128)(2,1)}, bf16[3,2,2,2,64,256]{5,4,3,2,1,0:T(8,128)(2,1)}) custom-call(bf16[2,512,128]{2,1,0:T(8,128)(2,1)} %get-tuple-element.16.q_ref, bf16[2,512,128]{2,1,0:T(8,128)(2,1)} %get-tuple-element.15.d_ref, bf16[2,1536,128]{2,1,0:T(8,128)(2,1)} %maximum_maximum_fusion.w_ref, s32[512,1]{1,0:T(8,128)} %copy.13.s_ref), custom_call_target="tpu_custom_call" | custom-call | tf_op jit(solution)/shard_map/pallas_call | solution.py:235
  46.4 1.9 %copy.14 = bf16[512,2,128]{2,1,0:T(2,128)(2,1)} copy(bf16[512,2,128]{2,0,1:T(8,128)(2,1)} %bitcast.12) | data formatting | bytes 524288
  48.3 21.3 %shard_map.77 = f32[64,256]{1,0:T(8,128)} custom-call(bf16[3,2,2,2,64,256]{5,4,3,2,1,0:T(8,128)(2,1)} %get-tuple-element.6.x_ref), custom_call_target="tpu_custom_call" | custom-call | tf_op jit(solution)/shard_map/pallas_call | solution.py:160
  69.6 0.8 %convert.4 = bf16[64,256]{1,0:T(8,128)(2,1)S(1)} convert(f32[64,256]{1,0:T(8,128)} %shard_map.77) | non-fusion elementwise | flops 16384 | bytes 98304 | tf_op jit(solution)/shard_map/convert.1
  70.5 0.6 fusion
Async XLA Ops:
  0.6 12.4 %copy-start.2 = (bf16[512,2,128]{2,1,0:T(2,128)(2,1)S(1)}, bf16[512,2,128]{2,1,0:T(2,128)(2,1)}, u32[]{:S(2)}) copy-start(bf16[512,2,128]{2,1,0:T(2,128)(2,1)} %param.8) | copy-start | bytes 786436
  0.6 12.3 %copy-start.3 = (bf16[512,2,128]{2,1,0:T(2,128)(2,1)S(1)}, bf16[512,2,128]{2,1,0:T(2,128)(2,1)}, u32[]{:S(2)}) copy-start(bf16[512,2,128]{2,1,0:T(2,128)(2,1)} %param.5) | copy-start | bytes 786436
  1.7 33.1 %copy-start = (bf16[512,128]{1,0:T(8,128)(2,1)S(1)}, bf16[512,128]{1,0:T(8,128)(2,1)}, u32[]{:S(2)}) copy-start(bf16[512,128]{1,0:T(8,128)(2,1)} %param.7) | copy-start | bytes 393220
  1.7 33.1 %copy-start.1 = (bf16[512,128]{1,0:T(8,128)(2,1)S(1)}, bf16[512,128]{1,0:T(8,128)(2,1)}, u32[]{:S(2)}) copy-start(bf16[512,128]{1,0:T(8,128)(2,1)} %param.6) | copy-start | bytes 393220
  1.7 32.9 %collective-permute-start.1 = (bf16[2,512,128]{2,1,0:T(8,128)(2,1)S(1)}, bf16[2,512,128]{2,1,0:T(8,128)(2,1)S(1)}, u32[]{:S(2)}, u32[]{:S(2)}) collective-permute-start(bf16[2,512,128]{2,1,0:T(8,128)(2,1)S(1)} %pad_maximum_fusion), channel_id=1, source_target_pairs={{0,14},{1,15},{2,12},{3,13},{4,10},{5,11},{6,8},{7,9},{8,22},{9,23... | collective-permute-start | bytes 786440 | tf_op jit(solution)/shard_map/ppermute | solution.py:30
  7.4 27.4 %collective-permute-start = (bf16[2,512,128]{2,1,0:T(8,128)(2,1)S(1)}, bf16[2,512,128]{2,1,0:T(8,128)(2,1)S(1)}, u32[]{:S(2)}, u32[]{:S(2)}) collective-permute-start(bf16[2,512,128]{2,1,0:T(8,128)(2,1)S(1)} %pad_maximum_fusion), channel_id=1, source_target_pairs={{0,16},{8,24},{16,32},{24,40},{32,48},{40,56},{48,64},{56,72},{64,... | collective-permute-start | bytes 786440 | tf_op jit(solution)/shard_map/ppermute | solution.py:14

commit v12 on v11

--- a/solution.py
+++ b/solution.py
@@ -182,7 +182,8 @@
 
 
 def attention_kernel(q_ref, d_ref, w_ref, s_ref, dq_ref, t_ref, dk_acc, dv_acc):
-    heads, rows, width = q_ref.shape
+    rows, width = q_ref.shape[0], w_ref.shape[2]
+    heads = q_ref.shape[1] // width
     span = w_ref.shape[1]
     tile = 128
     reach = min(span, WIN * rows + tile)
@@ -195,8 +196,9 @@
     for h in range(heads):
         for r0 in range(0, rows, tile):
             k0 = min(r0, span - reach)
-            qt = q_ref[h, r0 : r0 + tile, :]
-            dt = d_ref[h, r0 : r0 + tile, :]
+            lanes = slice(h * width, (h + 1) * width)
+            qt = q_ref[r0 : r0 + tile, lanes]
+            dt = d_ref[r0 : r0 + tile, lanes]
             kt = w_ref[0, k0 : k0 + reach, :]
             vt = w_ref[1, k0 : k0 + reach, :]
             starts = s_ref[r0 : r0 + tile, :]
@@ -213,7 +215,7 @@
             dprob = lax.dot_general(dt, vt, contract_last, preferred_element_type=f32)
             dscore = (prob * (dprob - delta)).astype(jnp.bfloat16)
             dq = jnp.dot(dscore, kt, preferred_element_type=f32) * scale
-            dq_ref[h, r0 : r0 + tile, :] = dq.astype(dq_ref.dtype)
+            dq_ref[r0 : r0 + tile, lanes] = dq.astype(dq_ref.dtype)
             dk_acc[k0 : k0 + reach, :] += lax.dot_general(dscore, qt, contract_first, preferred_element_type=f32)
             dv_acc[k0 : k0 + reach, :] += lax.dot_general(prob_low, dt, contract_first, preferred_element_type=f32)
     piece = t_ref.shape[4]
@@ -227,7 +229,7 @@
 
 
 def attention(q, dout, window, starts, parts):
-    heads, rows, width = q.shape
+    rows, width = q.shape[0], window.shape[2]
     span = window.shape[1]
     f32 = jnp.float32
     piece = rows // parts
@@ -289,13 +291,13 @@
     window_start = first_position - WIN * rows
     starts = (doc_start - window_start).reshape(rows, 1)
     dq, chunks = attention(
-        jnp.transpose(queries, (1, 0, 2)),
-        jnp.transpose(out_grad, (1, 0, 2)),
+        queries.reshape(rows, -1),
+        out_grad.reshape(rows, -1),
         window,
         starts,
         parts,
     )
-    q_grad = jnp.transpose(dq, (1, 0, 2))
+    q_grad = dq.reshape(queries.shape)
     k_grad, v_grad = grad_reduce(chunks, window_width, jnp.bfloat16)
     return (q_grad, k_grad, v_grad)
 

time: 71.5 us -> 71.3 us (level)
    reshape x0 -> x2, local copies, waits for them, and re-layouts: none -> 2.57 us  [the longest x1 1.72 us: body(): q_grad = dq.reshape(queries.shape)]
    unnamed x9 -> x8, local copies, waits for them, and re-layouts: 1.94 us -> 0.02 us
    transpose x1 -> x0, local copies, waits for them, and re-layouts: 0.85 us -> none  [body(): jnp.transpose(out_grad, (1, 0, 2))]
where the time goes in v12:
time: 71.3 us; the launch traced here: 70.9 us
  Pallas kernels  31.9 us (45%)
  waiting for transfers between devices  21 us (29%)
  starting transfers between devices  9.67 us (14%)
  local copies, waits for them, and re-layouts  4.07 us (6%)
  other arithmetic  3.54 us (5%)
    pallas_call x1, Pallas kernels, grad_reduce(): pl.pallas_call(grad_reduce_kernel, out_shape=jax.ShapeDtypeStruct(rest, f...  21.3 us
    ppermute x1, waiting for transfers between devices, nearest_next(): return lax.ppermute(block, ('dcn', 'blk', 'head'), route)  20.8 us
    pallas_call x1, Pallas kernels, attention(): pl.pallas_call(attention_kernel, out_shape=(jax.ShapeDtypeStruct(q.shape,...  10.7 us
    ppermute x1, starting transfers between devices, nearest_next(): return lax.ppermute(block, ('dcn', 'blk', 'head'), route)  5.67 us
    ppermute x1, starting transfers between devices, from_behind(): return lax.ppermute(block, axis, route)  4 us
    reshape x1, local copies, waits for them, and re-layouts, body(): q_grad = dq.reshape(queries.shape)  1.72 us
  transfers between devices with their start and end apart: 2, of which 2 were waited for; matrix products, arithmetic and copies ran while one was open for 3% of the time, Pallas kernels for 0%

profile of v12, /device:TPU:23, one launch (start us, length us, event | category | flops | bytes accessed | tf_op | source)
XLA Modules:
  0.0 70.9 jit_solution(14917604765903731794)
XLA Ops:
  0.6 0.0 copy-start.2
  0.6 0.0 copy-start.3
  0.6 1.1 %pad_maximum_fusion = bf16[2,512,128]{2,1,0:T(8,128)(2,1)S(1)} fusion(bf16[1,512,128]{2,1,0:T(8,128)(2,1)} %bitcast.9, bf16[1,512,128]{2,1,0:T(8,128)(2,1)} %bitcast.11), kind=kLoop, calls=%fused_computation.3 | loop fusion | flops 131072 | bytes 524288 | tf_op jit(solution)/shard_map/stack | solution.py:277
  1.7 0.0 copy-start
  1.7 0.0 copy-start.1
  1.7 5.7 %collective-permute-start.1 = (bf16[2,512,128]{2,1,0:T(8,128)(2,1)S(1)}, bf16[2,512,128]{2,1,0:T(8,128)(2,1)S(1)}, u32[]{:S(2)}, u32[]{:S(2)}) collective-permute-start(bf16[2,512,128]{2,1,0:T(8,128)(2,1)S(1)} %pad_maximum_fusion), channel_id=1, source_target_pairs={{0,14},{1,15},{2,12},{3,13},{4,10},{5,11},{6,8},{7,9},{8,22},{9,23... | collective-permute-start | bytes 786440 | tf_op jit(solution)/shard_map/ppermute | solution.py:30
  7.4 4.0 %collective-permute-start = (bf16[2,512,128]{2,1,0:T(8,128)(2,1)S(1)}, bf16[2,512,128]{2,1,0:T(8,128)(2,1)S(1)}, u32[]{:S(2)}, u32[]{:S(2)}) collective-permute-start(bf16[2,512,128]{2,1,0:T(8,128)(2,1)S(1)} %pad_maximum_fusion), channel_id=1, source_target_pairs={{0,16},{8,24},{16,32},{24,40},{32,48},{40,56},{48,64},{56,72},{64,... | collective-permute-start | bytes 786440 | tf_op jit(solution)/shard_map/ppermute | solution.py:14
  11.4 0.7 broadcast_subtract_fusion
  12.1 0.9 %copy.8.s_ref = s32[512,1]{1,0:T(8,128)} copy(s32[512,1]{0,1:T(1,128)S(1)} %bitcast.15) | data formatting | bytes 4096 | tf_op jit(solution)/shard_map/reshape | solution.py:292
  13.0 0.0 copy-done.2
  13.0 0.0 copy-done.3
  13.0 0.8 %copy_bitcast_fusion = (bf16[512,256]{1,0:T(8,128)(2,1)}, bf16[512,256]{1,0:T(8,128)(2,1)}) fusion(bf16[64,8,2,128]{3,2,1,0:T(2,128)(2,1)S(1)} %bitcast.13, bf16[64,8,2,128]{3,2,1,0:T(2,128)(2,1)S(1)} %bitcast.14), kind=kLoop, calls=%fused_computation.1 | loop fusion | bytes 1048576 | tf_op jit(solution)/shard_map/reshape | solution.py:295
  13.8 20.8 %collective-permute-done.1 = bf16[2,512,128]{2,1,0:T(8,128)(2,1)S(1)} collective-permute-done((bf16[2,512,128]{2,1,0:T(8,128)(2,1)S(1)}, bf16[2,512,128]{2,1,0:T(8,128)(2,1)S(1)}, u32[]{:S(2)}, u32[]{:S(2)}) %collective-permute-start.1) | collective-permute-done | bytes 262176 | tf_op jit(solution)/shard_map/ppermute | solution.py:30
  34.6 0.2 collective-permute-done
  34.8 0.0 copy-done
  34.8 0.0 copy-done.1
  34.8 1.0 %maximum_maximum_fusion.w_ref = bf16[2,1536,128]{2,1,0:T(8,128)(2,1)} fusion(bf16[1,512,128]{2,1,0:T(8,128)(2,1)S(1)} %bitcast.10, bf16[1,512,128]{2,1,0:T(8,128)(2,1)S(1)} %bitcast.12, bf16[2,512,128]{2,1,0:T(8,128)(2,1)S(1)} %collective-permute-done.1, bf16[2,512,128]{2,1,0:T(8,128)(2,1)S(1)} %collective-permute-done), kind=kLoop, calls=%fused_computation | loop fusion | flops 3145728 | bytes 1572864 | tf_op jit(solution)/shard_map/concatenate | solution.py:285
  35.8 10.7 %shard_map.76 = (bf16[512,256]{1,0:T(8,128)(2,1)}, bf16[3,2,2,2,64,256]{5,4,3,2,1,0:T(8,128)(2,1)}) custom-call(bf16[512,256]{1,0:T(8,128)(2,1)} %get-tuple-element.10.q_ref, bf16[512,256]{1,0:T(8,128)(2,1)} %get-tuple-element.9.d_ref, bf16[2,1536,128]{2,1,0:T(8,128)(2,1)} %maximum_maximum_fusion.w_ref, s32[512,1]{1,0:T(8,128)} %copy.8.s_ref), custom_call_target="tpu_custom_call" | custom-call | tf_op jit(solution)/shard_map/pallas_call | solution.py:237
  46.4 1.7 %reshape.21 = bf16[512,2,128]{2,1,0:T(2,128)(2,1)} reshape(bf16[512,256]{1,0:T(8,128)(2,1)} %get-tuple-element.5) | data formatting | bytes 524288 | tf_op jit(solution)/shard_map/reshape | solution.py:300
  48.1 21.3 %shard_map.77 = f32[64,256]{1,0:T(8,128)} custom-call(bf16[3,2,2,2,64,256]{5,4,3,2,1,0:T(8,128)(2,1)} %get-tuple-element.6.x_ref), custom_call_target="tpu_custom_call" | custom-call | tf_op jit(solution)/shard_map/pallas_call | solution.py:160
  69.4 0.8 %convert.4 = bf16[64,256]{1,0:T(8,128)(2,1)S(1)} convert(f32[64,256]{1,0:T(8,128)} %shard_map.77) | non-fusion elementwise | flops 16384 | bytes 98304 | tf_op jit(solution)/shard_map/convert.1
  70.3 0.6 fusion
Async XLA Ops:
  0.6 12.4 %copy-start.2 = (bf16[512,2,128]{2,1,0:T(2,128)(2,1)S(1)}, bf16[512,2,128]{2,1,0:T(2,128)(2,1)}, u32[]{:S(2)}) copy-start(bf16[512,2,128]{2,1,0:T(2,128)(2,1)} %param.8) | copy-start | bytes 786436
  0.6 12.3 %copy-start.3 = (bf16[512,2,128]{2,1,0:T(2,128)(2,1)S(1)}, bf16[512,2,128]{2,1,0:T(2,128)(2,1)}, u32[]{:S(2)}) copy-start(bf16[512,2,128]{2,1,0:T(2,128)(2,1)} %param.5) | copy-start | bytes 786436
  1.7 33.1 %copy-start = (bf16[512,128]{1,0:T(8,128)(2,1)S(1)}, bf16[512,128]{1,0:T(8,128)(2,1)}, u32[]{:S(2)}) copy-start(bf16[512,128]{1,0:T(8,128)(2,1)} %param.7) | copy-start | bytes 393220
  1.7 33.1 %copy-start.1 = (bf16[512,128]{1,0:T(8,128)(2,1)S(1)}, bf16[512,128]{1,0:T(8,128)(2,1)}, u32[]{:S(2)}) copy-start(bf16[512,128]{1,0:T(8,128)(2,1)} %param.6) | copy-start | bytes 393220
  1.7 32.9 %collective-permute-start.1 = (bf16[2,512,128]{2,1,0:T(8,128)(2,1)S(1)}, bf16[2,512,128]{2,1,0:T(8,128)(2,1)S(1)}, u32[]{:S(2)}, u32[]{:S(2)}) collective-permute-start(bf16[2,512,128]{2,1,0:T(8,128)(2,1)S(1)} %pad_maximum_fusion), channel_id=1, source_target_pairs={{0,14},{1,15},{2,12},{3,13},{4,10},{5,11},{6,8},{7,9},{8,22},{9,23... | collective-permute-start | bytes 786440 | tf_op jit(solution)/shard_map/ppermute | solution.py:30
  7.4 27.4 %collective-permute-start = (bf16[2,512,128]{2,1,0:T(8,128)(2,1)S(1)}, bf16[2,512,128]{2,1,0:T(8,128)(2,1)S(1)}, u32[]{:S(2)}, u32[]{:S(2)}) collective-permute-start(bf16[2,512,128]{2,1,0:T(8,128)(2,1)S(1)} %pad_maximum_fusion), channel_id=1, source_target_pairs={{0,16},{8,24},{16,32},{24,40},{32,48},{40,56},{48,64},{56,72},{64,... | collective-permute-start | bytes 786440 | tf_op jit(solution)/shard_map/ppermute | solution.py:14

commit v13 on v12

--- a/solution.py
+++ b/solution.py
@@ -140,7 +140,7 @@
                 back_copy(w, 0, slot, device(block + WIN - w, sender(w, slot))).wait_recv()
                 total[...] = total[...] + back[w, slot].astype(jnp.float32)
 
-    o_ref[...] = total[...]
+    o_ref[...] = total[...].astype(o_ref.dtype)
     for stage in range(3):
         for w in range(windows):
             if copies[stage][w] is not None:
@@ -159,7 +159,7 @@
     link = jnp.bfloat16
     total = pl.pallas_call(
         grad_reduce_kernel,
-        out_shape=jax.ShapeDtypeStruct(rest, f32),
+        out_shape=jax.ShapeDtypeStruct(rest, dtype),
         in_specs=[pl.BlockSpec(memory_space=pltpu.VMEM)],
         out_specs=pl.BlockSpec(memory_space=pltpu.VMEM),
         scratch_shapes=[
@@ -178,7 +178,7 @@
         ],
         compiler_params=pltpu.CompilerParams(collective_id=0, has_side_effects=True),
     )(chunks)
-    return total[:, :width].astype(dtype), total[:, width:].astype(dtype)
+    return total[:, :width], total[:, width:]
 
 
 def attention_kernel(q_ref, d_ref, w_ref, s_ref, dq_ref, t_ref, dk_acc, dv_acc):

time: 71.3 us -> 71.2 us (level)
  other arithmetic: 3.54 us -> 2.69 us
  local copies, waits for them, and re-layouts: 4.07 us -> 4.81 us
    another operation x1 -> x0, other arithmetic: 0.85 us -> none
    slice x1, local copies, waits for them, and re-layouts: 0.62 us -> 1.35 us  [grad_reduce(): return (total[:, :width], total[:, width:])]
where the time goes in v13:
time: 71.2 us; the launch traced here: 70.8 us
  Pallas kernels  31.9 us (45%)
  waiting for transfers between devices  21 us (29%)
  starting transfers between devices  9.67 us (14%)
  local copies, waits for them, and re-layouts  4.81 us (7%)
  other arithmetic  2.69 us (4%)
    pallas_call x1, Pallas kernels, grad_reduce(): pl.pallas_call(grad_reduce_kernel, out_shape=jax.ShapeDtypeStruct(rest, d...  21.3 us
    ppermute x1, waiting for transfers between devices, nearest_next(): return lax.ppermute(block, ('dcn', 'blk', 'head'), route)  20.8 us
    pallas_call x1, Pallas kernels, attention(): pl.pallas_call(attention_kernel, out_shape=(jax.ShapeDtypeStruct(q.shape,...  10.7 us
    ppermute x1, starting transfers between devices, nearest_next(): return lax.ppermute(block, ('dcn', 'blk', 'head'), route)  5.67 us
    ppermute x1, starting transfers between devices, from_behind(): return lax.ppermute(block, axis, route)  4 us
    reshape x1, local copies, waits for them, and re-layouts, body(): q_grad = dq.reshape(queries.shape)  1.72 us
  transfers between devices with their start and end apart: 2, of which 2 were waited for; matrix products, arithmetic and copies ran while one was open for 3% of the time, Pallas kernels for 0%

profile of v13, /device:TPU:23, one launch (start us, length us, event | category | flops | bytes accessed | tf_op | source)
XLA Modules:
  0.0 70.8 jit_solution(3429692601715369581)
XLA Ops:
  0.6 0.0 copy-start.2
  0.6 0.0 copy-start.3
  0.6 1.1 %pad_maximum_fusion = bf16[2,512,128]{2,1,0:T(8,128)(2,1)S(1)} fusion(bf16[1,512,128]{2,1,0:T(8,128)(2,1)} %bitcast.9, bf16[1,512,128]{2,1,0:T(8,128)(2,1)} %bitcast.11), kind=kLoop, calls=%fused_computation.3 | loop fusion | flops 131072 | bytes 524288 | tf_op jit(solution)/shard_map/stack | solution.py:277
  1.7 0.0 copy-start
  1.7 0.0 copy-start.1
  1.7 5.7 %collective-permute-start.1 = (bf16[2,512,128]{2,1,0:T(8,128)(2,1)S(1)}, bf16[2,512,128]{2,1,0:T(8,128)(2,1)S(1)}, u32[]{:S(2)}, u32[]{:S(2)}) collective-permute-start(bf16[2,512,128]{2,1,0:T(8,128)(2,1)S(1)} %pad_maximum_fusion), channel_id=1, source_target_pairs={{0,14},{1,15},{2,12},{3,13},{4,10},{5,11},{6,8},{7,9},{8,22},{9,23... | collective-permute-start | bytes 786440 | tf_op jit(solution)/shard_map/ppermute | solution.py:30
  7.4 4.0 %collective-permute-start = (bf16[2,512,128]{2,1,0:T(8,128)(2,1)S(1)}, bf16[2,512,128]{2,1,0:T(8,128)(2,1)S(1)}, u32[]{:S(2)}, u32[]{:S(2)}) collective-permute-start(bf16[2,512,128]{2,1,0:T(8,128)(2,1)S(1)} %pad_maximum_fusion), channel_id=1, source_target_pairs={{0,16},{8,24},{16,32},{24,40},{32,48},{40,56},{48,64},{56,72},{64,... | collective-permute-start | bytes 786440 | tf_op jit(solution)/shard_map/ppermute | solution.py:14
  11.4 0.7 broadcast_subtract_fusion
  12.1 0.9 %copy.8.s_ref = s32[512,1]{1,0:T(8,128)} copy(s32[512,1]{0,1:T(1,128)S(1)} %bitcast.15) | data formatting | bytes 4096 | tf_op jit(solution)/shard_map/reshape | solution.py:292
  13.0 0.0 copy-done.2
  13.0 0.0 copy-done.3
  13.0 0.8 %copy_bitcast_fusion = (bf16[512,256]{1,0:T(8,128)(2,1)}, bf16[512,256]{1,0:T(8,128)(2,1)}) fusion(bf16[64,8,2,128]{3,2,1,0:T(2,128)(2,1)S(1)} %bitcast.13, bf16[64,8,2,128]{3,2,1,0:T(2,128)(2,1)S(1)} %bitcast.14), kind=kLoop, calls=%fused_computation.1 | loop fusion | bytes 1048576 | tf_op jit(solution)/shard_map/reshape | solution.py:295
  13.8 20.8 %collective-permute-done.1 = bf16[2,512,128]{2,1,0:T(8,128)(2,1)S(1)} collective-permute-done((bf16[2,512,128]{2,1,0:T(8,128)(2,1)S(1)}, bf16[2,512,128]{2,1,0:T(8,128)(2,1)S(1)}, u32[]{:S(2)}, u32[]{:S(2)}) %collective-permute-start.1) | collective-permute-done | bytes 262176 | tf_op jit(solution)/shard_map/ppermute | solution.py:30
  34.6 0.2 collective-permute-done
  34.8 0.0 copy-done
  34.8 0.0 copy-done.1
  34.8 1.0 %maximum_maximum_fusion.w_ref = bf16[2,1536,128]{2,1,0:T(8,128)(2,1)} fusion(bf16[1,512,128]{2,1,0:T(8,128)(2,1)S(1)} %bitcast.10, bf16[1,512,128]{2,1,0:T(8,128)(2,1)S(1)} %bitcast.12, bf16[2,512,128]{2,1,0:T(8,128)(2,1)S(1)} %collective-permute-done.1, bf16[2,512,128]{2,1,0:T(8,128)(2,1)S(1)} %collective-permute-done), kind=kLoop, calls=%fused_computation | loop fusion | flops 3145728 | bytes 1572864 | tf_op jit(solution)/shard_map/concatenate | solution.py:285
  35.8 10.7 %shard_map.76 = (bf16[512,256]{1,0:T(8,128)(2,1)}, bf16[3,2,2,2,64,256]{5,4,3,2,1,0:T(8,128)(2,1)}) custom-call(bf16[512,256]{1,0:T(8,128)(2,1)} %get-tuple-element.10.q_ref, bf16[512,256]{1,0:T(8,128)(2,1)} %get-tuple-element.9.d_ref, bf16[2,1536,128]{2,1,0:T(8,128)(2,1)} %maximum_maximum_fusion.w_ref, s32[512,1]{1,0:T(8,128)} %copy.8.s_ref), custom_call_target="tpu_custom_call" | custom-call | tf_op jit(solution)/shard_map/pallas_call | solution.py:237
  46.4 1.7 %reshape.21 = bf16[512,2,128]{2,1,0:T(2,128)(2,1)} reshape(bf16[512,256]{1,0:T(8,128)(2,1)} %get-tuple-element.5) | data formatting | bytes 524288 | tf_op jit(solution)/shard_map/reshape | solution.py:300
  48.1 21.3 %shard_map.77 = bf16[64,256]{1,0:T(8,128)(2,1)} custom-call(bf16[3,2,2,2,64,256]{5,4,3,2,1,0:T(8,128)(2,1)} %get-tuple-element.6.x_ref), custom_call_target="tpu_custom_call" | custom-call | tf_op jit(solution)/shard_map/pallas_call | solution.py:160
  69.4 1.3 %fusion = (bf16[64,128]{1,0:T(8,128)(2,1)}, bf16[64,128]{1,0:T(8,128)(2,1)}) fusion(bf16[64,256]{1,0:T(8,128)(2,1)} %shard_map.77), kind=kLoop, calls=%fused_computation.5 | loop fusion | bytes 65536 | tf_op jit(solution)/shard_map/slice | solution.py:181
Async XLA Ops:
  0.6 12.4 %copy-start.2 = (bf16[512,2,128]{2,1,0:T(2,128)(2,1)S(1)}, bf16[512,2,128]{2,1,0:T(2,128)(2,1)}, u32[]{:S(2)}) copy-start(bf16[512,2,128]{2,1,0:T(2,128)(2,1)} %param.8) | copy-start | bytes 786436
  0.6 12.3 %copy-start.3 = (bf16[512,2,128]{2,1,0:T(2,128)(2,1)S(1)}, bf16[512,2,128]{2,1,0:T(2,128)(2,1)}, u32[]{:S(2)}) copy-start(bf16[512,2,128]{2,1,0:T(2,128)(2,1)} %param.5) | copy-start | bytes 786436
  1.7 33.1 %copy-start = (bf16[512,128]{1,0:T(8,128)(2,1)S(1)}, bf16[512,128]{1,0:T(8,128)(2,1)}, u32[]{:S(2)}) copy-start(bf16[512,128]{1,0:T(8,128)(2,1)} %param.7) | copy-start | bytes 393220
  1.7 33.1 %copy-start.1 = (bf16[512,128]{1,0:T(8,128)(2,1)S(1)}, bf16[512,128]{1,0:T(8,128)(2,1)}, u32[]{:S(2)}) copy-start(bf16[512,128]{1,0:T(8,128)(2,1)} %param.6) | copy-start | bytes 393220
  1.7 32.9 %collective-permute-start.1 = (bf16[2,512,128]{2,1,0:T(8,128)(2,1)S(1)}, bf16[2,512,128]{2,1,0:T(8,128)(2,1)S(1)}, u32[]{:S(2)}, u32[]{:S(2)}) collective-permute-start(bf16[2,512,128]{2,1,0:T(8,128)(2,1)S(1)} %pad_maximum_fusion), channel_id=1, source_target_pairs={{0,14},{1,15},{2,12},{3,13},{4,10},{5,11},{6,8},{7,9},{8,22},{9,23... | collective-permute-start | bytes 786440 | tf_op jit(solution)/shard_map/ppermute | solution.py:30
  7.4 27.4 %collective-permute-start = (bf16[2,512,128]{2,1,0:T(8,128)(2,1)S(1)}, bf16[2,512,128]{2,1,0:T(8,128)(2,1)S(1)}, u32[]{:S(2)}, u32[]{:S(2)}) collective-permute-start(bf16[2,512,128]{2,1,0:T(8,128)(2,1)S(1)} %pad_maximum_fusion), channel_id=1, source_target_pairs={{0,16},{8,24},{16,32},{24,40},{32,48},{40,56},{48,64},{56,72},{64,... | collective-permute-start | bytes 786440 | tf_op jit(solution)/shard_map/ppermute | solution.py:14

commit v14 on v13

--- a/solution.py
+++ b/solution.py
@@ -181,7 +181,7 @@
     return total[:, :width], total[:, width:]
 
 
-def attention_kernel(q_ref, d_ref, w_ref, s_ref, dq_ref, t_ref, dk_acc, dv_acc):
+def attention_kernel(q_ref, d_ref, far_ref, near_ref, own_ref, s_ref, dq_ref, t_ref, dk_acc, dv_acc, w_ref):
     rows, width = q_ref.shape[0], w_ref.shape[2]
     heads = q_ref.shape[1] // width
     span = w_ref.shape[1]
@@ -189,6 +189,8 @@
     reach = min(span, WIN * rows + tile)
     scale = width ** (-0.5)
     f32 = jnp.float32
+    for i, piece_ref in enumerate((far_ref, near_ref, own_ref)):
+        w_ref[:, i * rows : (i + 1) * rows, :] = piece_ref[...]
     dk_acc[...] = jnp.zeros_like(dk_acc)
     dv_acc[...] = jnp.zeros_like(dv_acc)
     contract_last = (((1,), (1,)), ((), ()))
@@ -228,9 +230,9 @@
             t_ref[place + (slice(None), slice(width, 2 * width))] = dv_acc[first : first + piece, :].astype(t_ref.dtype)
 
 
-def attention(q, dout, window, starts, parts):
-    rows, width = q.shape[0], window.shape[2]
-    span = window.shape[1]
+def attention(q, dout, pieces, starts, parts):
+    rows, width = q.shape[0], pieces[0].shape[2]
+    span = rows * len(pieces)
     f32 = jnp.float32
     piece = rows // parts
     vmem = pl.BlockSpec(memory_space=pltpu.VMEM)
@@ -240,10 +242,14 @@
             jax.ShapeDtypeStruct(q.shape, q.dtype),
             jax.ShapeDtypeStruct((span // rows, 2, 2, 2, piece, 2 * width), jnp.bfloat16),
         ),
-        in_specs=[vmem] * 4,
+        in_specs=[vmem] * 6,
         out_specs=(vmem, vmem),
-        scratch_shapes=[pltpu.VMEM((span, width), f32), pltpu.VMEM((span, width), f32)],
-    )(q, dout, window, starts)
+        scratch_shapes=[
+            pltpu.VMEM((span, width), f32),
+            pltpu.VMEM((span, width), f32),
+            pltpu.VMEM((2, span, width), q.dtype),
+        ],
+    )(q, dout, *pieces, starts)
 
 
 def local_grads(q, dout, starts, kwin, value_window, qpos, kpos):
@@ -282,7 +288,6 @@
         else:
             pieces.append(from_behind(packed, ("dcn", "blk"), step))
     pieces.append(packed)
-    window = jnp.concatenate(pieces, axis=1)
     window_span = (WIN + 1) * rows
     first_position = position * rows
     qpos = first_position + jnp.arange(rows, dtype=jnp.int32)
@@ -293,7 +298,7 @@
     dq, chunks = attention(
         queries.reshape(rows, -1),
         out_grad.reshape(rows, -1),
-        window,
+        pieces,
         starts,
         parts,
     )

time: 71.2 us -> 70.9 us (level)
  other arithmetic: 2.69 us -> 1.04 us
    concatenate x1 -> x0, other arithmetic: 0.95 us -> none  [body(): window = jnp.concatenate(pieces, axis=1)]
  transfers between devices with their start and end apart: 2 -> 2, of which waited for: 2 -> 2; matrix products, arithmetic and copies ran while one was open for 3% -> 2% of each run, Pallas kernels for 0% -> 0%
where the time goes in v14:
time: 70.9 us; the launch traced here: 70.5 us
  Pallas kernels  31.9 us (45%)
  waiting for transfers between devices  21.6 us (30%)
  starting transfers between devices  9.67 us (14%)
  local copies, waits for them, and re-layouts  5.52 us (8%)
  other arithmetic  1.04 us (1%)
  between operations  0.72 us (1%)
    ppermute x1, waiting for transfers between devices, nearest_next(): return lax.ppermute(block, ('dcn', 'blk', 'head'), route)  21.4 us
    pallas_call x1, Pallas kernels, grad_reduce(): pl.pallas_call(grad_reduce_kernel, out_shape=jax.ShapeDtypeStruct(rest, d...  21.3 us
    pallas_call x1, Pallas kernels, attention(): pl.pallas_call(attention_kernel, out_shape=(jax.ShapeDtypeStruct(q.shape,...  10.7 us
    ppermute x1, starting transfers between devices, nearest_next(): return lax.ppermute(block, ('dcn', 'blk', 'head'), route)  5.67 us
    ppermute x1, starting transfers between devices, from_behind(): return lax.ppermute(block, axis, route)  4 us
    reshape x1, local copies, waits for them, and re-layouts, body(): q_grad = dq.reshape(queries.shape)  1.72 us
  transfers between devices with their start and end apart: 2, of which 2 were waited for; matrix products, arithmetic and copies ran while one was open for 2% of the time, Pallas kernels for 0%

profile of v14, /device:TPU:23, one launch (start us, length us, event | category | flops | bytes accessed | tf_op | source)
XLA Modules:
  0.0 70.5 jit_solution(10438983883243885716)
XLA Ops:
  0.6 0.0 copy-start.5
  0.6 0.0 copy-start.2
  0.7 1.0 %pad_maximum_fusion.own_ref = bf16[2,512,128]{2,1,0:T(8,128)(2,1)S(1)} fusion(bf16[1,512,128]{2,1,0:T(8,128)(2,1)} %bitcast.11, bf16[1,512,128]{2,1,0:T(8,128)(2,1)} %bitcast.12), kind=kLoop, calls=%fused_computation.2 | loop fusion | flops 131072 | bytes 524288 | tf_op jit(solution)/shard_map/stack | solution.py:283
  1.7 0.0 copy-start
  1.7 0.0 copy-start.1
  1.7 5.7 %collective-permute-start.1 = (bf16[2,512,128]{2,1,0:T(8,128)(2,1)S(1)}, bf16[2,512,128]{2,1,0:T(8,128)(2,1)S(1)}, u32[]{:S(2)}, u32[]{:S(2)}) collective-permute-start(bf16[2,512,128]{2,1,0:T(8,128)(2,1)S(1)} %pad_maximum_fusion.own_ref), channel_id=1, source_target_pairs={{0,14},{1,15},{2,12},{3,13},{4,10},{5,11},{6,8},{7,9},{8,22},{9,23... | collective-permute-start | bytes 786440 | tf_op jit(solution)/shard_map/ppermute | solution.py:30
  7.4 4.0 %collective-permute-start = (bf16[2,512,128]{2,1,0:T(8,128)(2,1)S(1)}, bf16[2,512,128]{2,1,0:T(8,128)(2,1)S(1)}, u32[]{:S(2)}, u32[]{:S(2)}) collective-permute-start(bf16[2,512,128]{2,1,0:T(8,128)(2,1)S(1)} %pad_maximum_fusion.own_ref), channel_id=1, source_target_pairs={{0,16},{8,24},{16,32},{24,40},{32,48},{40,56},{48,64},{56,72},{64,... | collective-permute-start | bytes 786440 | tf_op jit(solution)/shard_map/ppermute | solution.py:14
  11.4 0.0 copy-done.5
  11.4 0.9 %copy.8.s_ref = s32[512,1]{1,0:T(8,128)} copy(s32[512,1]{0,1:T(1,128)S(1)} %bitcast.13) | data formatting | bytes 4096 | tf_op jit(solution)/shard_map/reshape | solution.py:297
  12.3 0.0 copy-done.2
  12.3 0.0 copy-done.1
  12.3 0.9 %copy_bitcast_fusion = (bf16[512,256]{1,0:T(8,128)(2,1)}, bf16[512,256]{1,0:T(8,128)(2,1)}) fusion(bf16[64,8,2,128]{3,2,1,0:T(2,128)(2,1)S(1)} %bitcast.9, bf16[64,8,2,128]{3,2,1,0:T(2,128)(2,1)S(1)} %bitcast.10), kind=kLoop, calls=%fused_computation | loop fusion | bytes 1048576 | tf_op jit(solution)/shard_map/reshape | solution.py:300
  13.2 0.0 copy-done
  13.2 21.4 %collective-permute-done.1.near_ref = bf16[2,512,128]{2,1,0:T(8,128)(2,1)S(1)} collective-permute-done((bf16[2,512,128]{2,1,0:T(8,128)(2,1)S(1)}, bf16[2,512,128]{2,1,0:T(8,128)(2,1)S(1)}, u32[]{:S(2)}, u32[]{:S(2)}) %collective-permute-start.1) | collective-permute-done | bytes 262176 | tf_op jit(solution)/shard_map/ppermute | solution.py:30
  34.6 0.0 copy-start.3
  34.6 0.2 collective-permute-done.far_ref
  34.8 0.0 copy-start.4
  34.8 0.5 copy-done.3
  35.3 0.2 copy-done.4
  35.5 10.7 %shard_map.76 = (bf16[512,256]{1,0:T(8,128)(2,1)}, bf16[3,2,2,2,64,256]{5,4,3,2,1,0:T(8,128)(2,1)}) custom-call(bf16[512,256]{1,0:T(8,128)(2,1)} %get-tuple-element.10.q_ref, bf16[512,256]{1,0:T(8,128)(2,1)} %get-tuple-element.9.d_ref, bf16[2,512,128]{2,1,0:T(8,128)(2,1)} %copy-done.4, bf16[2,512,128]{2,1,0:T(8,128)(2,1)} %copy-done.3, ...), custom_call_target="tpu_custom_call" | custom-call | tf_op jit(solution)/shard_map/pallas_call | solution.py:239
  46.2 1.7 %reshape.21 = bf16[512,2,128]{2,1,0:T(2,128)(2,1)} reshape(bf16[512,256]{1,0:T(8,128)(2,1)} %get-tuple-element.5) | data formatting | bytes 524288 | tf_op jit(solution)/shard_map/reshape | solution.py:305
  47.9 21.3 %shard_map.77 = bf16[64,256]{1,0:T(8,128)(2,1)} custom-call(bf16[3,2,2,2,64,256]{5,4,3,2,1,0:T(8,128)(2,1)} %get-tuple-element.6.x_ref), custom_call_target="tpu_custom_call" | custom-call | tf_op jit(solution)/shard_map/pallas_call | solution.py:160
  69.2 1.3 %fusion = (bf16[64,128]{1,0:T(8,128)(2,1)}, bf16[64,128]{1,0:T(8,128)(2,1)}) fusion(bf16[64,256]{1,0:T(8,128)(2,1)} %shard_map.77), kind=kLoop, calls=%fused_computation.4 | loop fusion | bytes 65536 | tf_op jit(solution)/shard_map/slice | solution.py:181
  (1 shorter events, 0.0 us)
Async XLA Ops:
  0.6 10.8 %copy-start.5 = (s32[512]{0:T(512)S(1)}, s32[512]{0:T(512)}, u32[]{:S(2)}) copy-start(s32[512]{0:T(512)} %param.9) | copy-start | bytes 6148
  0.6 11.7 %copy-start.2 = (bf16[512,2,128]{2,1,0:T(2,128)(2,1)S(1)}, bf16[512,2,128]{2,1,0:T(2,128)(2,1)}, u32[]{:S(2)}) copy-start(bf16[512,2,128]{2,1,0:T(2,128)(2,1)} %param.5) | copy-start | bytes 786436
  1.7 11.5 %copy-start = (bf16[2,512,128]{2,1,0:T(8,128)(2,1)}, bf16[2,512,128]{2,1,0:T(8,128)(2,1)S(1)}, u32[]{:S(2)}) copy-start(bf16[2,512,128]{2,1,0:T(8,128)(2,1)S(1)} %pad_maximum_fusion.own_ref) | copy-start | bytes 786436
  1.7 10.6 %copy-start.1 = (bf16[512,2,128]{2,1,0:T(2,128)(2,1)S(1)}, bf16[512,2,128]{2,1,0:T(2,128)(2,1)}, u32[]{:S(2)}) copy-start(bf16[512,2,128]{2,1,0:T(2,128)(2,1)} %param.8) | copy-start | bytes 786436
  1.7 32.9 %collective-permute-start.1 = (bf16[2,512,128]{2,1,0:T(8,128)(2,1)S(1)}, bf16[2,512,128]{2,1,0:T(8,128)(2,1)S(1)}, u32[]{:S(2)}, u32[]{:S(2)}) collective-permute-start(bf16[2,512,128]{2,1,0:T(8,128)(2,1)S(1)} %pad_maximum_fusion.own_ref), channel_id=1, source_target_pairs={{0,14},{1,15},{2,12},{3,13},{4,10},{5,11},{6,8},{7,9},{8,22},{9,23... | collective-permute-start | bytes 786440 | tf_op jit(solution)/shard_map/ppermute | solution.py:30
  7.4 27.4 %collective-permute-start = (bf16[2,512,128]{2,1,0:T(8,128)(2,1)S(1)}, bf16[2,512,128]{2,1,0:T(8,128)(2,1)S(1)}, u32[]{:S(2)}, u32[]{:S(2)}) collective-permute-start(bf16[2,512,128]{2,1,0:T(8,128)(2,1)S(1)} %pad_maximum_fusion.own_ref), channel_id=1, source_target_pairs={{0,16},{8,24},{16,32},{24,40},{32,48},{40,56},{48,64},{56,72},{64,... | collective-permute-start | bytes 786440 | tf_op jit(solution)/shard_map/ppermute | solution.py:14
  34.6 0.7 %copy-start.3 = (bf16[2,512,128]{2,1,0:T(8,128)(2,1)}, bf16[2,512,128]{2,1,0:T(8,128)(2,1)S(1)}, u32[]{:S(2)}) copy-start(bf16[2,512,128]{2,1,0:T(8,128)(2,1)S(1)} %collective-permute-done.1.near_ref) | copy-start | bytes 786436
  34.8 0.7 %copy-start.4 = (bf16[2,512,128]{2,1,0:T(8,128)(2,1)}, bf16[2,512,128]{2,1,0:T(8,128)(2,1)S(1)}, u32[]{:S(2)}) copy-start(bf16[2,512,128]{2,1,0:T(8,128)(2,1)S(1)} %collective-permute-done.far_ref) | copy-start | bytes 786436
